TPU v7x, 32 devices: a whole 2x2x4 slice. The times are simulated.
32 devices in a mesh: dp: 4 (over x, core), ctx: 8 (over z, y).
Axes of the slice: x: 2, y: 2, z: 4, core: 2. Of those that a mesh axis runs over, the one named last changes fastest.
Arguments:
- query: bfloat16 [4, 1024, 2048], P('dp', 'ctx'), may hold values from -6 to 6
- keys: bfloat16 [4, 1024, 2048], P('dp', 'ctx'), may hold values from -6 to 6
- values: bfloat16 [4, 1024, 2048], P('dp', 'ctx'), may hold values from -6 to 6
- cotangent: bfloat16 [4, 1024, 2048], P('dp', 'ctx'), may hold values from -6 to 6
- long_filter: bfloat16 [1024, 2048], P('ctx'), may hold values from -1.05 to 1.05, as said below
- short_weights: float32 [3, 3, 2048], replicated, may hold values from -3 to 3
- skip: float32 [2048], replicated, may hold values from -4 to 4
- lengths: int32 [4, 16], P('dp'), may hold values from 1 to 256, 1024 in all within a row
Outputs:
- gated: bfloat16 [4, 1024, 2048], P('dp', 'ctx')
- grad_query: bfloat16 [4, 1024, 2048], P('dp', 'ctx')
- grad_keys: bfloat16 [4, 1024, 2048], P('dp', 'ctx')
- grad_values: bfloat16 [4, 1024, 2048], P('dp', 'ctx')
- grad_filter: float32 [1024, 2048], P('ctx', 'dp')
- grad_short: float32 [3, 3, 2048], replicated
- grad_skip: float32 [2048], replicated
Inputs may be any that keep to these rules, and one draw needn't show every extreme that they name: Each row lists, in order, the lengths of the 16 documents packed into one sequence; they sum to 1024 and the longest is exactly 256. `long_filter`: one filter for every channel over the lags 0 .. 1023.
All inputs are finite; a program needn't handle non-finite values.
Results may differ from a plain program's by a relative error of at most 0.024.
Values may be sent and summed in bfloat16 or wider, within the bound.
No kernel may reach another device: no remote copies, remote signals or barrier semaphores. Data moves between devices by JAX's collectives and lax.ppermute only.
A program may use at most 192 MiB of HBM per device.

v0:
```python
import math

import jax
import jax.numpy as jnp
import ml_dtypes
import numpy as np
from jax import lax
from jax.experimental import pallas as pl
from jax.experimental.pallas import tpu as pltpu
from jax.sharding import PartitionSpec as P


def shifted(x, axis, by):
    length = lax.axis_size(axis)
    pairs = [(i, i + by) for i in range(length) if 0 <= i + by < length]
    return lax.ppermute(x, axis, pairs)


def table_halves(table):
    upper = table.astype(ml_dtypes.bfloat16)
    lower = (table - upper.astype(np.float64)).astype(ml_dtypes.bfloat16)
    return jnp.asarray(upper), jnp.asarray(lower)


def split_product(form, table, data, exact=True):
    upper, lower = table_halves(table)
    wide = jnp.float32
    if not exact:
        return jnp.einsum(form, upper, data.astype(jnp.bfloat16), preferred_element_type=wide)
    if data.dtype == jnp.bfloat16:
        total = jnp.einsum(form, upper, data, preferred_element_type=wide)
        return total + jnp.einsum(form, lower, data, preferred_element_type=wide)
    data_upper = lax.optimization_barrier(data.astype(jnp.bfloat16))
    data_lower = (data - data_upper.astype(wide)).astype(jnp.bfloat16)
    total = jnp.einsum(form, upper, data_upper, preferred_element_type=wide)
    total = total + jnp.einsum(form, lower, data_upper, preferred_element_type=wide)
    return total + jnp.einsum(form, upper, data_lower, preferred_element_type=wide)


def batched_product(table, data):
    count, outer, twice, lanes = data.shape
    upper = jnp.asarray(table.astype(ml_dtypes.bfloat16))
    upper = jnp.broadcast_to(upper, (count, outer, twice, twice))
    return jnp.einsum(
        "skab,skbc->skac", upper, data.astype(jnp.bfloat16), preferred_element_type=jnp.float32
    )


def factors(size):
    bits = size.bit_length() - 1
    inner = 1 << (bits // 2)
    return size // inner, inner


def twiddles(outer, inner, size):
    phase = 2.0 * np.pi * np.outer(np.arange(outer), np.arange(inner)) / size
    cosine = jnp.asarray(np.cos(phase), jnp.float32)[None, :, :, None]
    sine = jnp.asarray(np.sin(phase), jnp.float32)[None, :, :, None]
    return cosine, sine


def inner_table(inner, sign):
    phase = 2.0 * np.pi * np.outer(np.arange(inner), np.arange(inner)) / inner
    cosine, sine = np.cos(phase), sign * np.sin(phase)
    return np.block([[cosine, sine], [-sine, cosine]])


def fft_forward(signal):
    count, length, lanes = signal.shape
    size = 2 * length
    outer, inner = factors(size)
    half = outer // 2
    phase = 2.0 * np.pi * np.outer(np.arange(outer), np.arange(half)) / outer
    first = np.concatenate([np.cos(phase), -np.sin(phase)], 0)
    blocks = signal.reshape(count, half, inner, lanes).transpose(1, 0, 2, 3)
    stage = split_product("kn,nsqb->ksqb", first, blocks)
    real_part, imag_part = stage[:outer], stage[outer:]
    cosine, sine = twiddles(outer, inner, size)
    cosine, sine = cosine.transpose(1, 0, 2, 3), sine.transpose(1, 0, 2, 3)
    turned = jnp.stack(
        [real_part * cosine + imag_part * sine, imag_part * cosine - real_part * sine]
    ).astype(jnp.bfloat16)
    turned = turned.transpose(0, 3, 2, 1, 4).reshape(2 * inner, count, outer, lanes)
    return split_product("ab,bskc->askc", inner_table(inner, 1.0), turned, exact=False)


def fft_inverse(spectrum, length):
    twice, count, outer, lanes = spectrum.shape
    inner = twice // 2
    size = outer * inner
    half = outer // 2
    stage = split_product("ab,bskc->askc", inner_table(inner, -1.0), spectrum, exact=False)
    real_part, imag_part = stage[:inner], stage[inner:]
    cosine, sine = twiddles(outer, inner, size)
    cosine, sine = cosine.transpose(2, 0, 1, 3), sine.transpose(2, 0, 1, 3)
    turned = jnp.stack(
        [real_part * cosine - imag_part * sine, imag_part * cosine + real_part * sine]
    ).astype(jnp.bfloat16)
    turned = turned.transpose(0, 3, 2, 1, 4).reshape(2 * outer, count, inner, lanes)
    phase = 2.0 * np.pi * np.outer(np.arange(half), np.arange(outer)) / outer
    last = np.concatenate([np.cos(phase), -np.sin(phase)], 1) / size
    result = split_product("nk,ksqb->nsqb", last, turned, exact=False)
    return result.transpose(1, 0, 2, 3).reshape(count, length, lanes)


def spectral_products(spectra):
    inner = spectra.shape[0] // 2
    parts = [(spectra[:inner, i], spectra[inner:, i]) for i in range(3)]
    (f_re, f_im), (m_re, m_im), (g_re, g_im) = parts
    conv = jnp.concatenate([m_re * f_re - m_im * f_im, m_re * f_im + m_im * f_re], 0)
    back = jnp.concatenate([g_re * f_re + g_im * f_im, g_im * f_re - g_re * f_im], 0)
    cross = jnp.concatenate([g_re * m_re + g_im * m_im, g_im * m_re - g_re * m_im], 0)
    return jnp.stack([conv, back, cross], 1)


def all_sum(data, axis):
    size = lax.axis_size(axis)
    total = data
    for step in range(1, size):
        total = total + lax.ppermute(data, axis, [(i, (i + step) % size) for i in range(size)])
    return total


def mesh_sum(data, axes):
    count = 1
    for axis in axes:
        count *= lax.axis_size(axis)
    rows, chans = data.shape
    pieces = data.reshape(rows, count, chans // count).transpose(1, 0, 2)
    mine = jnp.sum(lax.all_to_all(pieces, axes, 0, 0, tiled=True), axis=0)
    spread = jnp.broadcast_to(mine[None], (count,) + mine.shape)
    gathered = lax.all_to_all(spread, axes, 0, 0, tiled=True)
    return gathered.transpose(1, 0, 2).reshape(rows, chans)


def halving_scatter(data, axis):
    size = lax.axis_size(axis)
    index = lax.axis_index(axis)
    rows, chans = data.shape
    blocks = data.reshape(rows, size, chans // size)
    step = size // 2
    while step >= 1:
        half = blocks.shape[1] // 2
        upper = (index // step) % 2 == 1
        keep = jnp.where(upper, blocks[:, half:], blocks[:, :half])
        give = jnp.where(upper, blocks[:, :half], blocks[:, half:])
        blocks = keep + lax.ppermute(give, axis, [(i, i ^ step) for i in range(size)])
        step //= 2
    return blocks.reshape(rows, chans // size)


def epilogue_kernel(conv_ref, back_ref, src_ref, up_ref, mask_ref, w_ref, skip_ref, out_ref, stats_ref):
    wide, narrow = jnp.float32, jnp.bfloat16
    taps = w_ref.shape[1]
    head = taps - 1
    frame = src_ref.shape[1]
    rows = out_ref.shape[1]

    def mask(i):
        return mask_ref[i] > 0.5

    def down(x, by):
        return pltpu.roll(x, by, 0) if by else x

    def lift(x, by):
        return pltpu.roll(x, frame - by, 0) if by else x

    sources = [src_ref[i].astype(wide) for i in range(3)]
    weights = w_ref[...]
    shorts = []
    for i in range(3):
        total = weights[i, 0:1] * sources[i]
        for off in range(1, taps):
            total = total + jnp.where(mask(off), weights[i, off : off + 1] * down(sources[i], off), 0.0)
        shorts.append(total.astype(narrow).astype(wide))
    q_short, k_short, v_short = shorts
    upstream = up_ref[...].astype(wide)
    skip = skip_ref[...]
    mixed = (k_short * v_short).astype(narrow).astype(wide)
    grad_conv = (upstream * q_short).astype(narrow).astype(wide)
    conv = conv_ref[...].astype(wide) + skip * mixed
    grad_mixed = back_ref[...].astype(wide) + skip * grad_conv
    own = mask(2 * taps)
    out_ref[0] = lift(q_short * conv, head)[:rows].astype(narrow)
    grads = [upstream * conv, grad_mixed * v_short, grad_mixed * k_short]
    stats = []
    for i in range(3):
        grad = grads[i]
        acc = weights[i, 0:1] * grad
        stats.append(jnp.sum(jnp.where(own, sources[i] * grad, 0.0), axis=0, keepdims=True))
        for off in range(1, taps):
            later = lift(jnp.where(mask(taps + off), grad, 0.0), off)
            acc = acc + weights[i, off : off + 1] * later
            lagged = jnp.where(own & mask(off), down(sources[i], off) * grad, 0.0)
            stats.append(jnp.sum(lagged, axis=0, keepdims=True))
        out_ref[1 + i] = lift(acc, head)[:rows].astype(narrow)
    stats.append(jnp.sum(jnp.where(own, grad_conv * mixed, 0.0), axis=0, keepdims=True))
    width = stats[0].shape[1]
    stats.append(jnp.zeros((stats_ref.shape[0] - len(stats), width), wide))
    stats_ref[...] = jnp.concatenate(stats, 0)


def epilogue(back, sources, upstream, masks, short_weights, skip, rows):
    _, frame, chans = back.shape
    taps = short_weights.shape[1]
    block = 256 if chans % 256 == 0 else chans
    grid = (chans // block,)
    stat_rows = 16
    return pl.pallas_call(
        epilogue_kernel,
        grid=grid,
        in_specs=[
            pl.BlockSpec((None, frame, block), lambda c: (0, 0, c)),
            pl.BlockSpec((None, frame, block), lambda c: (1, 0, c)),
            pl.BlockSpec((3, frame, block), lambda c: (0, 0, c)),
            pl.BlockSpec((frame, block), lambda c: (0, c)),
            pl.BlockSpec(masks.shape, lambda c: (0, 0, 0)),
            pl.BlockSpec((3, taps, block), lambda c: (0, 0, c)),
            pl.BlockSpec((1, block), lambda c: (0, c)),
        ],
        out_specs=[
            pl.BlockSpec((4, rows, block), lambda c: (0, 0, c)),
            pl.BlockSpec((stat_rows, block), lambda c: (0, c)),
        ],
        out_shape=[
            jax.ShapeDtypeStruct((4, rows, chans), jnp.bfloat16),
            jax.ShapeDtypeStruct((stat_rows, chans), jnp.float32),
        ],
    )(back, back, sources, upstream, masks, short_weights, skip[None])


def local(query, keys, values, cotangent, long_filter, short_weights, skip, lengths):
    parts = lax.axis_size("ctx")
    index = lax.axis_index("ctx")
    groups = lax.axis_size("dp")
    q_rows, k_rows, v_rows, c_rows = query[0], keys[0], values[0], cotangent[0]
    rows, chans = q_rows.shape
    taps = short_weights.shape[1]
    head = taps - 1
    seq_len = rows * parts
    lanes = chans // parts
    ext = rows + head
    frame = -(-(rows + 2 * head) // 8) * 8
    doc_len = lengths[0]
    starts = jnp.cumsum(doc_len) - doc_len

    position = index * rows + jnp.arange(ext, dtype=jnp.int32)
    begin = jnp.max(jnp.where(starts[None, :] <= position[:, None], starts[None, :], 0), axis=1)
    valid = position[None, :] - jnp.arange(taps, dtype=jnp.int32)[:, None] >= begin[None, :]
    valid_after = valid & (position < seq_len)[None, :]

    prev = shifted(jnp.stack([a[rows - head :] for a in (q_rows, k_rows, v_rows)]), "ctx", 1)
    nxt = shifted(jnp.stack([a[:head] for a in (q_rows, k_rows, v_rows, c_rows)]), "ctx", -1)
    padded = [
        jnp.concatenate([prev[i], src, nxt[i]], 0).astype(jnp.float32)
        for i, src in enumerate((q_rows, k_rows, v_rows))
    ]

    def short_forward(wide, weights):
        summed = weights[0] * wide[head : head + ext]
        for offset in range(1, taps):
            begin_at = head - offset
            summed = summed + jnp.where(
                valid[offset][:, None], weights[offset] * wide[begin_at : begin_at + ext], 0.0
            )
        return summed.astype(jnp.bfloat16).astype(jnp.float32)

    q_short = short_forward(padded[0], short_weights[0])
    k_short = short_forward(padded[1], short_weights[1])
    v_short = short_forward(padded[2], short_weights[2])
    upstream = jnp.concatenate([c_rows, nxt[3]], 0).astype(jnp.float32)
    mixed = (k_short * v_short).astype(jnp.bfloat16)
    grad_conv = (upstream * q_short).astype(jnp.bfloat16)
    mixed_wide = mixed.astype(jnp.float32)
    grad_wide = grad_conv.astype(jnp.float32)

    chunks = 2 if lanes % 2 == 0 else 1
    width = lanes // chunks

    def to_columns(data):
        count = data.shape[0]
        split = data.reshape(count, rows, parts, lanes).transpose(0, 2, 1, 3)
        moved = lax.all_to_all(split, "ctx", 1, 1, tiled=True)
        return moved.reshape(count, seq_len, chunks, width)

    all_columns = to_columns(jnp.stack([long_filter, mixed[:rows], grad_conv[:rows]]))
    returned = []
    for part in range(chunks):
        columns = all_columns[:, :, part]
        spectra = fft_forward(columns)
        raw = fft_inverse(spectral_products(spectra), seq_len).astype(jnp.bfloat16)
        raw = jnp.concatenate(
            [jnp.zeros((3, head, width), raw.dtype), raw, jnp.zeros((3, frame - rows - head, width), raw.dtype)], 1
        )
        blocks = jnp.stack([raw[:, j * rows : j * rows + frame] for j in range(parts)], 1)
        returned.append(lax.all_to_all(blocks, "ctx", 1, 1, tiled=True))
    back = jnp.stack(returned, 3).transpose(0, 2, 1, 3, 4).reshape(3, frame, chans)

    spot = index * rows - head + jnp.arange(frame, dtype=jnp.int32)
    spot_begin = jnp.max(jnp.where(starts[None, :] <= spot[:, None], starts[None, :], 0), axis=1)
    spot_valid = spot[None, :] - jnp.arange(taps, dtype=jnp.int32)[:, None] >= spot_begin[None, :]
    spot_after = spot_valid & ((spot >= 0) & (spot < seq_len))[None, :]
    spot_own = ((spot >= index * rows) & (spot < index * rows + rows))[None, :]
    masks = jnp.concatenate([spot_valid, spot_after, spot_own], 0).astype(jnp.float32)
    masks = jnp.concatenate([masks, jnp.zeros(((-masks.shape[0]) % 8, frame), jnp.float32)], 0)
    tail = frame - rows - 2 * head
    sources = jnp.stack([
        jnp.concatenate([prev[i], src, nxt[i], jnp.zeros((tail, chans), src.dtype)], 0)
        for i, src in enumerate((q_rows, k_rows, v_rows))
    ])
    framed_up = jnp.concatenate(
        [jnp.zeros((head, chans), c_rows.dtype), c_rows, nxt[3], jnp.zeros((tail, chans), c_rows.dtype)], 0
    )
    outs, stats = epilogue(back, sources, framed_up, masks[:, :, None], short_weights, skip, rows)
    summed = mesh_sum(stats[: 3 * taps + 1], ("dp", "ctx"))
    gated, grad_q, grad_k, grad_v = outs[0], outs[1], outs[2], outs[3]
    filter_part = halving_scatter(back[2, head : head + rows].astype(jnp.float32), "dp")
    scale = 1.0 / (groups * seq_len)
    return (
        gated[None],
        grad_q.astype(jnp.bfloat16)[None],
        grad_k.astype(jnp.bfloat16)[None],
        grad_v.astype(jnp.bfloat16)[None],
        filter_part * scale,
        summed[: 3 * taps].reshape(3, taps, chans) * scale,
        summed[3 * taps] * scale,
    )


def solution(mesh):
    in_specs = (
        P("dp", "ctx", None),
        P("dp", "ctx", None),
        P("dp", "ctx", None),
        P("dp", "ctx", None),
        P("ctx", None),
        P(),
        P(),
        P("dp", None),
    )
    out_specs = (
        P("dp", "ctx", None),
        P("dp", "ctx", None),
        P("dp", "ctx", None),
        P("dp", "ctx", None),
        P("ctx", "dp"),
        P(),
        P(),
    )
    return jax.shard_map(local, mesh=mesh, in_specs=in_specs, out_specs=out_specs, check_vma=False)
```

profile of v0, /device:TPU:0, one launch (start us, length us, event | category | flops | bytes accessed | tf_op | source)
XLA Modules:
  0.0 192.0 jit_solution(13207037553518141563)
XLA Ops:
  4.6 5.5 %collective-permute-start = (bf16[3,2,2048]{2,1,0:T(2,128)(2,1)S(1)}, bf16[3,2,2048]{2,1,0:T(2,128)(2,1)S(1)}, u32[]{:S(2)}, u32[]{:S(2)}) collective-permute-start(bf16[3,2,2048]{2,1,0:T(2,128)(2,1)S(1)} %pad_maximum_fusion.3), channel_id=1, source_target_pairs={{0,1},{1,2},{2,3},{3,4},{4,5},{5,6},{6,7},{8,9},{9,10},{10,11},{11... | collective-permute-start | bytes 73736 | tf_op jit(solution)/shard_map/ppermute | solution.py:16
  19.0 1.4 maximum_bitcast_fusion.5
  20.4 6.2 %all-to-all-start = ((bf16[3,8,128,256]{2,3,0,1:T(8,128)(2,1)}), bf16[3,8,128,256]{2,3,0,1:T(8,128)(2,1)S(1)}, u32[]{:S(2)}, u32[]{:S(2)}) async-start(bf16[3,8,128,256]{2,3,0,1:T(8,128)(2,1)} %maximum_bitcast_fusion.5), calls=%async_computation | async-start | bytes 3145728 | tf_op jit(solution)/shard_map/all_to_all | solution.py:283
  26.7 36.3 %all-to-all-done = bf16[3,8,128,256]{2,3,0,1:T(8,128)(2,1)S(1)} async-done(((bf16[3,8,128,256]{2,3,0,1:T(8,128)(2,1)}), bf16[3,8,128,256]{2,3,0,1:T(8,128)(2,1)S(1)}, u32[]{:S(2)}, u32[]{:S(2)}) %all-to-all-start) | async-done | bytes 1572896 | tf_op jit(solution)/shard_map/all_to_all | solution.py:283
  70.0 2.4 %fusion.20 = (bf16[1,64,3,32,128]{4,1,3,2,0:T(8,128)(2,1)S(1)}, bf16[1,64,3,32,128]{4,1,3,2,0:T(8,128)(2,1)S(1)}, bf16[1,64,3,32,128]{4,1,3,2,0:T(8,128)(2,1)S(1)}, bf16[1,64,3,32,128]{4,1,3,2,0:T(8,128)(2,1)S(1)}) fusion(f32[128,3,32,128]{3,0,2,1:T(8,128)S(1)} %add_bitcast_fusion.1, f32[64,32]{0,1:T(8,128)S(1)} %copy-done.17, f32[64,32]{0,1:T(8,128)S(1)} %copy-done.16, ...), kind=kLoop, calls=%fused_computation.36 | loop fusion | flops 12582912 | bytes 18890752 | tf_op jit(solution)/shard_map/stack | solution.py:80
  73.5 2.5 %fusion.14 = f32[64,3,64,128]{3,0,2,1:T(8,128)S(1)} fusion(bf16[64,64,1,1]{1,0,3,2:T(8,128)(2,1)S(1)} %copy-done.10, bf16[64,3,64,128]{3,2,1,0:T(8,128)(2,1)S(1)} %bitcast.246), kind=kOutput, calls=%fused_computation.20 | convolution fusion | flops 201326592 | bytes 9445376 | tf_op jit(solution)/shard_map/ab,bskc->askc/dot_general | solution.py:29
  78.4 2.5 %fusion.18 = f32[64,3,64,128]{3,0,2,1:T(8,128)S(1)} fusion(bf16[64,64,1,1]{1,0,3,2:T(8,128)(2,1)S(1)} %copy-done.10, bf16[64,3,64,128]{3,2,1,0:T(8,128)(2,1)S(1)} %bitcast.244), kind=kOutput, calls=%fused_computation.24 | convolution fusion | flops 201326592 | bytes 9445376 | tf_op jit(solution)/shard_map/ab,bskc->askc/dot_general | solution.py:29
  85.8 2.4 %fusion.22 = (bf16[1,32,3,64,128]{4,1,3,2,0:T(8,128)(2,1)S(1)}, bf16[1,32,3,64,128]{4,1,3,2,0:T(8,128)(2,1)S(1)}, bf16[1,32,3,64,128]{4,1,3,2,0:T(8,128)(2,1)S(1)}, bf16[1,32,3,64,128]{4,1,3,2,0:T(8,128)(2,1)S(1)}) fusion(f32[64,3,64,128]{3,0,2,1:T(8,128)S(1)} %fusion, f32[32,64]{0,1:T(8,128)S(1)} %copy-done.12, f32[32,64]{0,1:T(8,128)S(1)} %copy-done.11, ...), kind=kLoop, calls=%fused_computation.38 | loop fusion | flops 12582912 | bytes 18890752 | tf_op jit(solution)/shard_map/stack | solution.py:96
  96.1 4.2 %all-to-all-start.1 = ((bf16[3,8,136,128]{3,2,0,1:T(8,128)(2,1)}), bf16[3,8,136,128]{3,2,0,1:T(8,128)(2,1)}, u32[]{:S(2)}, u32[]{:S(2)}) async-start(bf16[3,8,136,128]{3,2,0,1:T(8,128)(2,1)} %fusion.74), calls=%async_computation.1 | async-start | bytes 1671168 | tf_op jit(solution)/shard_map/all_to_all | solution.py:296
  108.2 13.3 %all-to-all-done.1 = bf16[3,8,136,128]{3,2,0,1:T(8,128)(2,1)} async-done(((bf16[3,8,136,128]{3,2,0,1:T(8,128)(2,1)}), bf16[3,8,136,128]{3,2,0,1:T(8,128)(2,1)}, u32[]{:S(2)}, u32[]{:S(2)}) %all-to-all-start.1) | async-done | bytes 835616 | tf_op jit(solution)/shard_map/all_to_all | solution.py:296
  121.4 3.5 %all-to-all-start.2 = ((bf16[3,8,136,128]{3,2,0,1:T(8,128)(2,1)}), bf16[3,8,136,128]{3,2,0,1:T(8,128)(2,1)S(1)}, u32[]{:S(2)}, u32[]{:S(2)}) async-start(bf16[3,8,136,128]{3,2,0,1:T(8,128)(2,1)} %fusion.78), calls=%async_computation.2 | async-start | bytes 1671168 | tf_op jit(solution)/shard_map/all_to_all | solution.py:296
  126.2 1.6 maximum_maximum_fusion
  127.8 1.4 pad_maximum_fusion.src_ref
  130.4 15.9 %all-to-all-done.2 = bf16[3,8,136,128]{3,2,0,1:T(8,128)(2,1)S(1)} async-done(((bf16[3,8,136,128]{3,2,0,1:T(8,128)(2,1)}), bf16[3,8,136,128]{3,2,0,1:T(8,128)(2,1)S(1)}, u32[]{:S(2)}, u32[]{:S(2)}) %all-to-all-start.2) | async-done | bytes 835616 | tf_op jit(solution)/shard_map/all_to_all | solution.py:296
  146.6 1.7 copy.169
  149.7 1.7 reshape.201
  151.4 2.0 %fusion.95 = (f32[128,2,512]{2,1,0:T(2,128)S(1)}, f32[128,2,512]{2,1,0:T(2,128)S(1)}) fusion(f32[128,4,512]{2,1,0:T(4,128)} %reshape.201), kind=kLoop, calls=%fused_computation.197 | loop fusion | bytes 2097152 | tf_op jit(solution)/shard_map/slice | solution.py:145
  153.4 9.7 %shard_map.297 = (bf16[4,128,2048]{2,1,0:T(8,128)(2,1)}, f32[16,2048]{1,0:T(8,128)}) custom-call(bf16[3,136,2048]{2,1,0:T(8,128)(2,1)} %copy-done, bf16[3,136,2048]{2,1,0:T(8,128)(2,1)} %copy-done, bf16[3,136,2048]{2,1,0:T(8,128)(2,1)} %pad_maximum_fusion.src_ref, bf16[136,2048]{1,0:T(8,128)(2,1)} %get-tuple-element.78.up_ref, f32[8,136,1]{2,1,0:T(8,128)} %copy.170.mask_ref, ...), custom_call_target="tpu_custom_call" | custom-call | tf_op jit(solution)/shard_map/pallas_call | solution.py:209
  165.0 3.5 %all-to-all-start.3 = ((f32[32,1,640]{2,1,0:T(1,128)}), f32[32,1,640]{2,1,0:T(1,128)S(1)}, u32[]{:S(2)}, u32[]{:S(2)}) async-start(f32[32,1,640]{2,1,0:T(1,128)} %reshape.209), calls=%async_computation.3 | async-start | bytes 163840 | tf_op jit(solution)/shard_map/all_to_all | solution.py:130
  168.8 1.8 collective-permute-start.2
  170.6 5.4 %all-to-all-done.3 = f32[32,1,640]{2,1,0:T(1,128)S(1)} async-done(((f32[32,1,640]{2,1,0:T(1,128)}), f32[32,1,640]{2,1,0:T(1,128)S(1)}, u32[]{:S(2)}, u32[]{:S(2)}) %all-to-all-start.3) | async-done | bytes 81952 | tf_op jit(solution)/shard_map/all_to_all | solution.py:130
  178.3 2.6 %all-to-all-start.4 = ((f32[32,1,640]{2,1,0:T(1,128)}), f32[32,1,640]{2,1,0:T(1,128)S(1)}, u32[]{:S(2)}, u32[]{:S(2)}) async-start(f32[32,1,640]{2,1,0:T(1,128)} %reshape.211), calls=%async_computation.4 | async-start | bytes 163840 | tf_op jit(solution)/shard_map/all_to_all | solution.py:132
  180.9 2.9 %fusion.93 = (bf16[1,128,2048]{2,1,0:T(8,128)(2,1)}, bf16[1,128,2048]{2,1,0:T(8,128)(2,1)}, bf16[1,128,2048]{2,1,0:T(8,128)(2,1)}, bf16[1,128,2048]{2,1,0:T(8,128)(2,1)}) fusion(bf16[4,128,2048]{2,1,0:T(8,128)(2,1)} %get-tuple-element.9), kind=kLoop, calls=%fused_computation.195 | loop fusion | bytes 4194304 | tf_op jit(solution)/shard_map/slice | solution.py:316
  183.8 4.6 %all-to-all-done.4 = f32[32,1,640]{2,1,0:T(1,128)S(1)} async-done(((f32[32,1,640]{2,1,0:T(1,128)}), f32[32,1,640]{2,1,0:T(1,128)S(1)}, u32[]{:S(2)}, u32[]{:S(2)}) %all-to-all-start.4) | async-done | bytes 81952 | tf_op jit(solution)/shard_map/all_to_all | solution.py:132
  (152 shorter events, 55.4 us)
Async XLA Ops:
  0.6 13.5 %copy-start.1 = (bf16[1,128,2048]{2,1,0:T(8,128)(2,1)S(1)}, bf16[1,128,2048]{2,1,0:T(8,128)(2,1)}, u32[]{:S(2)}) copy-start(bf16[1,128,2048]{2,1,0:T(8,128)(2,1)} %param.28) | copy-start | bytes 1572868
  0.6 13.7 %copy-start.3 = (bf16[1,128,2048]{2,1,0:T(8,128)(2,1)S(1)}, bf16[1,128,2048]{2,1,0:T(8,128)(2,1)}, u32[]{:S(2)}) copy-start(bf16[1,128,2048]{2,1,0:T(8,128)(2,1)} %param.26) | copy-start | bytes 1572868
  3.2 10.9 %collective-permute-start.1 = (bf16[4,2,2048]{2,1,0:T(2,128)(2,1)S(1)}, bf16[4,2,2048]{2,1,0:T(2,128)(2,1)S(1)}, u32[]{:S(2)}, u32[]{:S(2)}) collective-permute-start(bf16[4,2,2048]{2,1,0:T(2,128)(2,1)S(1)} %pad_maximum_fusion.2), channel_id=1, source_target_pairs={{1,0},{2,1},{3,2},{4,3},{5,4},{6,5},{7,6},{9,8},{10,9},{11,10},{12... | collective-permute-start | bytes 98312 | tf_op jit(solution)/shard_map/ppermute | solution.py:16
  4.6 9.5 %collective-permute-start = (bf16[3,2,2048]{2,1,0:T(2,128)(2,1)S(1)}, bf16[3,2,2048]{2,1,0:T(2,128)(2,1)S(1)}, u32[]{:S(2)}, u32[]{:S(2)}) collective-permute-start(bf16[3,2,2048]{2,1,0:T(2,128)(2,1)S(1)} %pad_maximum_fusion.3), channel_id=1, source_target_pairs={{0,1},{1,2},{2,3},{3,4},{4,5},{5,6},{6,7},{8,9},{9,10},{10,11},{11... | collective-permute-start | bytes 73736 | tf_op jit(solution)/shard_map/ppermute | solution.py:16
  14.2 1.0 copy-start.5
  16.2 1.0 copy-start.7
  20.4 42.7 %all-to-all-start = ((bf16[3,8,128,256]{2,3,0,1:T(8,128)(2,1)}), bf16[3,8,128,256]{2,3,0,1:T(8,128)(2,1)S(1)}, u32[]{:S(2)}, u32[]{:S(2)}) async-start(bf16[3,8,128,256]{2,3,0,1:T(8,128)(2,1)} %maximum_bitcast_fusion.5), calls=%async_computation | async-start | bytes 3145728 | tf_op jit(solution)/shard_map/all_to_all | solution.py:283
  65.0 0.8 copy-start.15
  66.8 1.0 copy-start.14
  68.9 1.1 copy-start.16
  68.9 1.1 copy-start.17
  84.6 1.2 copy-start.11
  84.6 1.2 copy-start.12
  96.1 25.3 %all-to-all-start.1 = ((bf16[3,8,136,128]{3,2,0,1:T(8,128)(2,1)}), bf16[3,8,136,128]{3,2,0,1:T(8,128)(2,1)}, u32[]{:S(2)}, u32[]{:S(2)}) async-start(bf16[3,8,136,128]{3,2,0,1:T(8,128)(2,1)} %fusion.74), calls=%async_computation.1 | async-start | bytes 1671168 | tf_op jit(solution)/shard_map/all_to_all | solution.py:296
  106.8 19.4 %copy-start.2 = (bf16[1,128,2048]{2,1,0:T(8,128)(2,1)S(1)}, bf16[1,128,2048]{2,1,0:T(8,128)(2,1)}, u32[]{:S(2)}) copy-start(bf16[1,128,2048]{2,1,0:T(8,128)(2,1)} %param.28) | copy-start | bytes 1572868
  106.8 19.4 %copy-start.4 = (bf16[1,128,2048]{2,1,0:T(8,128)(2,1)S(1)}, bf16[1,128,2048]{2,1,0:T(8,128)(2,1)}, u32[]{:S(2)}) copy-start(bf16[1,128,2048]{2,1,0:T(8,128)(2,1)} %param.26) | copy-start | bytes 1572868
  106.8 19.4 %copy-start.6 = (bf16[1,128,2048]{2,1,0:T(8,128)(2,1)S(1)}, bf16[1,128,2048]{2,1,0:T(8,128)(2,1)}, u32[]{:S(2)}) copy-start(bf16[1,128,2048]{2,1,0:T(8,128)(2,1)} %param.27) | copy-start | bytes 1572868
  106.8 19.4 %copy-start.8 = (bf16[1,128,2048]{2,1,0:T(8,128)(2,1)S(1)}, bf16[1,128,2048]{2,1,0:T(8,128)(2,1)}, u32[]{:S(2)}) copy-start(bf16[1,128,2048]{2,1,0:T(8,128)(2,1)} %param.29) | copy-start | bytes 1572868
  121.4 24.9 %all-to-all-start.2 = ((bf16[3,8,136,128]{3,2,0,1:T(8,128)(2,1)}), bf16[3,8,136,128]{3,2,0,1:T(8,128)(2,1)S(1)}, u32[]{:S(2)}, u32[]{:S(2)}) async-start(bf16[3,8,136,128]{3,2,0,1:T(8,128)(2,1)} %fusion.78), calls=%async_computation.2 | async-start | bytes 1671168 | tf_op jit(solution)/shard_map/all_to_all | solution.py:296
  149.6 1.8 copy-start
  165.0 11.0 %all-to-all-start.3 = ((f32[32,1,640]{2,1,0:T(1,128)}), f32[32,1,640]{2,1,0:T(1,128)S(1)}, u32[]{:S(2)}, u32[]{:S(2)}) async-start(f32[32,1,640]{2,1,0:T(1,128)} %reshape.209), calls=%async_computation.3 | async-start | bytes 163840 | tf_op jit(solution)/shard_map/all_to_all | solution.py:130
  168.8 20.6 %collective-permute-start.2 = (f32[128,2,512]{2,0,1:T(8,128)S(1)}, f32[128,2,512]{2,0,1:T(8,128)S(1)}, u32[]{:S(2)}, u32[]{:S(2)}) collective-permute-start(f32[128,2,512]{2,0,1:T(8,128)S(1)} %copy_select_fusion), channel_id=1, source_target_pairs={{0,16},{8,24},{16,0},{24,8},{1,17},{9,25},{17,1},{25,9},{2,18},{10... | collective-permute-start | bytes 1572872 | tf_op jit(solution)/shard_map/ppermute | solution.py:147
  178.3 10.0 %all-to-all-start.4 = ((f32[32,1,640]{2,1,0:T(1,128)}), f32[32,1,640]{2,1,0:T(1,128)S(1)}, u32[]{:S(2)}, u32[]{:S(2)}) async-start(f32[32,1,640]{2,1,0:T(1,128)} %reshape.211), calls=%async_computation.4 | async-start | bytes 163840 | tf_op jit(solution)/shard_map/all_to_all | solution.py:132
  189.6 1.6 collective-permute-start.3
  (3 other events, 2.2 us)
where the time goes:
time: 193 us; the launch traced here: 192 us
  waiting for transfers between devices  75.5 us (39%)
  local copies, waits for them, and re-layouts  40.8 us (21%)
  starting transfers between devices  28.9 us (15%)
  other arithmetic  21.7 us (11%)
  matrix products  13.9 us (7%)
  Pallas kernels  9.72 us (5%)
    all_to_all x1, waiting for transfers between devices, to_columns(): moved = lax.all_to_all(split, 'ctx', 1, 1, tiled=True)  36.3 us
    all_to_all x2, waiting for transfers between devices, local(): returned.append(lax.all_to_all(blocks, 'ctx', 1, 1, tiled=True))  29.2 us
    unnamed x55, local copies, waits for them, and re-layouts  14.4 us
    pallas_call x1, Pallas kernels, epilogue(): pl.pallas_call(epilogue_kernel, grid=grid, in_specs=[pl.BlockSpec((None,...  9.72 us
    dot_general x6, matrix products, split_product(): jnp.einsum(form, upper, data.astype(jnp.bfloat16), preferred_element_type...  9.71 us
    all_to_all x2, starting transfers between devices, local(): returned.append(lax.all_to_all(blocks, 'ctx', 1, 1, tiled=True))  7.77 us
    ppermute x2, starting transfers between devices, shifted(): return lax.ppermute(x, axis, pairs)  6.79 us
    all_to_all x1, starting transfers between devices, to_columns(): moved = lax.all_to_all(split, 'ctx', 1, 1, tiled=True)  6.22 us
  transfers between devices with their start and end apart: 9, of which 5 were waited for; matrix products, arithmetic and copies ran while one was open for 13% of the time, Pallas kernels for 0%

commit v1 on v0

--- a/solution.py
+++ b/solution.py
@@ -277,23 +277,28 @@
     chunks = 2 if lanes % 2 == 0 else 1
     width = lanes // chunks
 
-    def to_columns(data):
+    def to_columns(data, part):
         count = data.shape[0]
-        split = data.reshape(count, rows, parts, lanes).transpose(0, 2, 1, 3)
-        moved = lax.all_to_all(split, "ctx", 1, 1, tiled=True)
-        return moved.reshape(count, seq_len, chunks, width)
-
-    all_columns = to_columns(jnp.stack([long_filter, mixed[:rows], grad_conv[:rows]]))
+        split = data.reshape(count, rows, parts, chunks, width)[:, :, :, part]
+        moved = lax.all_to_all(split.transpose(0, 2, 1, 3), "ctx", 1, 1, tiled=True)
+        return moved.reshape(count, seq_len, width)
+
+    sent = jnp.stack([long_filter, mixed[:rows], grad_conv[:rows]])
     returned = []
+    previous = None
     for part in range(chunks):
-        columns = all_columns[:, :, part]
+        columns = to_columns(sent, part)
+        if previous is not None:
+            columns, previous = lax.optimization_barrier((columns, previous))
+            returned.append(lax.all_to_all(previous, "ctx", 1, 1, tiled=True))
         spectra = fft_forward(columns)
         raw = fft_inverse(spectral_products(spectra), seq_len).astype(jnp.bfloat16)
         raw = jnp.concatenate(
             [jnp.zeros((3, head, width), raw.dtype), raw, jnp.zeros((3, frame - rows - head, width), raw.dtype)], 1
         )
         blocks = jnp.stack([raw[:, j * rows : j * rows + frame] for j in range(parts)], 1)
-        returned.append(lax.all_to_all(blocks, "ctx", 1, 1, tiled=True))
+        previous = blocks
+    returned.append(lax.all_to_all(previous, "ctx", 1, 1, tiled=True))
     back = jnp.stack(returned, 3).transpose(0, 2, 1, 3, 4).reshape(3, frame, chans)
 
     spot = index * rows - head + jnp.arange(frame, dtype=jnp.int32)

time: 193 us -> 188 us (0.974)
  local copies, waits for them, and re-layouts: 40.8 us -> 35.6 us
  waiting for transfers between devices: 75.5 us -> 71.3 us
  starting transfers between devices: 28.9 us -> 32.2 us
    all_to_all x3 -> x4, waiting for transfers between devices: 65.5 us -> 61.3 us  [the longest x2 37.3 us: local(): returned.append(lax.all_to_all(previous, 'ctx', 1, 1, tiled=True))]
    unnamed x55 -> x95, local copies, waits for them, and re-layouts: 14.4 us -> 11 us
    all_to_all x3 -> x4, starting transfers between devices: 14 us -> 17.2 us  [the longest x2 9.94 us: to_columns(): moved = lax.all_to_all(split.transpose(0, 2, 1, 3), 'ctx', 1, 1, tiled=True)]
    transpose x0 -> x3, local copies, waits for them, and re-layouts: none -> 2.51 us  [to_columns(): moved = lax.all_to_all(split.transpose(0, 2, 1, 3), 'ctx', 1, 1, tiled=True)]
    all_to_all x3 -> x4, local copies, waits for them, and re-layouts: 2.29 us -> 0.26 us  [the longest x2 0.13 us: to_columns(): moved = lax.all_to_all(split.transpose(0, 2, 1, 3), 'ctx', 1, 1, tiled=True)]
  transfers between devices with their start and end apart: 9 -> 10, of which waited for: 5 -> 6; matrix products, arithmetic and copies ran while one was open for 13% -> 17% of each run, Pallas kernels for 0% -> 0%
where the time goes in v1:
time: 188 us; the launch traced here: 186 us
  waiting for transfers between devices  71.3 us (38%)
  local copies, waits for them, and re-layouts  35.6 us (19%)
  starting transfers between devices  32.2 us (17%)
  other arithmetic  22 us (12%)
  matrix products  13.8 us (7%)
  Pallas kernels  9.73 us (5%)
    all_to_all x2, waiting for transfers between devices, local(): returned.append(lax.all_to_all(previous, 'ctx', 1, 1, tiled=True))  37.3 us
    all_to_all x2, waiting for transfers between devices, to_columns(): moved = lax.all_to_all(split.transpose(0, 2, 1, 3), 'ctx', 1, 1, tiled=True)  24 us
    unnamed x95, local copies, waits for them, and re-layouts  11 us
    all_to_all x2, starting transfers between devices, to_columns(): moved = lax.all_to_all(split.transpose(0, 2, 1, 3), 'ctx', 1, 1, tiled=True)  9.94 us
    pallas_call x1, Pallas kernels, epilogue(): pl.pallas_call(epilogue_kernel, grid=grid, in_specs=[pl.BlockSpec((None,...  9.73 us
    dot_general x6, matrix products, split_product(): jnp.einsum(form, upper, data.astype(jnp.bfloat16), preferred_element_type...  9.69 us
    all_to_all x2, starting transfers between devices, local(): returned.append(lax.all_to_all(previous, 'ctx', 1, 1, tiled=True))  7.29 us
    ppermute x2, starting transfers between devices, shifted(): return lax.ppermute(x, axis, pairs)  6.79 us
  transfers between devices with their start and end apart: 10, of which 6 were waited for; matrix products, arithmetic and copies ran while one was open for 17% of the time, Pallas kernels for 0%

profile of v1, /device:TPU:0, one launch (start us, length us, event | category | flops | bytes accessed | tf_op | source)
XLA Modules:
  0.0 186.4 jit_solution(7881437159699549216)
XLA Ops:
  4.6 5.5 %collective-permute-start = (bf16[3,2,2048]{2,1,0:T(2,128)(2,1)S(1)}, bf16[3,2,2048]{2,1,0:T(2,128)(2,1)S(1)}, u32[]{:S(2)}, u32[]{:S(2)}) collective-permute-start(bf16[3,2,2048]{2,1,0:T(2,128)(2,1)S(1)} %pad_maximum_fusion.4), channel_id=1, source_target_pairs={{0,1},{1,2},{2,3},{3,4},{4,5},{5,6},{6,7},{8,9},{9,10},{10,11},{11... | collective-permute-start | bytes 73736 | tf_op jit(solution)/shard_map/ppermute | solution.py:16
  21.2 6.2 %all-to-all-start.1 = ((bf16[3,8,128,128]{3,2,0,1:T(8,128)(2,1)}), bf16[3,8,128,128]{3,2,0,1:T(8,128)(2,1)S(1)}, u32[]{:S(2)}, u32[]{:S(2)}) async-start(bf16[3,8,128,128]{3,2,0,1:T(8,128)(2,1)} %copy.194), calls=%async_computation.1 | async-start | bytes 1572864 | tf_op jit(solution)/shard_map/all_to_all | solution.py:283
  28.6 18.5 %all-to-all-done.1 = bf16[3,8,128,128]{3,2,0,1:T(8,128)(2,1)S(1)} async-done(((bf16[3,8,128,128]{3,2,0,1:T(8,128)(2,1)}), bf16[3,8,128,128]{3,2,0,1:T(8,128)(2,1)S(1)}, u32[]{:S(2)}, u32[]{:S(2)}) %all-to-all-start.1) | async-done | bytes 786464 | tf_op jit(solution)/shard_map/all_to_all | solution.py:283
  47.1 3.7 %all-to-all-start = ((bf16[3,8,128,128]{3,2,0,1:T(8,128)(2,1)}), bf16[3,8,128,128]{3,2,0,1:T(8,128)(2,1)S(1)}, u32[]{:S(2)}, u32[]{:S(2)}) async-start(bf16[3,8,128,128]{3,2,0,1:T(8,128)(2,1)} %copy.191), calls=%async_computation | async-start | bytes 1572864 | tf_op jit(solution)/shard_map/all_to_all | solution.py:283
  55.4 2.5 %fusion.18 = f32[64,3,64,128]{3,0,2,1:T(8,128)S(1)} fusion(bf16[64,64,1,1]{1,0,3,2:T(8,128)(2,1)S(1)} %copy-done.25, bf16[64,3,64,128]{3,2,1,0:T(8,128)(2,1)S(1)} %bitcast.246), kind=kOutput, calls=%fused_computation.24 | convolution fusion | flops 201326592 | bytes 9445376 | tf_op jit(solution)/shard_map/ab,bskc->askc/dot_general | solution.py:29
  65.5 5.5 %all-to-all-done = bf16[3,8,128,128]{3,2,0,1:T(8,128)(2,1)S(1)} async-done(((bf16[3,8,128,128]{3,2,0,1:T(8,128)(2,1)}), bf16[3,8,128,128]{3,2,0,1:T(8,128)(2,1)S(1)}, u32[]{:S(2)}, u32[]{:S(2)}) %all-to-all-start) | async-done | bytes 786464 | tf_op jit(solution)/shard_map/all_to_all | solution.py:283
  75.5 2.5 %fusion.14 = f32[64,3,64,128]{3,0,2,1:T(8,128)S(1)} fusion(bf16[64,64,1,1]{1,0,3,2:T(8,128)(2,1)S(1)} %copy-done.26, bf16[64,3,64,128]{3,2,1,0:T(8,128)(2,1)S(1)} %bitcast.244), kind=kOutput, calls=%fused_computation.20 | convolution fusion | flops 201326592 | bytes 9445376 | tf_op jit(solution)/shard_map/ab,bskc->askc/dot_general | solution.py:29
  81.3 1.4 fusion.26
  90.6 3.7 %all-to-all-start.3 = ((bf16[3,8,136,128]{3,2,0,1:T(8,128)(2,1)}), bf16[3,8,136,128]{3,2,0,1:T(8,128)(2,1)S(1)}, u32[]{:S(2)}, u32[]{:S(2)}) async-start(bf16[3,8,136,128]{3,2,0,1:T(8,128)(2,1)} %fusion.76), calls=%async_computation.3 | async-start | bytes 1671168 | tf_op jit(solution)/shard_map/all_to_all | solution.py:301
  94.4 21.3 %all-to-all-done.3 = bf16[3,8,136,128]{3,2,0,1:T(8,128)(2,1)S(1)} async-done(((bf16[3,8,136,128]{3,2,0,1:T(8,128)(2,1)}), bf16[3,8,136,128]{3,2,0,1:T(8,128)(2,1)S(1)}, u32[]{:S(2)}, u32[]{:S(2)}) %all-to-all-start.3) | async-done | bytes 835616 | tf_op jit(solution)/shard_map/all_to_all | solution.py:301
  115.7 3.6 %all-to-all-start.2 = ((bf16[3,8,136,128]{3,2,0,1:T(8,128)(2,1)}), bf16[3,8,136,128]{3,2,0,1:T(8,128)(2,1)S(1)}, u32[]{:S(2)}, u32[]{:S(2)}) async-start(bf16[3,8,136,128]{3,2,0,1:T(8,128)(2,1)} %copy-done.6), calls=%async_computation.2 | async-start | bytes 1671168 | tf_op jit(solution)/shard_map/all_to_all | solution.py:293
  120.6 2.6 %maximum_maximum_fusion = (bf16[136,2048]{1,0:T(8,128)(2,1)}, bf16[1,136,2048]{2,1,0:T(8,128)(2,1)S(1)}, bf16[1,136,2048]{2,1,0:T(8,128)(2,1)S(1)}, bf16[1,136,2048]{2,1,0:T(8,128)(2,1)S(1)}) fusion(bf16[2,2048]{1,0:T(2,128)(2,1)S(1)} %copy-done.20, bf16[128,2048]{1,0:T(8,128)(2,1)} %bitcast.272, bf16[136]{0:T(256)(128)(2,1)S(1)} %pad.9.clone, ...), kind=kLoop, calls=%fused_computation.115 | loop fusion | flops 8077312 | bytes 4383264 | tf_op jit(solution)/shard_map/concatenate | solution.py:316
  123.2 1.4 pad_maximum_fusion.src_ref
  124.6 16.0 %all-to-all-done.2 = bf16[3,8,136,128]{3,2,0,1:T(8,128)(2,1)S(1)} async-done(((bf16[3,8,136,128]{3,2,0,1:T(8,128)(2,1)}), bf16[3,8,136,128]{3,2,0,1:T(8,128)(2,1)S(1)}, u32[]{:S(2)}, u32[]{:S(2)}) %all-to-all-start.2) | async-done | bytes 835616 | tf_op jit(solution)/shard_map/all_to_all | solution.py:293
  140.9 1.7 copy.211
  144.1 1.7 reshape.206
  145.8 2.0 %fusion.92 = (f32[128,2,512]{2,1,0:T(2,128)S(1)}, f32[128,2,512]{2,1,0:T(2,128)S(1)}) fusion(f32[128,4,512]{2,1,0:T(4,128)} %reshape.206), kind=kLoop, calls=%fused_computation.196 | loop fusion | bytes 2097152 | tf_op jit(solution)/shard_map/slice | solution.py:145
  147.8 9.7 %shard_map.297 = (bf16[4,128,2048]{2,1,0:T(8,128)(2,1)}, f32[16,2048]{1,0:T(8,128)}) custom-call(bf16[3,136,2048]{2,1,0:T(8,128)(2,1)} %copy-done, bf16[3,136,2048]{2,1,0:T(8,128)(2,1)} %copy-done, bf16[3,136,2048]{2,1,0:T(8,128)(2,1)} %pad_maximum_fusion.src_ref, bf16[136,2048]{1,0:T(8,128)(2,1)} %get-tuple-element.78.up_ref, f32[8,136,1]{2,1,0:T(8,128)} %copy.212.mask_ref, ...), custom_call_target="tpu_custom_call" | custom-call | tf_op jit(solution)/shard_map/pallas_call | solution.py:209
  159.4 3.6 %all-to-all-start.4 = ((f32[32,1,640]{2,1,0:T(1,128)}), f32[32,1,640]{2,1,0:T(1,128)S(1)}, u32[]{:S(2)}, u32[]{:S(2)}) async-start(f32[32,1,640]{2,1,0:T(1,128)} %reshape.214), calls=%async_computation.4 | async-start | bytes 163840 | tf_op jit(solution)/shard_map/all_to_all | solution.py:130
  163.1 1.8 collective-permute-start.2
  165.0 5.4 %all-to-all-done.4 = f32[32,1,640]{2,1,0:T(1,128)S(1)} async-done(((f32[32,1,640]{2,1,0:T(1,128)}), f32[32,1,640]{2,1,0:T(1,128)S(1)}, u32[]{:S(2)}, u32[]{:S(2)}) %all-to-all-start.4) | async-done | bytes 81952 | tf_op jit(solution)/shard_map/all_to_all | solution.py:130
  172.7 2.6 %all-to-all-start.5 = ((f32[32,1,640]{2,1,0:T(1,128)}), f32[32,1,640]{2,1,0:T(1,128)S(1)}, u32[]{:S(2)}, u32[]{:S(2)}) async-start(f32[32,1,640]{2,1,0:T(1,128)} %reshape.216), calls=%async_computation.5 | async-start | bytes 163840 | tf_op jit(solution)/shard_map/all_to_all | solution.py:132
  175.3 2.9 %fusion.91 = (bf16[1,128,2048]{2,1,0:T(8,128)(2,1)}, bf16[1,128,2048]{2,1,0:T(8,128)(2,1)}, bf16[1,128,2048]{2,1,0:T(8,128)(2,1)}, bf16[1,128,2048]{2,1,0:T(8,128)(2,1)}) fusion(bf16[4,128,2048]{2,1,0:T(8,128)(2,1)} %get-tuple-element.13), kind=kLoop, calls=%fused_computation.195 | loop fusion | bytes 4194304 | tf_op jit(solution)/shard_map/slice | solution.py:321
  178.2 4.6 %all-to-all-done.5 = f32[32,1,640]{2,1,0:T(1,128)S(1)} async-done(((f32[32,1,640]{2,1,0:T(1,128)}), f32[32,1,640]{2,1,0:T(1,128)S(1)}, u32[]{:S(2)}, u32[]{:S(2)}) %all-to-all-start.5) | async-done | bytes 81952 | tf_op jit(solution)/shard_map/all_to_all | solution.py:132
  (196 shorter events, 54.2 us)
Async XLA Ops:
  0.6 14.3 %copy-start.1 = (bf16[1,128,2048]{2,1,0:T(8,128)(2,1)S(1)}, bf16[1,128,2048]{2,1,0:T(8,128)(2,1)}, u32[]{:S(2)}) copy-start(bf16[1,128,2048]{2,1,0:T(8,128)(2,1)} %param.28) | copy-start | bytes 1572868
  0.6 14.1 %copy-start.3 = (bf16[1,128,2048]{2,1,0:T(8,128)(2,1)S(1)}, bf16[1,128,2048]{2,1,0:T(8,128)(2,1)}, u32[]{:S(2)}) copy-start(bf16[1,128,2048]{2,1,0:T(8,128)(2,1)} %param.27) | copy-start | bytes 1572868
  3.2 11.5 %collective-permute-start.1 = (bf16[4,2,2048]{2,1,0:T(2,128)(2,1)S(1)}, bf16[4,2,2048]{2,1,0:T(2,128)(2,1)S(1)}, u32[]{:S(2)}, u32[]{:S(2)}) collective-permute-start(bf16[4,2,2048]{2,1,0:T(2,128)(2,1)S(1)} %pad_maximum_fusion.3), channel_id=1, source_target_pairs={{1,0},{2,1},{3,2},{4,3},{5,4},{6,5},{7,6},{9,8},{10,9},{11,10},{12... | collective-permute-start | bytes 98312 | tf_op jit(solution)/shard_map/ppermute | solution.py:16
  4.6 10.0 %collective-permute-start = (bf16[3,2,2048]{2,1,0:T(2,128)(2,1)S(1)}, bf16[3,2,2048]{2,1,0:T(2,128)(2,1)S(1)}, u32[]{:S(2)}, u32[]{:S(2)}) collective-permute-start(bf16[3,2,2048]{2,1,0:T(2,128)(2,1)S(1)} %pad_maximum_fusion.4), channel_id=1, source_target_pairs={{0,1},{1,2},{2,3},{3,4},{4,5},{5,6},{6,7},{8,9},{9,10},{10,11},{11... | collective-permute-start | bytes 73736 | tf_op jit(solution)/shard_map/ppermute | solution.py:16
  21.2 25.9 %all-to-all-start.1 = ((bf16[3,8,128,128]{3,2,0,1:T(8,128)(2,1)}), bf16[3,8,128,128]{3,2,0,1:T(8,128)(2,1)S(1)}, u32[]{:S(2)}, u32[]{:S(2)}) async-start(bf16[3,8,128,128]{3,2,0,1:T(8,128)(2,1)} %copy.194), calls=%async_computation.1 | async-start | bytes 1572864 | tf_op jit(solution)/shard_map/all_to_all | solution.py:283
  28.6 22.3 %copy-start.34 = (bf16[128,32,1,1]{0,1,3,2:T(8,128)(2,1)S(1)}, bf16[128,32,1,1]{0,1,3,2:T(8,128)(2,1)}, u32[]{:S(2)}) copy-start(bf16[128,32,1,1]{0,1,3,2:T(8,128)(2,1)} %constant.116) | copy-start | bytes 24580
  47.1 23.9 %all-to-all-start = ((bf16[3,8,128,128]{3,2,0,1:T(8,128)(2,1)}), bf16[3,8,128,128]{3,2,0,1:T(8,128)(2,1)S(1)}, u32[]{:S(2)}, u32[]{:S(2)}) async-start(bf16[3,8,128,128]{3,2,0,1:T(8,128)(2,1)} %copy.191), calls=%async_computation | async-start | bytes 1572864 | tf_op jit(solution)/shard_map/all_to_all | solution.py:283
  65.2 5.8 %copy-start.35 = (bf16[128,32,1,1]{0,1,3,2:T(8,128)(2,1)S(1)}, bf16[128,32,1,1]{0,1,3,2:T(8,128)(2,1)}, u32[]{:S(2)}) copy-start(bf16[128,32,1,1]{0,1,3,2:T(8,128)(2,1)} %constant.116) | copy-start | bytes 24580
  65.5 6.6 %copy-start.6 = (bf16[3,8,136,128]{3,2,0,1:T(8,128)(2,1)}, bf16[3,8,136,128]{3,2,0,1:T(8,128)(2,1)S(1)}, u32[]{:S(2)}) copy-start(bf16[3,8,136,128]{3,2,0,1:T(8,128)(2,1)S(1)} %fusion.72) | copy-start | bytes 2506756
  90.5 28.8 %copy-start.37 = (s32[16]{0:T(128)S(1)}, s32[16]{0:T(128)}, u32[]{:S(2)}) copy-start(s32[16]{0:T(128)} %copy-done.36) | copy-start | bytes 196
  90.5 30.0 %copy-start.4 = (bf16[1,128,2048]{2,1,0:T(8,128)(2,1)S(1)}, bf16[1,128,2048]{2,1,0:T(8,128)(2,1)}, u32[]{:S(2)}) copy-start(bf16[1,128,2048]{2,1,0:T(8,128)(2,1)} %param.27) | copy-start | bytes 1572868
  90.5 30.0 %copy-start.10 = (bf16[2,2048]{1,0:T(2,128)(2,1)S(1)}, bf16[2,2048]{1,0:T(2,128)(2,1)}, u32[]{:S(2)}) copy-start(bf16[2,2048]{1,0:T(2,128)(2,1)} %copy-done.9) | copy-start | bytes 24580
  90.5 30.0 %copy-start.12 = (bf16[2,2048]{1,0:T(2,128)(2,1)S(1)}, bf16[2,2048]{1,0:T(2,128)(2,1)}, u32[]{:S(2)}) copy-start(bf16[2,2048]{1,0:T(2,128)(2,1)} %copy-done.11) | copy-start | bytes 24580
  90.5 30.0 %copy-start.14 = (bf16[2,2048]{1,0:T(2,128)(2,1)S(1)}, bf16[2,2048]{1,0:T(2,128)(2,1)}, u32[]{:S(2)}) copy-start(bf16[2,2048]{1,0:T(2,128)(2,1)} %copy-done.13) | copy-start | bytes 24580
  90.5 30.0 %copy-start.16 = (bf16[2,2048]{1,0:T(2,128)(2,1)S(1)}, bf16[2,2048]{1,0:T(2,128)(2,1)}, u32[]{:S(2)}) copy-start(bf16[2,2048]{1,0:T(2,128)(2,1)} %copy-done.15) | copy-start | bytes 24580
  90.5 30.0 %copy-start.18 = (bf16[2,2048]{1,0:T(2,128)(2,1)S(1)}, bf16[2,2048]{1,0:T(2,128)(2,1)}, u32[]{:S(2)}) copy-start(bf16[2,2048]{1,0:T(2,128)(2,1)} %copy-done.17) | copy-start | bytes 24580
  90.5 30.0 %copy-start.20 = (bf16[2,2048]{1,0:T(2,128)(2,1)S(1)}, bf16[2,2048]{1,0:T(2,128)(2,1)}, u32[]{:S(2)}) copy-start(bf16[2,2048]{1,0:T(2,128)(2,1)} %copy-done.19) | copy-start | bytes 24580
  90.6 30.0 %copy-start.22 = (bf16[2,2048]{1,0:T(2,128)(2,1)S(1)}, bf16[2,2048]{1,0:T(2,128)(2,1)}, u32[]{:S(2)}) copy-start(bf16[2,2048]{1,0:T(2,128)(2,1)} %copy-done.21) | copy-start | bytes 24580
  90.6 25.1 %all-to-all-start.3 = ((bf16[3,8,136,128]{3,2,0,1:T(8,128)(2,1)}), bf16[3,8,136,128]{3,2,0,1:T(8,128)(2,1)S(1)}, u32[]{:S(2)}, u32[]{:S(2)}) async-start(bf16[3,8,136,128]{3,2,0,1:T(8,128)(2,1)} %fusion.76), calls=%async_computation.3 | async-start | bytes 1671168 | tf_op jit(solution)/shard_map/all_to_all | solution.py:301
  115.7 25.0 %all-to-all-start.2 = ((bf16[3,8,136,128]{3,2,0,1:T(8,128)(2,1)}), bf16[3,8,136,128]{3,2,0,1:T(8,128)(2,1)S(1)}, u32[]{:S(2)}, u32[]{:S(2)}) async-start(bf16[3,8,136,128]{3,2,0,1:T(8,128)(2,1)} %copy-done.6), calls=%async_computation.2 | async-start | bytes 1671168 | tf_op jit(solution)/shard_map/all_to_all | solution.py:293
  159.4 11.0 %all-to-all-start.4 = ((f32[32,1,640]{2,1,0:T(1,128)}), f32[32,1,640]{2,1,0:T(1,128)S(1)}, u32[]{:S(2)}, u32[]{:S(2)}) async-start(f32[32,1,640]{2,1,0:T(1,128)} %reshape.214), calls=%async_computation.4 | async-start | bytes 163840 | tf_op jit(solution)/shard_map/all_to_all | solution.py:130
  163.1 20.6 %collective-permute-start.2 = (f32[128,2,512]{2,0,1:T(8,128)S(1)}, f32[128,2,512]{2,0,1:T(8,128)S(1)}, u32[]{:S(2)}, u32[]{:S(2)}) collective-permute-start(f32[128,2,512]{2,0,1:T(8,128)S(1)} %copy_select_fusion), channel_id=1, source_target_pairs={{0,16},{8,24},{16,0},{24,8},{1,17},{9,25},{17,1},{25,9},{2,18},{10... | collective-permute-start | bytes 1572872 | tf_op jit(solution)/shard_map/ppermute | solution.py:147
  172.7 10.0 %all-to-all-start.5 = ((f32[32,1,640]{2,1,0:T(1,128)}), f32[32,1,640]{2,1,0:T(1,128)S(1)}, u32[]{:S(2)}, u32[]{:S(2)}) async-start(f32[32,1,640]{2,1,0:T(1,128)} %reshape.216), calls=%async_computation.5 | async-start | bytes 163840 | tf_op jit(solution)/shard_map/all_to_all | solution.py:132
  184.0 1.6 collective-permute-start.3
  (24 other events, 24.8 us)

commit v2 on v1

--- a/solution.py
+++ b/solution.py
@@ -292,6 +292,8 @@
             columns, previous = lax.optimization_barrier((columns, previous))
             returned.append(lax.all_to_all(previous, "ctx", 1, 1, tiled=True))
         spectra = fft_forward(columns)
+        if returned:
+            spectra, returned[-1] = lax.optimization_barrier((spectra, returned[-1]))
         raw = fft_inverse(spectral_products(spectra), seq_len).astype(jnp.bfloat16)
         raw = jnp.concatenate(
             [jnp.zeros((3, head, width), raw.dtype), raw, jnp.zeros((3, frame - rows - head, width), raw.dtype)], 1

time: 188 us -> 190 us (1.011)
  waiting for transfers between devices: 71.3 us -> 52.9 us
  matrix products: 13.8 us -> 21.9 us
  local copies, waits for them, and re-layouts: 35.6 us -> 41.3 us
  other arithmetic: 22 us -> 27.2 us
    all_to_all x2, waiting for transfers between devices: 37.3 us -> 25.4 us  [local(): returned.append(lax.all_to_all(previous, 'ctx', 1, 1, tiled=True))]
    all_to_all x2, waiting for transfers between devices: 24 us -> 17.5 us  [to_columns(): moved = lax.all_to_all(split.transpose(0, 2, 1, 3), 'ctx', 1, 1, tiled=True)]
    unnamed x95 -> x87, local copies, waits for them, and re-layouts: 11 us -> 15 us
    sub x2, other arithmetic: 1.57 us -> 4.41 us  [spectral_products(): m_re * f_re - m_im * f_im]
    dot_general x2, matrix products: 2.04 us -> 4.82 us  [split_product(): return total + jnp.einsum(form, lower, data, preferred_element_type=wide)]
    dot_general x6, matrix products: 9.69 us -> 12.4 us  [split_product(): jnp.einsum(form, upper, data.astype(jnp.bfloat16), preferred_element_type...]
    dot_general x2, matrix products: 2.03 us -> 4.72 us  [split_product(): total = jnp.einsum(form, upper, data, preferred_element_type=wide)]
    add x2, other arithmetic: 1.02 us -> 3.21 us  [spectral_products(): g_re * m_re + g_im * m_im]
  transfers between devices with their start and end apart: 10 -> 10, of which waited for: 6 -> 6; matrix products, arithmetic and copies ran while one was open for 17% -> 26% of each run, Pallas kernels for 0% -> 0%
where the time goes in v2:
time: 190 us; the launch traced here: 188 us
  waiting for transfers between devices  52.9 us (28%)
  local copies, waits for them, and re-layouts  41.3 us (22%)
  starting transfers between devices  33.7 us (18%)
  other arithmetic  27.2 us (14%)
  matrix products  21.9 us (12%)
  Pallas kernels  9.72 us (5%)
    all_to_all x2, waiting for transfers between devices, local(): returned.append(lax.all_to_all(previous, 'ctx', 1, 1, tiled=True))  25.4 us
    all_to_all x2, waiting for transfers between devices, to_columns(): moved = lax.all_to_all(split.transpose(0, 2, 1, 3), 'ctx', 1, 1, tiled=True)  17.5 us
    unnamed x87, local copies, waits for them, and re-layouts  15 us
    dot_general x6, matrix products, split_product(): jnp.einsum(form, upper, data.astype(jnp.bfloat16), preferred_element_type...  12.4 us
    all_to_all x2, starting transfers between devices, to_columns(): moved = lax.all_to_all(split.transpose(0, 2, 1, 3), 'ctx', 1, 1, tiled=True)  9.94 us
    pallas_call x1, Pallas kernels, epilogue(): pl.pallas_call(epilogue_kernel, grid=grid, in_specs=[pl.BlockSpec((None,...  9.72 us
    all_to_all x2, starting transfers between devices, local(): returned.append(lax.all_to_all(previous, 'ctx', 1, 1, tiled=True))  8.87 us
    ppermute x2, starting transfers between devices, shifted(): return lax.ppermute(x, axis, pairs)  6.79 us
  transfers between devices with their start and end apart: 10, of which 6 were waited for; matrix products, arithmetic and copies ran while one was open for 26% of the time, Pallas kernels for 0%

profile of v2, /device:TPU:0, one launch (start us, length us, event | category | flops | bytes accessed | tf_op | source)
XLA Modules:
  0.0 188.3 jit_solution(14810192805330977180)
XLA Ops:
  4.6 5.5 %collective-permute-start = (bf16[3,2,2048]{2,1,0:T(2,128)(2,1)S(1)}, bf16[3,2,2048]{2,1,0:T(2,128)(2,1)S(1)}, u32[]{:S(2)}, u32[]{:S(2)}) collective-permute-start(bf16[3,2,2048]{2,1,0:T(2,128)(2,1)S(1)} %pad_maximum_fusion.4), channel_id=1, source_target_pairs={{0,1},{1,2},{2,3},{3,4},{4,5},{5,6},{6,7},{8,9},{9,10},{10,11},{11... | collective-permute-start | bytes 73736 | tf_op jit(solution)/shard_map/ppermute | solution.py:16
  21.3 6.2 %all-to-all-start.1 = ((bf16[3,8,128,128]{3,2,0,1:T(8,128)(2,1)}), bf16[3,8,128,128]{3,2,0,1:T(8,128)(2,1)S(1)}, u32[]{:S(2)}, u32[]{:S(2)}) async-start(bf16[3,8,128,128]{3,2,0,1:T(8,128)(2,1)} %copy.194), calls=%async_computation.1 | async-start | bytes 1572864 | tf_op jit(solution)/shard_map/all_to_all | solution.py:283
  30.4 16.8 %all-to-all-done.1 = bf16[3,8,128,128]{3,2,0,1:T(8,128)(2,1)S(1)} async-done(((bf16[3,8,128,128]{3,2,0,1:T(8,128)(2,1)}), bf16[3,8,128,128]{3,2,0,1:T(8,128)(2,1)S(1)}, u32[]{:S(2)}, u32[]{:S(2)}) %all-to-all-start.1) | async-done | bytes 786464 | tf_op jit(solution)/shard_map/all_to_all | solution.py:283
  47.2 3.7 %all-to-all-start = ((bf16[3,8,128,128]{3,2,0,1:T(8,128)(2,1)}), bf16[3,8,128,128]{3,2,0,1:T(8,128)(2,1)S(1)}, u32[]{:S(2)}, u32[]{:S(2)}) async-start(bf16[3,8,128,128]{3,2,0,1:T(8,128)(2,1)} %copy.191), calls=%async_computation | async-start | bytes 1572864 | tf_op jit(solution)/shard_map/all_to_all | solution.py:283
  55.4 2.5 %fusion.18 = f32[64,3,64,128]{3,0,2,1:T(8,128)S(1)} fusion(bf16[64,64,1,1]{1,0,3,2:T(8,128)(2,1)S(1)} %copy-done.23, bf16[64,3,64,128]{3,2,1,0:T(8,128)(2,1)S(1)} %bitcast.246), kind=kOutput, calls=%fused_computation.24 | convolution fusion | flops 201326592 | bytes 9445376 | tf_op jit(solution)/shard_map/ab,bskc->askc/dot_general | solution.py:29
  71.1 3.7 %fusion.53 = f32[3,32,128,128]{2,3,1,0:T(8,128)} fusion(bf16[128,32,1,1]{0,1,3,2:T(8,128)(2,1)S(1)} %copy-done.28, bf16[32,3,32,128]{3,2,0,1:T(8,128)(2,1)S(1)} %bitcast.240), kind=kOutput, calls=%fused_computation.105 | convolution fusion | flops 100663296 | bytes 7086080 | tf_op jit(solution)/shard_map/kn,nsqb->ksqb/dot_general | solution.py:31
  74.8 5.1 %all-to-all-start.2 = ((bf16[3,8,136,128]{3,2,0,1:T(8,128)(2,1)}), bf16[3,8,136,128]{3,2,0,1:T(8,128)(2,1)S(1)}, u32[]{:S(2)}, u32[]{:S(2)}) async-start(bf16[3,8,136,128]{3,2,0,1:T(8,128)(2,1)} %fusion.72), calls=%async_computation.2 | async-start | bytes 1671168 | tf_op jit(solution)/shard_map/all_to_all | solution.py:293
  79.9 3.8 %add_bitcast_fusion = f32[128,3,32,128]{3,0,2,1:T(8,128)S(1)} fusion(f32[3,32,128,128]{2,3,1,0:T(8,128)} %fusion.53, bf16[128,32,1,1]{0,1,3,2:T(8,128)(2,1)S(1)} %copy-done.27, bf16[32,3,32,128]{3,2,0,1:T(8,128)(2,1)S(1)} %bitcast.241), kind=kOutput, calls=%fused_computation | convolution fusion | flops 102236160 | bytes 13377536 | tf_op jit(solution)/shard_map/kn,nsqb->ksqb/dot_general | solution.py:32
  86.0 5.2 %fusion.14 = f32[64,3,64,128]{3,0,2,1:T(8,128)} fusion(bf16[64,64,1,1]{1,0,3,2:T(8,128)(2,1)S(1)} %copy-done.23, bf16[64,3,64,128]{3,2,1,0:T(8,128)(2,1)S(1)} %bitcast.244), kind=kOutput, calls=%fused_computation.20 | convolution fusion | flops 201326592 | bytes 9445376 | tf_op jit(solution)/shard_map/ab,bskc->askc/dot_general | solution.py:29
  91.2 9.7 %all-to-all-done.2 = bf16[3,8,136,128]{3,2,0,1:T(8,128)(2,1)S(1)} async-done(((bf16[3,8,136,128]{3,2,0,1:T(8,128)(2,1)}), bf16[3,8,136,128]{3,2,0,1:T(8,128)(2,1)S(1)}, u32[]{:S(2)}, u32[]{:S(2)}) %all-to-all-start.2) | async-done | bytes 835616 | tf_op jit(solution)/shard_map/all_to_all | solution.py:293
  100.9 2.7 %fusion.67 = (bf16[32,64,128]{2,0,1:T(8,128)(2,1)S(1)}, bf16[32,64,128]{2,0,1:T(8,128)(2,1)S(1)}) fusion(f32[64,3,64,128]{3,0,2,1:T(8,128)} %fusion.14), kind=kLoop, calls=%fused_computation.126 | loop fusion | flops 2097152 | bytes 5242880 | tf_op jit(solution)/shard_map/add | solution.py:112
  103.6 3.6 %fusion.63 = (bf16[32,64,128]{2,0,1:T(8,128)(2,1)S(1)}, bf16[32,64,128]{2,0,1:T(8,128)(2,1)S(1)}, bf16[32,64,128]{2,0,1:T(8,128)(2,1)S(1)}, bf16[32,64,128]{2,0,1:T(8,128)(2,1)S(1)}) fusion(f32[64,3,64,128]{3,0,2,1:T(8,128)} %fusion.14), kind=kLoop, calls=%fused_computation.122 | loop fusion | flops 4194304 | bytes 8388608 | tf_op jit(solution)/shard_map/sub | solution.py:110
  117.8 3.8 %all-to-all-start.3 = ((bf16[3,8,136,128]{3,2,0,1:T(8,128)(2,1)}), bf16[3,8,136,128]{3,2,0,1:T(8,128)(2,1)S(1)}, u32[]{:S(2)}, u32[]{:S(2)}) async-start(bf16[3,8,136,128]{3,2,0,1:T(8,128)(2,1)} %fusion.76), calls=%async_computation.3 | async-start | bytes 1671168 | tf_op jit(solution)/shard_map/all_to_all | solution.py:303
  122.9 2.6 %maximum_maximum_fusion = (bf16[136,2048]{1,0:T(8,128)(2,1)}, bf16[1,136,2048]{2,1,0:T(8,128)(2,1)S(1)}, bf16[1,136,2048]{2,1,0:T(8,128)(2,1)S(1)}, bf16[1,136,2048]{2,1,0:T(8,128)(2,1)S(1)}) fusion(bf16[2,2048]{1,0:T(2,128)(2,1)S(1)} %copy-done.19, bf16[128,2048]{1,0:T(8,128)(2,1)} %bitcast.272, bf16[136]{0:T(256)(128)(2,1)S(1)} %copy-done.32, ...), kind=kLoop, calls=%fused_computation.115 | loop fusion | flops 8077312 | bytes 4383264 | tf_op jit(solution)/shard_map/concatenate | solution.py:318
  127.0 15.7 %all-to-all-done.3 = bf16[3,8,136,128]{3,2,0,1:T(8,128)(2,1)S(1)} async-done(((bf16[3,8,136,128]{3,2,0,1:T(8,128)(2,1)}), bf16[3,8,136,128]{3,2,0,1:T(8,128)(2,1)S(1)}, u32[]{:S(2)}, u32[]{:S(2)}) %all-to-all-start.3) | async-done | bytes 835616 | tf_op jit(solution)/shard_map/all_to_all | solution.py:303
  143.0 1.7 copy.211
  147.8 2.0 %fusion.92 = (f32[128,2,512]{2,1,0:T(2,128)S(1)}, f32[128,2,512]{2,1,0:T(2,128)S(1)}) fusion(f32[128,4,512]{2,1,0:T(4,128)} %reshape.206), kind=kLoop, calls=%fused_computation.196 | loop fusion | bytes 2097152 | tf_op jit(solution)/shard_map/slice | solution.py:145
  149.8 9.7 %shard_map.297 = (bf16[4,128,2048]{2,1,0:T(8,128)(2,1)}, f32[16,2048]{1,0:T(8,128)}) custom-call(bf16[3,136,2048]{2,1,0:T(8,128)(2,1)} %copy-done, bf16[3,136,2048]{2,1,0:T(8,128)(2,1)} %copy-done, bf16[3,136,2048]{2,1,0:T(8,128)(2,1)} %pad_maximum_fusion.src_ref, bf16[136,2048]{1,0:T(8,128)(2,1)} %get-tuple-element.82.up_ref, f32[8,136,1]{2,1,0:T(8,128)} %copy.212.mask_ref, ...), custom_call_target="tpu_custom_call" | custom-call | tf_op jit(solution)/shard_map/pallas_call | solution.py:209
  161.4 3.5 %all-to-all-start.4 = ((f32[32,1,640]{2,1,0:T(1,128)}), f32[32,1,640]{2,1,0:T(1,128)S(1)}, u32[]{:S(2)}, u32[]{:S(2)}) async-start(f32[32,1,640]{2,1,0:T(1,128)} %reshape.214), calls=%async_computation.4 | async-start | bytes 163840 | tf_op jit(solution)/shard_map/all_to_all | solution.py:130
  165.1 1.8 collective-permute-start.2
  166.9 5.4 %all-to-all-done.4 = f32[32,1,640]{2,1,0:T(1,128)S(1)} async-done(((f32[32,1,640]{2,1,0:T(1,128)}), f32[32,1,640]{2,1,0:T(1,128)S(1)}, u32[]{:S(2)}, u32[]{:S(2)}) %all-to-all-start.4) | async-done | bytes 81952 | tf_op jit(solution)/shard_map/all_to_all | solution.py:130
  174.6 2.6 %all-to-all-start.5 = ((f32[32,1,640]{2,1,0:T(1,128)}), f32[32,1,640]{2,1,0:T(1,128)S(1)}, u32[]{:S(2)}, u32[]{:S(2)}) async-start(f32[32,1,640]{2,1,0:T(1,128)} %reshape.216), calls=%async_computation.5 | async-start | bytes 163840 | tf_op jit(solution)/shard_map/all_to_all | solution.py:132
  177.2 2.9 %fusion.91 = (bf16[1,128,2048]{2,1,0:T(8,128)(2,1)}, bf16[1,128,2048]{2,1,0:T(8,128)(2,1)}, bf16[1,128,2048]{2,1,0:T(8,128)(2,1)}, bf16[1,128,2048]{2,1,0:T(8,128)(2,1)}) fusion(bf16[4,128,2048]{2,1,0:T(8,128)(2,1)} %get-tuple-element.17), kind=kLoop, calls=%fused_computation.195 | loop fusion | bytes 4194304 | tf_op jit(solution)/shard_map/slice | solution.py:323
  180.1 4.6 %all-to-all-done.5 = f32[32,1,640]{2,1,0:T(1,128)S(1)} async-done(((f32[32,1,640]{2,1,0:T(1,128)}), f32[32,1,640]{2,1,0:T(1,128)S(1)}, u32[]{:S(2)}, u32[]{:S(2)}) %all-to-all-start.5) | async-done | bytes 81952 | tf_op jit(solution)/shard_map/all_to_all | solution.py:132
  (188 shorter events, 61.9 us)
Async XLA Ops:
  0.6 14.4 %copy-start.1 = (bf16[1,128,2048]{2,1,0:T(8,128)(2,1)S(1)}, bf16[1,128,2048]{2,1,0:T(8,128)(2,1)}, u32[]{:S(2)}) copy-start(bf16[1,128,2048]{2,1,0:T(8,128)(2,1)} %param.28) | copy-start | bytes 1572868
  0.6 14.2 %copy-start.3 = (bf16[1,128,2048]{2,1,0:T(8,128)(2,1)S(1)}, bf16[1,128,2048]{2,1,0:T(8,128)(2,1)}, u32[]{:S(2)}) copy-start(bf16[1,128,2048]{2,1,0:T(8,128)(2,1)} %param.27) | copy-start | bytes 1572868
  3.2 11.5 %collective-permute-start.1 = (bf16[4,2,2048]{2,1,0:T(2,128)(2,1)S(1)}, bf16[4,2,2048]{2,1,0:T(2,128)(2,1)S(1)}, u32[]{:S(2)}, u32[]{:S(2)}) collective-permute-start(bf16[4,2,2048]{2,1,0:T(2,128)(2,1)S(1)} %pad_maximum_fusion.3), channel_id=1, source_target_pairs={{1,0},{2,1},{3,2},{4,3},{5,4},{6,5},{7,6},{9,8},{10,9},{11,10},{12... | collective-permute-start | bytes 98312 | tf_op jit(solution)/shard_map/ppermute | solution.py:16
  4.6 10.1 %collective-permute-start = (bf16[3,2,2048]{2,1,0:T(2,128)(2,1)S(1)}, bf16[3,2,2048]{2,1,0:T(2,128)(2,1)S(1)}, u32[]{:S(2)}, u32[]{:S(2)}) collective-permute-start(bf16[3,2,2048]{2,1,0:T(2,128)(2,1)S(1)} %pad_maximum_fusion.4), channel_id=1, source_target_pairs={{0,1},{1,2},{2,3},{3,4},{4,5},{5,6},{6,7},{8,9},{9,10},{10,11},{11... | collective-permute-start | bytes 73736 | tf_op jit(solution)/shard_map/ppermute | solution.py:16
  21.3 25.9 %all-to-all-start.1 = ((bf16[3,8,128,128]{3,2,0,1:T(8,128)(2,1)}), bf16[3,8,128,128]{3,2,0,1:T(8,128)(2,1)S(1)}, u32[]{:S(2)}, u32[]{:S(2)}) async-start(bf16[3,8,128,128]{3,2,0,1:T(8,128)(2,1)} %copy.194), calls=%async_computation.1 | async-start | bytes 1572864 | tf_op jit(solution)/shard_map/all_to_all | solution.py:283
  30.4 20.6 %copy-start.28 = (bf16[128,32,1,1]{0,1,3,2:T(8,128)(2,1)S(1)}, bf16[128,32,1,1]{0,1,3,2:T(8,128)(2,1)}, u32[]{:S(2)}) copy-start(bf16[128,32,1,1]{0,1,3,2:T(8,128)(2,1)} %constant.116) | copy-start | bytes 24580
  47.2 23.9 %all-to-all-start = ((bf16[3,8,128,128]{3,2,0,1:T(8,128)(2,1)}), bf16[3,8,128,128]{3,2,0,1:T(8,128)(2,1)S(1)}, u32[]{:S(2)}, u32[]{:S(2)}) async-start(bf16[3,8,128,128]{3,2,0,1:T(8,128)(2,1)} %copy.191), calls=%async_computation | async-start | bytes 1572864 | tf_op jit(solution)/shard_map/all_to_all | solution.py:283
  74.8 26.0 %all-to-all-start.2 = ((bf16[3,8,136,128]{3,2,0,1:T(8,128)(2,1)}), bf16[3,8,136,128]{3,2,0,1:T(8,128)(2,1)S(1)}, u32[]{:S(2)}, u32[]{:S(2)}) async-start(bf16[3,8,136,128]{3,2,0,1:T(8,128)(2,1)} %fusion.72), calls=%async_computation.2 | async-start | bytes 1671168 | tf_op jit(solution)/shard_map/all_to_all | solution.py:293
  114.3 7.3 %copy-start.29 = (s32[136]{0:T(256)S(1)}, s32[136]{0:T(256)}, u32[]{:S(2)}) copy-start(s32[136]{0:T(256)} %iota_add_fusion) | copy-start | bytes 1636
  114.3 7.3 %copy-start.31 = (s32[16]{0:T(128)S(1)}, s32[16]{0:T(128)}, u32[]{:S(2)}) copy-start(s32[16]{0:T(128)} %copy-done.30) | copy-start | bytes 196
  116.4 6.5 %copy-start.4 = (bf16[1,128,2048]{2,1,0:T(8,128)(2,1)S(1)}, bf16[1,128,2048]{2,1,0:T(8,128)(2,1)}, u32[]{:S(2)}) copy-start(bf16[1,128,2048]{2,1,0:T(8,128)(2,1)} %param.27) | copy-start | bytes 1572868
  116.4 6.5 %copy-start.9 = (bf16[2,2048]{1,0:T(2,128)(2,1)S(1)}, bf16[2,2048]{1,0:T(2,128)(2,1)}, u32[]{:S(2)}) copy-start(bf16[2,2048]{1,0:T(2,128)(2,1)} %copy-done.8) | copy-start | bytes 24580
  116.4 6.5 %copy-start.11 = (bf16[2,2048]{1,0:T(2,128)(2,1)S(1)}, bf16[2,2048]{1,0:T(2,128)(2,1)}, u32[]{:S(2)}) copy-start(bf16[2,2048]{1,0:T(2,128)(2,1)} %copy-done.10) | copy-start | bytes 24580
  116.4 6.5 %copy-start.13 = (bf16[2,2048]{1,0:T(2,128)(2,1)S(1)}, bf16[2,2048]{1,0:T(2,128)(2,1)}, u32[]{:S(2)}) copy-start(bf16[2,2048]{1,0:T(2,128)(2,1)} %copy-done.12) | copy-start | bytes 24580
  116.4 6.5 %copy-start.15 = (bf16[2,2048]{1,0:T(2,128)(2,1)S(1)}, bf16[2,2048]{1,0:T(2,128)(2,1)}, u32[]{:S(2)}) copy-start(bf16[2,2048]{1,0:T(2,128)(2,1)} %copy-done.14) | copy-start | bytes 24580
  116.4 6.5 %copy-start.17 = (bf16[2,2048]{1,0:T(2,128)(2,1)S(1)}, bf16[2,2048]{1,0:T(2,128)(2,1)}, u32[]{:S(2)}) copy-start(bf16[2,2048]{1,0:T(2,128)(2,1)} %copy-done.16) | copy-start | bytes 24580
  116.4 6.5 %copy-start.19 = (bf16[2,2048]{1,0:T(2,128)(2,1)S(1)}, bf16[2,2048]{1,0:T(2,128)(2,1)}, u32[]{:S(2)}) copy-start(bf16[2,2048]{1,0:T(2,128)(2,1)} %copy-done.18) | copy-start | bytes 24580
  116.4 6.5 %copy-start.21 = (bf16[2,2048]{1,0:T(2,128)(2,1)S(1)}, bf16[2,2048]{1,0:T(2,128)(2,1)}, u32[]{:S(2)}) copy-start(bf16[2,2048]{1,0:T(2,128)(2,1)} %copy-done.20) | copy-start | bytes 24580
  116.4 6.5 %copy-start.32 = (bf16[136]{0:T(256)(128)(2,1)S(1)}, bf16[136]{0:T(256)(128)(2,1)}, u32[]{:S(2)}) copy-start(bf16[136]{0:T(256)(128)(2,1)} %pad.9.clone) | copy-start | bytes 820
  117.8 25.0 %all-to-all-start.3 = ((bf16[3,8,136,128]{3,2,0,1:T(8,128)(2,1)}), bf16[3,8,136,128]{3,2,0,1:T(8,128)(2,1)S(1)}, u32[]{:S(2)}, u32[]{:S(2)}) async-start(bf16[3,8,136,128]{3,2,0,1:T(8,128)(2,1)} %fusion.76), calls=%async_computation.3 | async-start | bytes 1671168 | tf_op jit(solution)/shard_map/all_to_all | solution.py:303
  161.4 10.9 %all-to-all-start.4 = ((f32[32,1,640]{2,1,0:T(1,128)}), f32[32,1,640]{2,1,0:T(1,128)S(1)}, u32[]{:S(2)}, u32[]{:S(2)}) async-start(f32[32,1,640]{2,1,0:T(1,128)} %reshape.214), calls=%async_computation.4 | async-start | bytes 163840 | tf_op jit(solution)/shard_map/all_to_all | solution.py:130
  165.1 20.6 %collective-permute-start.2 = (f32[128,2,512]{2,0,1:T(8,128)S(1)}, f32[128,2,512]{2,0,1:T(8,128)S(1)}, u32[]{:S(2)}, u32[]{:S(2)}) collective-permute-start(f32[128,2,512]{2,0,1:T(8,128)S(1)} %copy_select_fusion), channel_id=1, source_target_pairs={{0,16},{8,24},{16,0},{24,8},{1,17},{9,25},{17,1},{25,9},{2,18},{10... | collective-permute-start | bytes 1572872 | tf_op jit(solution)/shard_map/ppermute | solution.py:147
  174.6 10.0 %all-to-all-start.5 = ((f32[32,1,640]{2,1,0:T(1,128)}), f32[32,1,640]{2,1,0:T(1,128)S(1)}, u32[]{:S(2)}, u32[]{:S(2)}) async-start(f32[32,1,640]{2,1,0:T(1,128)} %reshape.216), calls=%async_computation.5 | async-start | bytes 163840 | tf_op jit(solution)/shard_map/all_to_all | solution.py:132
  185.9 1.6 collective-permute-start.3
  (20 other events, 26.7 us)

commit v3 on v1

--- a/solution.py
+++ b/solution.py
@@ -131,6 +131,41 @@
     spread = jnp.broadcast_to(mine[None], (count,) + mine.shape)
     gathered = lax.all_to_all(spread, axes, 0, 0, tiled=True)
     return gathered.transpose(1, 0, 2).reshape(rows, chans)
+
+
+def halving_rows(data, axis):
+    size = lax.axis_size(axis)
+    index = lax.axis_index(axis)
+    blocks = data.reshape(size, data.shape[0] // size, data.shape[1])
+    step = size // 2
+    while step >= 1:
+        half = blocks.shape[0] // 2
+        upper = (index // step) % 2 == 1
+        keep = jnp.where(upper, blocks[half:], blocks[:half])
+        give = jnp.where(upper, blocks[:half], blocks[half:])
+        blocks = keep + lax.ppermute(give, axis, [(i, i ^ step) for i in range(size)])
+        step //= 2
+    return blocks.reshape(-1, data.shape[1])
+
+
+def route_filter_grad(block, rows):
+    parts = lax.axis_size("ctx")
+    groups = lax.axis_size("dp")
+    ratio = parts // groups
+    pieces = block.reshape(ratio, rows, block.shape[1])
+    columns = []
+    for lane_block in range(ratio):
+        total = None
+        for piece in range(ratio):
+            pairs = [
+                (sd * parts + sc, (sc // ratio) * parts + sd * ratio + piece)
+                for sd in range(groups)
+                for sc in range(lane_block, parts, ratio)
+            ]
+            got = lax.ppermute(pieces[piece], ("dp", "ctx"), pairs)
+            total = got if total is None else total + got
+        columns.append(total)
+    return jnp.concatenate(columns, 1)
 
 
 def halving_scatter(data, axis):
@@ -285,6 +320,7 @@
 
     sent = jnp.stack([long_filter, mixed[:rows], grad_conv[:rows]])
     returned = []
+    lagged_parts = []
     previous = None
     for part in range(chunks):
         columns = to_columns(sent, part)
@@ -292,14 +328,18 @@
             columns, previous = lax.optimization_barrier((columns, previous))
             returned.append(lax.all_to_all(previous, "ctx", 1, 1, tiled=True))
         spectra = fft_forward(columns)
-        raw = fft_inverse(spectral_products(spectra), seq_len).astype(jnp.bfloat16)
+        raw = fft_inverse(spectral_products(spectra), seq_len)
+        lagged_parts.append(raw[2])
+        raw = raw[:2].astype(jnp.bfloat16)
         raw = jnp.concatenate(
-            [jnp.zeros((3, head, width), raw.dtype), raw, jnp.zeros((3, frame - rows - head, width), raw.dtype)], 1
+            [jnp.zeros((2, head, width), raw.dtype), raw, jnp.zeros((2, frame - rows - head, width), raw.dtype)], 1
         )
         blocks = jnp.stack([raw[:, j * rows : j * rows + frame] for j in range(parts)], 1)
         previous = blocks
     returned.append(lax.all_to_all(previous, "ctx", 1, 1, tiled=True))
-    back = jnp.stack(returned, 3).transpose(0, 2, 1, 3, 4).reshape(3, frame, chans)
+    back = jnp.stack(returned, 3).transpose(0, 2, 1, 3, 4).reshape(2, frame, chans)
+    lagged = halving_rows(jnp.concatenate(lagged_parts, 1), "dp")
+    filter_part = route_filter_grad(lagged, rows)
 
     spot = index * rows - head + jnp.arange(frame, dtype=jnp.int32)
     spot_begin = jnp.max(jnp.where(starts[None, :] <= spot[:, None], starts[None, :], 0), axis=1)
@@ -319,7 +359,6 @@
     outs, stats = epilogue(back, sources, framed_up, masks[:, :, None], short_weights, skip, rows)
     summed = mesh_sum(stats[: 3 * taps + 1], ("dp", "ctx"))
     gated, grad_q, grad_k, grad_v = outs[0], outs[1], outs[2], outs[3]
-    filter_part = halving_scatter(back[2, head : head + rows].astype(jnp.float32), "dp")
     scale = 1.0 / (groups * seq_len)
     return (
         gated[None],

time: 188 us -> 178 us (0.947)
  waiting for transfers between devices: 71.3 us -> 51 us
  starting transfers between devices: 32.2 us -> 41.4 us
    all_to_all x2, waiting for transfers between devices: 37.3 us -> 11.1 us  [local(): returned.append(lax.all_to_all(previous, 'ctx', 1, 1, tiled=True))]
    ppermute x2 -> x6, waiting for transfers between devices: 0.01 us -> 8.13 us  [the longest x2 8.12 us: halving_rows(): lax.ppermute(give, axis, [(i, i ^ step) for i in range(size)])]
    ppermute x2 -> x6, starting transfers between devices: 2.01 us -> 8.75 us  [the longest x4 7.19 us: route_filter_grad(): got = lax.ppermute(pieces[piece], ('dp', 'ctx'), pairs)]
    all_to_all x2, waiting for transfers between devices: 24 us -> 19.2 us  [to_columns(): moved = lax.all_to_all(split.transpose(0, 2, 1, 3), 'ctx', 1, 1, tiled=True)]
    all_to_all x2, starting transfers between devices: 7.29 us -> 10.8 us  [local(): returned.append(lax.all_to_all(previous, 'ctx', 1, 1, tiled=True))]
    unnamed x95 -> x55, local copies, waits for them, and re-layouts: 11 us -> 14 us
    convert_element_type x3 -> x0, local copies, waits for them, and re-layouts: 2.32 us -> none  [the longest x1 1.7 us: local(): back[2, head:head + rows].astype(jnp.float32)]
  transfers between devices with their start and end apart: 10 -> 14, of which waited for: 6 -> 7; matrix products, arithmetic and copies ran while one was open for 17% -> 23% of each run, Pallas kernels for 0% -> 5%
where the time goes in v3:
time: 178 us; the launch traced here: 177 us
  waiting for transfers between devices  51 us (29%)
  starting transfers between devices  41.4 us (23%)
  local copies, waits for them, and re-layouts  35.5 us (20%)
  other arithmetic  23.8 us (13%)
  matrix products  13.8 us (8%)
  Pallas kernels  9.72 us (5%)
    all_to_all x2, waiting for transfers between devices, to_columns(): moved = lax.all_to_all(split.transpose(0, 2, 1, 3), 'ctx', 1, 1, tiled=True)  19.2 us
    unnamed x55, local copies, waits for them, and re-layouts  14 us
    all_to_all x2, waiting for transfers between devices, local(): returned.append(lax.all_to_all(previous, 'ctx', 1, 1, tiled=True))  11.1 us
    all_to_all x2, starting transfers between devices, local(): returned.append(lax.all_to_all(previous, 'ctx', 1, 1, tiled=True))  10.8 us
    all_to_all x2, starting transfers between devices, to_columns(): moved = lax.all_to_all(split.transpose(0, 2, 1, 3), 'ctx', 1, 1, tiled=True)  9.94 us
    pallas_call x1, Pallas kernels, epilogue(): pl.pallas_call(epilogue_kernel, grid=grid, in_specs=[pl.BlockSpec((None,...  9.72 us
    dot_general x6, matrix products, split_product(): jnp.einsum(form, upper, data.astype(jnp.bfloat16), preferred_element_type...  9.67 us
    ppermute x2, waiting for transfers between devices, halving_rows(): lax.ppermute(give, axis, [(i, i ^ step) for i in range(size)])  8.12 us
  transfers between devices with their start and end apart: 14, of which 7 were waited for; matrix products, arithmetic and copies ran while one was open for 23% of the time, Pallas kernels for 5%

profile of v3, /device:TPU:0, one launch (start us, length us, event | category | flops | bytes accessed | tf_op | source)
XLA Modules:
  0.0 176.8 jit_solution(12033037992865475480)
XLA Ops:
  4.6 5.5 %collective-permute-start = (bf16[3,2,2048]{2,1,0:T(2,128)(2,1)S(1)}, bf16[3,2,2048]{2,1,0:T(2,128)(2,1)S(1)}, u32[]{:S(2)}, u32[]{:S(2)}) collective-permute-start(bf16[3,2,2048]{2,1,0:T(2,128)(2,1)S(1)} %pad_maximum_fusion.5), channel_id=1, source_target_pairs={{0,1},{1,2},{2,3},{3,4},{4,5},{5,6},{6,7},{8,9},{9,10},{10,11},{11... | collective-permute-start | bytes 73736 | tf_op jit(solution)/shard_map/ppermute | solution.py:16
  12.8 1.3 copy.185
  20.6 6.2 %all-to-all-start.1 = ((bf16[3,8,128,128]{3,2,0,1:T(8,128)(2,1)}), bf16[3,8,128,128]{3,2,0,1:T(8,128)(2,1)S(1)}, u32[]{:S(2)}, u32[]{:S(2)}) async-start(bf16[3,8,128,128]{3,2,0,1:T(8,128)(2,1)} %copy.192), calls=%async_computation.1 | async-start | bytes 1572864 | tf_op jit(solution)/shard_map/all_to_all | solution.py:318
  28.1 18.4 %all-to-all-done.1 = bf16[3,8,128,128]{3,2,0,1:T(8,128)(2,1)S(1)} async-done(((bf16[3,8,128,128]{3,2,0,1:T(8,128)(2,1)}), bf16[3,8,128,128]{3,2,0,1:T(8,128)(2,1)S(1)}, u32[]{:S(2)}, u32[]{:S(2)}) %all-to-all-start.1) | async-done | bytes 786464 | tf_op jit(solution)/shard_map/all_to_all | solution.py:318
  46.5 3.7 %all-to-all-start = ((bf16[3,8,128,128]{3,2,0,1:T(8,128)(2,1)}), bf16[3,8,128,128]{3,2,0,1:T(8,128)(2,1)S(1)}, u32[]{:S(2)}, u32[]{:S(2)}) async-start(bf16[3,8,128,128]{3,2,0,1:T(8,128)(2,1)} %copy.189), calls=%async_computation | async-start | bytes 1572864 | tf_op jit(solution)/shard_map/all_to_all | solution.py:318
  54.8 2.5 %fusion.18 = f32[64,3,64,128]{3,0,2,1:T(8,128)S(1)} fusion(bf16[64,64,1,1]{1,0,3,2:T(8,128)(2,1)S(1)} %copy-done.12, bf16[64,3,64,128]{3,2,1,0:T(8,128)(2,1)S(1)} %bitcast.253), kind=kOutput, calls=%fused_computation.24 | convolution fusion | flops 201326592 | bytes 9445376 | tf_op jit(solution)/shard_map/ab,bskc->askc/dot_general | solution.py:29
  60.6 1.3 fusion.22
  74.8 2.5 %fusion.14 = f32[64,3,64,128]{3,0,2,1:T(8,128)S(1)} fusion(bf16[64,64,1,1]{1,0,3,2:T(8,128)(2,1)S(1)} %copy-done.12, bf16[64,3,64,128]{3,2,1,0:T(8,128)(2,1)S(1)} %bitcast.252), kind=kOutput, calls=%fused_computation.20 | convolution fusion | flops 201326592 | bytes 9445376 | tf_op jit(solution)/shard_map/ab,bskc->askc/dot_general | solution.py:29
  80.2 1.3 fusion.26
  89.1 5.0 %all-to-all-start.3 = ((bf16[2,8,136,128]{3,2,0,1:T(8,128)(2,1)}), bf16[2,8,136,128]{3,2,0,1:T(8,128)(2,1)}, u32[]{:S(2)}, u32[]{:S(2)}) async-start(bf16[2,8,136,128]{3,2,0,1:T(8,128)(2,1)} %fusion.71), calls=%async_computation.3 | async-start | bytes 1114112 | tf_op jit(solution)/shard_map/all_to_all | solution.py:339
  96.1 1.5 collective-permute-start.2
  98.7 2.8 %maximum_maximum_fusion = (bf16[136,2048]{1,0:T(8,128)(2,1)}, bf16[1,136,2048]{2,1,0:T(8,128)(2,1)S(1)}, bf16[1,136,2048]{2,1,0:T(8,128)(2,1)S(1)}, bf16[1,136,2048]{2,1,0:T(8,128)(2,1)S(1)}) fusion(bf16[2,2048]{1,0:T(2,128)(2,1)S(1)} %get-tuple-element.75, bf16[128,2048]{1,0:T(8,128)(2,1)} %bitcast.278, bf16[136]{0:T(256)(128)(2,1)S(1)} %pad.13.clone, ...), kind=kLoop, calls=%fused_computation.111 | loop fusion | flops 8077312 | bytes 4383264 | tf_op jit(solution)/shard_map/concatenate | solution.py:356
  101.5 8.0 %collective-permute-done.2 = f32[2,256,256]{2,1,0:T(8,128)} collective-permute-done((f32[2,256,256]{2,1,0:T(8,128)}, f32[2,256,256]{2,1,0:T(8,128)}, u32[]{:S(2)}, u32[]{:S(2)}) %collective-permute-start.2) | collective-permute-done | bytes 524320 | tf_op jit(solution)/shard_map/ppermute | solution.py:146
  110.6 5.7 %all-to-all-start.2 = ((bf16[2,8,136,128]{3,2,0,1:T(8,128)(2,1)}), bf16[2,8,136,128]{3,2,0,1:T(8,128)(2,1)S(1)}, u32[]{:S(2)}, u32[]{:S(2)}) async-start(bf16[2,8,136,128]{3,2,0,1:T(8,128)(2,1)} %fusion.67), calls=%async_computation.2 | async-start | bytes 1114112 | tf_op jit(solution)/shard_map/all_to_all | solution.py:329
  116.4 1.4 pad_maximum_fusion.src_ref
  120.0 4.6 %collective-permute-start.5 = (f32[128,256]{1,0:T(8,128)S(1)}, f32[128,256]{1,0:T(8,128)S(1)}, u32[]{:S(2)}, u32[]{:S(2)}) collective-permute-start(f32[128,256]{1,0:T(8,128)S(1)} %get-tuple-element.62), channel_id=1, source_target_pairs={{0,1},{2,9},{4,17},{6,25},{8,3},{10,11},{12,19},{14,27},{16,5},{18... | collective-permute-start | bytes 393224 | tf_op jit(solution)/shard_map/ppermute | solution.py:165
  126.3 11.1 %all-to-all-done.2 = bf16[2,8,136,128]{3,2,0,1:T(8,128)(2,1)S(1)} async-done(((bf16[2,8,136,128]{3,2,0,1:T(8,128)(2,1)}), bf16[2,8,136,128]{3,2,0,1:T(8,128)(2,1)S(1)}, u32[]{:S(2)}, u32[]{:S(2)}) %all-to-all-start.2) | async-done | bytes 557088 | tf_op jit(solution)/shard_map/all_to_all | solution.py:329
  138.7 1.7 reshape.213.conv_ref.back_ref
  140.4 9.7 %shard_map.297 = (bf16[4,128,2048]{2,1,0:T(8,128)(2,1)}, f32[16,2048]{1,0:T(8,128)}) custom-call(bf16[2,136,2048]{2,1,0:T(8,128)(2,1)} %reshape.213.conv_ref.back_ref, bf16[2,136,2048]{2,1,0:T(8,128)(2,1)} %reshape.213.conv_ref.back_ref, bf16[3,136,2048]{2,1,0:T(8,128)(2,1)} %pad_maximum_fusion.src_ref, bf16[136,2048]{1,0:T(8,128)(2,1)} %get-tuple-element.80.up_ref, ...), custom_call_target="tpu_custom_call" | custom-call | tf_op jit(solution)/shard_map/pallas_call | solution.py:244
  152.0 2.6 %all-to-all-start.4 = ((f32[32,1,640]{2,1,0:T(1,128)}), f32[32,1,640]{2,1,0:T(1,128)S(1)}, u32[]{:S(2)}, u32[]{:S(2)}) async-start(f32[32,1,640]{2,1,0:T(1,128)} %reshape.223), calls=%async_computation.4 | async-start | bytes 163840 | tf_op jit(solution)/shard_map/all_to_all | solution.py:130
  155.4 6.6 %all-to-all-done.4 = f32[32,1,640]{2,1,0:T(1,128)S(1)} async-done(((f32[32,1,640]{2,1,0:T(1,128)}), f32[32,1,640]{2,1,0:T(1,128)S(1)}, u32[]{:S(2)}, u32[]{:S(2)}) %all-to-all-start.4) | async-done | bytes 81952 | tf_op jit(solution)/shard_map/all_to_all | solution.py:130
  164.3 2.6 %all-to-all-start.5 = ((f32[32,1,640]{2,1,0:T(1,128)}), f32[32,1,640]{2,1,0:T(1,128)S(1)}, u32[]{:S(2)}, u32[]{:S(2)}) async-start(f32[32,1,640]{2,1,0:T(1,128)} %reshape.225), calls=%async_computation.5 | async-start | bytes 163840 | tf_op jit(solution)/shard_map/all_to_all | solution.py:132
  166.9 1.3 fusion.86
  168.2 6.1 %all-to-all-done.5 = f32[32,1,640]{2,1,0:T(1,128)S(1)} async-done(((f32[32,1,640]{2,1,0:T(1,128)}), f32[32,1,640]{2,1,0:T(1,128)S(1)}, u32[]{:S(2)}, u32[]{:S(2)}) %all-to-all-start.5) | async-done | bytes 81952 | tf_op jit(solution)/shard_map/all_to_all | solution.py:132
  (171 shorter events, 61.8 us)
Async XLA Ops:
  0.6 13.5 %copy-start = (bf16[1,128,2048]{2,1,0:T(8,128)(2,1)S(1)}, bf16[1,128,2048]{2,1,0:T(8,128)(2,1)}, u32[]{:S(2)}) copy-start(bf16[1,128,2048]{2,1,0:T(8,128)(2,1)} %param.28) | copy-start | bytes 1572868
  0.6 13.7 %copy-start.2 = (bf16[1,128,2048]{2,1,0:T(8,128)(2,1)S(1)}, bf16[1,128,2048]{2,1,0:T(8,128)(2,1)}, u32[]{:S(2)}) copy-start(bf16[1,128,2048]{2,1,0:T(8,128)(2,1)} %param.26) | copy-start | bytes 1572868
  3.2 10.9 %collective-permute-start.1 = (bf16[4,2,2048]{2,1,0:T(2,128)(2,1)S(1)}, bf16[4,2,2048]{2,1,0:T(2,128)(2,1)S(1)}, u32[]{:S(2)}, u32[]{:S(2)}) collective-permute-start(bf16[4,2,2048]{2,1,0:T(2,128)(2,1)S(1)} %pad_maximum_fusion.4), channel_id=1, source_target_pairs={{1,0},{2,1},{3,2},{4,3},{5,4},{6,5},{7,6},{9,8},{10,9},{11,10},{12... | collective-permute-start | bytes 98312 | tf_op jit(solution)/shard_map/ppermute | solution.py:16
  4.6 9.5 %collective-permute-start = (bf16[3,2,2048]{2,1,0:T(2,128)(2,1)S(1)}, bf16[3,2,2048]{2,1,0:T(2,128)(2,1)S(1)}, u32[]{:S(2)}, u32[]{:S(2)}) collective-permute-start(bf16[3,2,2048]{2,1,0:T(2,128)(2,1)S(1)} %pad_maximum_fusion.5), channel_id=1, source_target_pairs={{0,1},{1,2},{2,3},{3,4},{4,5},{5,6},{6,7},{8,9},{9,10},{10,11},{11... | collective-permute-start | bytes 73736 | tf_op jit(solution)/shard_map/ppermute | solution.py:16
  20.6 25.9 %all-to-all-start.1 = ((bf16[3,8,128,128]{3,2,0,1:T(8,128)(2,1)}), bf16[3,8,128,128]{3,2,0,1:T(8,128)(2,1)S(1)}, u32[]{:S(2)}, u32[]{:S(2)}) async-start(bf16[3,8,128,128]{3,2,0,1:T(8,128)(2,1)} %copy.192), calls=%async_computation.1 | async-start | bytes 1572864 | tf_op jit(solution)/shard_map/all_to_all | solution.py:318
  28.1 22.2 %copy-start.17 = (bf16[128,32,1,1]{0,1,3,2:T(8,128)(2,1)S(1)}, bf16[128,32,1,1]{0,1,3,2:T(8,128)(2,1)}, u32[]{:S(2)}) copy-start(bf16[128,32,1,1]{0,1,3,2:T(8,128)(2,1)} %constant.116) | copy-start | bytes 24580
  46.5 23.9 %all-to-all-start = ((bf16[3,8,128,128]{3,2,0,1:T(8,128)(2,1)}), bf16[3,8,128,128]{3,2,0,1:T(8,128)(2,1)S(1)}, u32[]{:S(2)}, u32[]{:S(2)}) async-start(bf16[3,8,128,128]{3,2,0,1:T(8,128)(2,1)} %copy.189), calls=%async_computation | async-start | bytes 1572864 | tf_op jit(solution)/shard_map/all_to_all | solution.py:318
  59.5 1.1 copy-start.9
  59.5 1.1 copy-start.10
  89.1 21.5 %all-to-all-start.3 = ((bf16[2,8,136,128]{3,2,0,1:T(8,128)(2,1)}), bf16[2,8,136,128]{3,2,0,1:T(8,128)(2,1)}, u32[]{:S(2)}, u32[]{:S(2)}) async-start(bf16[2,8,136,128]{3,2,0,1:T(8,128)(2,1)} %fusion.71), calls=%async_computation.3 | async-start | bytes 1114112 | tf_op jit(solution)/shard_map/all_to_all | solution.py:339
  94.7 4.0 %copy-start.1 = (bf16[1,128,2048]{2,1,0:T(8,128)(2,1)S(1)}, bf16[1,128,2048]{2,1,0:T(8,128)(2,1)}, u32[]{:S(2)}) copy-start(bf16[1,128,2048]{2,1,0:T(8,128)(2,1)} %param.28) | copy-start | bytes 1572868
  94.7 4.0 %copy-start.3 = (bf16[1,128,2048]{2,1,0:T(8,128)(2,1)S(1)}, bf16[1,128,2048]{2,1,0:T(8,128)(2,1)}, u32[]{:S(2)}) copy-start(bf16[1,128,2048]{2,1,0:T(8,128)(2,1)} %param.26) | copy-start | bytes 1572868
  94.7 3.9 %copy-start.5 = (bf16[1,128,2048]{2,1,0:T(8,128)(2,1)S(1)}, bf16[1,128,2048]{2,1,0:T(8,128)(2,1)}, u32[]{:S(2)}) copy-start(bf16[1,128,2048]{2,1,0:T(8,128)(2,1)} %param.27) | copy-start | bytes 1572868
  96.1 13.3 %collective-permute-start.2 = (f32[2,256,256]{2,1,0:T(8,128)}, f32[2,256,256]{2,1,0:T(8,128)}, u32[]{:S(2)}, u32[]{:S(2)}) collective-permute-start(f32[2,256,256]{2,1,0:T(8,128)} %bitcast.118), channel_id=1, source_target_pairs={{0,16},{8,24},{16,0},{24,8},{1,17},{9,25},{17,1},{25,9},{2,18},{10... | collective-permute-start | bytes 1572872 | tf_op jit(solution)/shard_map/ppermute | solution.py:146
  98.7 10.7 %copy-start.7 = (f32[512,256]{1,0:T(8,128)S(1)}, f32[512,256]{1,0:T(8,128)}, u32[]{:S(2)}) copy-start(f32[512,256]{1,0:T(8,128)} %get-tuple-element.55) | copy-start | bytes 1572868
  110.6 26.8 %all-to-all-start.2 = ((bf16[2,8,136,128]{3,2,0,1:T(8,128)(2,1)}), bf16[2,8,136,128]{3,2,0,1:T(8,128)(2,1)S(1)}, u32[]{:S(2)}, u32[]{:S(2)}) async-start(bf16[2,8,136,128]{3,2,0,1:T(8,128)(2,1)} %fusion.67), calls=%async_computation.2 | async-start | bytes 1114112 | tf_op jit(solution)/shard_map/all_to_all | solution.py:329
  116.3 1.6 collective-permute-start.3
  118.0 36.5 %collective-permute-start.4 = (f32[128,256]{1,0:T(8,128)S(1)}, f32[128,256]{1,0:T(8,128)S(1)}, u32[]{:S(2)}, u32[]{:S(2)}) collective-permute-start(f32[128,256]{1,0:T(8,128)S(1)} %get-tuple-element.63), channel_id=1, source_target_pairs={{0,0},{2,8},{4,16},{6,24},{8,2},{10,10},{12,18},{14,26},{16,4},{18... | collective-permute-start | bytes 393224 | tf_op jit(solution)/shard_map/ppermute | solution.py:165
  118.7 35.9 %collective-permute-start.6 = (f32[128,256]{1,0:T(8,128)S(1)}, f32[128,256]{1,0:T(8,128)S(1)}, u32[]{:S(2)}, u32[]{:S(2)}) collective-permute-start(f32[128,256]{1,0:T(8,128)S(1)} %get-tuple-element.63), channel_id=1, source_target_pairs={{1,0},{3,8},{5,16},{7,24},{9,2},{11,10},{13,18},{15,26},{17,4},{19... | collective-permute-start | bytes 393224 | tf_op jit(solution)/shard_map/ppermute | solution.py:165
  120.0 34.6 %collective-permute-start.5 = (f32[128,256]{1,0:T(8,128)S(1)}, f32[128,256]{1,0:T(8,128)S(1)}, u32[]{:S(2)}, u32[]{:S(2)}) collective-permute-start(f32[128,256]{1,0:T(8,128)S(1)} %get-tuple-element.62), channel_id=1, source_target_pairs={{0,1},{2,9},{4,17},{6,25},{8,3},{10,11},{12,19},{14,27},{16,5},{18... | collective-permute-start | bytes 393224 | tf_op jit(solution)/shard_map/ppermute | solution.py:165
  124.6 30.1 %collective-permute-start.7 = (f32[128,256]{1,0:T(8,128)S(1)}, f32[128,256]{1,0:T(8,128)S(1)}, u32[]{:S(2)}, u32[]{:S(2)}) collective-permute-start(f32[128,256]{1,0:T(8,128)S(1)} %get-tuple-element.62), channel_id=1, source_target_pairs={{1,1},{3,9},{5,17},{7,25},{9,3},{11,11},{13,19},{15,27},{17,5},{19... | collective-permute-start | bytes 393224 | tf_op jit(solution)/shard_map/ppermute | solution.py:165
  151.2 15.7 %copy-start.8 = (bf16[4,128,2048]{2,1,0:T(8,128)(2,1)S(1)}, bf16[4,128,2048]{2,1,0:T(8,128)(2,1)}, u32[]{:S(2)}) copy-start(bf16[4,128,2048]{2,1,0:T(8,128)(2,1)} %get-tuple-element.13) | copy-start | bytes 6291460
  152.0 10.0 %all-to-all-start.4 = ((f32[32,1,640]{2,1,0:T(1,128)}), f32[32,1,640]{2,1,0:T(1,128)S(1)}, u32[]{:S(2)}, u32[]{:S(2)}) async-start(f32[32,1,640]{2,1,0:T(1,128)} %reshape.223), calls=%async_computation.4 | async-start | bytes 163840 | tf_op jit(solution)/shard_map/all_to_all | solution.py:130
  164.3 10.0 %all-to-all-start.5 = ((f32[32,1,640]{2,1,0:T(1,128)}), f32[32,1,640]{2,1,0:T(1,128)S(1)}, u32[]{:S(2)}, u32[]{:S(2)}) async-start(f32[32,1,640]{2,1,0:T(1,128)} %reshape.225), calls=%async_computation.5 | async-start | bytes 163840 | tf_op jit(solution)/shard_map/all_to_all | solution.py:132
  (8 other events, 7.5 us)

commit v4 on v3

--- a/solution.py
+++ b/solution.py
@@ -1,3 +1,4 @@
+import functools
 import math
 
 import jax
@@ -184,12 +185,13 @@
     return blocks.reshape(rows, chans // size)
 
 
-def epilogue_kernel(conv_ref, back_ref, src_ref, up_ref, mask_ref, w_ref, skip_ref, out_ref, stats_ref):
+def epilogue_kernel(conv_ref, back_ref, src_ref, up_ref, mask_ref, w_ref, skip_ref, *outputs, want_stats):
+    out_ref, stats_ref = (None, outputs[0]) if want_stats else (outputs[0], None)
     wide, narrow = jnp.float32, jnp.bfloat16
     taps = w_ref.shape[1]
     head = taps - 1
     frame = src_ref.shape[1]
-    rows = out_ref.shape[1]
+    rows = out_ref.shape[1] if out_ref is not None else frame - 4 * head
 
     def mask(i):
         return mask_ref[i] > 0.5
@@ -216,33 +218,44 @@
     conv = conv_ref[...].astype(wide) + skip * mixed
     grad_mixed = back_ref[...].astype(wide) + skip * grad_conv
     own = mask(2 * taps)
-    out_ref[0] = lift(q_short * conv, head)[:rows].astype(narrow)
     grads = [upstream * conv, grad_mixed * v_short, grad_mixed * k_short]
+    if not want_stats:
+        out_ref[0] = lift(q_short * conv, head)[:rows].astype(narrow)
+        for i in range(3):
+            grad = grads[i]
+            acc = weights[i, 0:1] * grad
+            for off in range(1, taps):
+                later = lift(jnp.where(mask(taps + off), grad, 0.0), off)
+                acc = acc + weights[i, off : off + 1] * later
+            out_ref[1 + i] = lift(acc, head)[:rows].astype(narrow)
+        return
     stats = []
     for i in range(3):
         grad = grads[i]
-        acc = weights[i, 0:1] * grad
         stats.append(jnp.sum(jnp.where(own, sources[i] * grad, 0.0), axis=0, keepdims=True))
         for off in range(1, taps):
-            later = lift(jnp.where(mask(taps + off), grad, 0.0), off)
-            acc = acc + weights[i, off : off + 1] * later
             lagged = jnp.where(own & mask(off), down(sources[i], off) * grad, 0.0)
             stats.append(jnp.sum(lagged, axis=0, keepdims=True))
-        out_ref[1 + i] = lift(acc, head)[:rows].astype(narrow)
     stats.append(jnp.sum(jnp.where(own, grad_conv * mixed, 0.0), axis=0, keepdims=True))
     width = stats[0].shape[1]
     stats.append(jnp.zeros((stats_ref.shape[0] - len(stats), width), wide))
     stats_ref[...] = jnp.concatenate(stats, 0)
 
 
-def epilogue(back, sources, upstream, masks, short_weights, skip, rows):
+def epilogue(back, sources, upstream, masks, short_weights, skip, rows, want_stats):
     _, frame, chans = back.shape
     taps = short_weights.shape[1]
     block = 256 if chans % 256 == 0 else chans
     grid = (chans // block,)
     stat_rows = 16
+    if want_stats:
+        out_specs = pl.BlockSpec((stat_rows, block), lambda c: (0, c))
+        out_shape = jax.ShapeDtypeStruct((stat_rows, chans), jnp.float32)
+    else:
+        out_specs = pl.BlockSpec((4, rows, block), lambda c: (0, 0, c))
+        out_shape = jax.ShapeDtypeStruct((4, rows, chans), jnp.bfloat16)
     return pl.pallas_call(
-        epilogue_kernel,
+        functools.partial(epilogue_kernel, want_stats=want_stats),
         grid=grid,
         in_specs=[
             pl.BlockSpec((None, frame, block), lambda c: (0, 0, c)),
@@ -253,14 +266,8 @@
             pl.BlockSpec((3, taps, block), lambda c: (0, 0, c)),
             pl.BlockSpec((1, block), lambda c: (0, c)),
         ],
-        out_specs=[
-            pl.BlockSpec((4, rows, block), lambda c: (0, 0, c)),
-            pl.BlockSpec((stat_rows, block), lambda c: (0, c)),
-        ],
-        out_shape=[
-            jax.ShapeDtypeStruct((4, rows, chans), jnp.bfloat16),
-            jax.ShapeDtypeStruct((stat_rows, chans), jnp.float32),
-        ],
+        out_specs=out_specs,
+        out_shape=out_shape,
     )(back, back, sources, upstream, masks, short_weights, skip[None])
 
 
@@ -356,8 +363,10 @@
     framed_up = jnp.concatenate(
         [jnp.zeros((head, chans), c_rows.dtype), c_rows, nxt[3], jnp.zeros((tail, chans), c_rows.dtype)], 0
     )
-    outs, stats = epilogue(back, sources, framed_up, masks[:, :, None], short_weights, skip, rows)
+    operands = (back, sources, framed_up, masks[:, :, None], short_weights, skip, rows)
+    stats = epilogue(*operands, True)
     summed = mesh_sum(stats[: 3 * taps + 1], ("dp", "ctx"))
+    outs = epilogue(*operands, False)
     gated, grad_q, grad_k, grad_v = outs[0], outs[1], outs[2], outs[3]
     scale = 1.0 / (groups * seq_len)
     return (

time: 178 us -> 182 us (1.022)
  waiting for transfers between devices: 51 us -> 42.9 us
  Pallas kernels: 9.72 us -> 16.4 us
  starting transfers between devices: 41.4 us -> 44.7 us
    pallas_call x1 -> x2, Pallas kernels: 9.72 us -> 16.4 us  [epilogue(): pl.pallas_call(functools.partial(epilogue_kernel, want_stats=want_stats),...]
    all_to_all x1, waiting for transfers between devices: 6.61 us -> 0.01 us  [mesh_sum(): mine = jnp.sum(lax.all_to_all(pieces, axes, 0, 0, tiled=True), axis=0)]
    all_to_all x1, starting transfers between devices: 2.57 us -> 5.83 us  [mesh_sum(): gathered = lax.all_to_all(spread, axes, 0, 0, tiled=True)]
    unnamed x55 -> x53, local copies, waits for them, and re-layouts: 14 us -> 14 us
  transfers between devices with their start and end apart: 14 -> 14, of which waited for: 7 -> 6; matrix products, arithmetic and copies ran while one was open for 23% -> 23% of each run, Pallas kernels for 5% -> 9%
where the time goes in v4:
time: 182 us; the launch traced here: 180 us
  starting transfers between devices  44.7 us (25%)
  waiting for transfers between devices  42.9 us (24%)
  local copies, waits for them, and re-layouts  37 us (20%)
  other arithmetic  23.8 us (13%)
  Pallas kernels  16.4 us (9%)
  matrix products  13.8 us (8%)
    all_to_all x2, waiting for transfers between devices, to_columns(): moved = lax.all_to_all(split.transpose(0, 2, 1, 3), 'ctx', 1, 1, tiled=True)  19.1 us
    pallas_call x2, Pallas kernels, epilogue(): pl.pallas_call(functools.partial(epilogue_kernel, want_stats=want_stats),...  16.4 us
    unnamed x53, local copies, waits for them, and re-layouts  14 us
    all_to_all x2, waiting for transfers between devices, local(): returned.append(lax.all_to_all(previous, 'ctx', 1, 1, tiled=True))  11.1 us
    all_to_all x2, starting transfers between devices, local(): returned.append(lax.all_to_all(previous, 'ctx', 1, 1, tiled=True))  10.8 us
    all_to_all x2, starting transfers between devices, to_columns(): moved = lax.all_to_all(split.transpose(0, 2, 1, 3), 'ctx', 1, 1, tiled=True)  9.94 us
    dot_general x6, matrix products, split_product(): jnp.einsum(form, upper, data.astype(jnp.bfloat16), preferred_element_type...  9.68 us
    ppermute x2, waiting for transfers between devices, halving_rows(): lax.ppermute(give, axis, [(i, i ^ step) for i in range(size)])  8.13 us
  transfers between devices with their start and end apart: 14, of which 6 were waited for; matrix products, arithmetic and copies ran while one was open for 23% of the time, Pallas kernels for 9%

profile of v4, /device:TPU:0, one launch (start us, length us, event | category | flops | bytes accessed | tf_op | source)
XLA Modules:
  0.0 180.2 jit_solution(15665472899209743612)
XLA Ops:
  4.6 5.5 %collective-permute-start = (bf16[3,2,2048]{2,1,0:T(2,128)(2,1)S(1)}, bf16[3,2,2048]{2,1,0:T(2,128)(2,1)S(1)}, u32[]{:S(2)}, u32[]{:S(2)}) collective-permute-start(bf16[3,2,2048]{2,1,0:T(2,128)(2,1)S(1)} %pad_maximum_fusion.5), channel_id=1, source_target_pairs={{0,1},{1,2},{2,3},{3,4},{4,5},{5,6},{6,7},{8,9},{9,10},{10,11},{11... | collective-permute-start | bytes 73736 | tf_op jit(solution)/shard_map/ppermute | solution.py:17
  12.8 1.3 copy.190
  20.6 6.2 %all-to-all-start.1 = ((bf16[3,8,128,128]{3,2,0,1:T(8,128)(2,1)}), bf16[3,8,128,128]{3,2,0,1:T(8,128)(2,1)S(1)}, u32[]{:S(2)}, u32[]{:S(2)}) async-start(bf16[3,8,128,128]{3,2,0,1:T(8,128)(2,1)} %copy.197), calls=%async_computation.1 | async-start | bytes 1572864 | tf_op jit(solution)/shard_map/all_to_all | solution.py:325
  28.1 18.4 %all-to-all-done.1 = bf16[3,8,128,128]{3,2,0,1:T(8,128)(2,1)S(1)} async-done(((bf16[3,8,128,128]{3,2,0,1:T(8,128)(2,1)}), bf16[3,8,128,128]{3,2,0,1:T(8,128)(2,1)S(1)}, u32[]{:S(2)}, u32[]{:S(2)}) %all-to-all-start.1) | async-done | bytes 786464 | tf_op jit(solution)/shard_map/all_to_all | solution.py:325
  46.5 3.7 %all-to-all-start = ((bf16[3,8,128,128]{3,2,0,1:T(8,128)(2,1)}), bf16[3,8,128,128]{3,2,0,1:T(8,128)(2,1)S(1)}, u32[]{:S(2)}, u32[]{:S(2)}) async-start(bf16[3,8,128,128]{3,2,0,1:T(8,128)(2,1)} %copy.194), calls=%async_computation | async-start | bytes 1572864 | tf_op jit(solution)/shard_map/all_to_all | solution.py:325
  54.8 2.5 %fusion.18 = f32[64,3,64,128]{3,0,2,1:T(8,128)S(1)} fusion(bf16[64,64,1,1]{1,0,3,2:T(8,128)(2,1)S(1)} %copy-done.11, bf16[64,3,64,128]{3,2,1,0:T(8,128)(2,1)S(1)} %bitcast.253), kind=kOutput, calls=%fused_computation.24 | convolution fusion | flops 201326592 | bytes 9445376 | tf_op jit(solution)/shard_map/ab,bskc->askc/dot_general | solution.py:30
  60.6 1.3 fusion.22
  74.8 2.5 %fusion.14 = f32[64,3,64,128]{3,0,2,1:T(8,128)S(1)} fusion(bf16[64,64,1,1]{1,0,3,2:T(8,128)(2,1)S(1)} %copy-done.11, bf16[64,3,64,128]{3,2,1,0:T(8,128)(2,1)S(1)} %bitcast.252), kind=kOutput, calls=%fused_computation.20 | convolution fusion | flops 201326592 | bytes 9445376 | tf_op jit(solution)/shard_map/ab,bskc->askc/dot_general | solution.py:30
  80.2 1.3 fusion.26
  89.1 5.1 %all-to-all-start.3 = ((bf16[2,8,136,128]{3,2,0,1:T(8,128)(2,1)}), bf16[2,8,136,128]{3,2,0,1:T(8,128)(2,1)}, u32[]{:S(2)}, u32[]{:S(2)}) async-start(bf16[2,8,136,128]{3,2,0,1:T(8,128)(2,1)} %fusion.71), calls=%async_computation.3 | async-start | bytes 1114112 | tf_op jit(solution)/shard_map/all_to_all | solution.py:346
  96.2 1.5 collective-permute-start.2
  98.7 2.8 %maximum_maximum_fusion = (bf16[136,2048]{1,0:T(8,128)(2,1)}, bf16[1,136,2048]{2,1,0:T(8,128)(2,1)S(1)}, bf16[1,136,2048]{2,1,0:T(8,128)(2,1)S(1)}, bf16[1,136,2048]{2,1,0:T(8,128)(2,1)S(1)}) fusion(bf16[2,2048]{1,0:T(2,128)(2,1)S(1)} %get-tuple-element.71, bf16[128,2048]{1,0:T(8,128)(2,1)} %bitcast.278, bf16[136]{0:T(256)(128)(2,1)S(1)} %pad.13.clone, ...), kind=kLoop, calls=%fused_computation.111 | loop fusion | flops 8077312 | bytes 4383264 | tf_op jit(solution)/shard_map/concatenate | solution.py:363
  101.5 8.0 %collective-permute-done.2 = f32[2,256,256]{2,1,0:T(8,128)} collective-permute-done((f32[2,256,256]{2,1,0:T(8,128)}, f32[2,256,256]{2,1,0:T(8,128)}, u32[]{:S(2)}, u32[]{:S(2)}) %collective-permute-start.2) | collective-permute-done | bytes 524320 | tf_op jit(solution)/shard_map/ppermute | solution.py:147
  110.6 5.7 %all-to-all-start.2 = ((bf16[2,8,136,128]{3,2,0,1:T(8,128)(2,1)}), bf16[2,8,136,128]{3,2,0,1:T(8,128)(2,1)S(1)}, u32[]{:S(2)}, u32[]{:S(2)}) async-start(bf16[2,8,136,128]{3,2,0,1:T(8,128)(2,1)} %fusion.67), calls=%async_computation.2 | async-start | bytes 1114112 | tf_op jit(solution)/shard_map/all_to_all | solution.py:336
  116.5 1.4 pad_maximum_fusion.src_ref
  120.1 4.6 %collective-permute-start.5 = (f32[128,256]{1,0:T(8,128)S(1)}, f32[128,256]{1,0:T(8,128)S(1)}, u32[]{:S(2)}, u32[]{:S(2)}) collective-permute-start(f32[128,256]{1,0:T(8,128)S(1)} %get-tuple-element.58), channel_id=1, source_target_pairs={{0,1},{2,9},{4,17},{6,25},{8,3},{10,11},{12,19},{14,27},{16,5},{18... | collective-permute-start | bytes 393224 | tf_op jit(solution)/shard_map/ppermute | solution.py:166
  126.4 11.1 %all-to-all-done.2 = bf16[2,8,136,128]{3,2,0,1:T(8,128)(2,1)S(1)} async-done(((bf16[2,8,136,128]{3,2,0,1:T(8,128)(2,1)}), bf16[2,8,136,128]{3,2,0,1:T(8,128)(2,1)S(1)}, u32[]{:S(2)}, u32[]{:S(2)}) %all-to-all-start.2) | async-done | bytes 557088 | tf_op jit(solution)/shard_map/all_to_all | solution.py:336
  138.8 1.7 reshape.213.conv_ref.back_ref
  140.4 7.9 %shard_map.298 = f32[16,2048]{1,0:T(8,128)} custom-call(bf16[2,136,2048]{2,1,0:T(8,128)(2,1)} %reshape.213.conv_ref.back_ref, bf16[2,136,2048]{2,1,0:T(8,128)(2,1)} %reshape.213.conv_ref.back_ref, bf16[3,136,2048]{2,1,0:T(8,128)(2,1)} %pad_maximum_fusion.src_ref, bf16[136,2048]{1,0:T(8,128)(2,1)} %get-tuple-element.76.up_ref, f32[8,136,1]{2,1,0:T(8,128)} %copy.215.mask_ref, ...), custom_call_target="tpu_custom_call" | custom-call | tf_op jit(solution)/shard_map/pallas_call | solution.py:257
  150.2 2.6 %all-to-all-start.4 = ((f32[32,1,640]{2,1,0:T(1,128)}), f32[32,1,640]{2,1,0:T(1,128)S(1)}, u32[]{:S(2)}, u32[]{:S(2)}) async-start(f32[32,1,640]{2,1,0:T(1,128)} %reshape.223), calls=%async_computation.4 | async-start | bytes 163840 | tf_op jit(solution)/shard_map/all_to_all | solution.py:131
  153.6 8.6 %shard_map.297 = bf16[4,128,2048]{2,1,0:T(8,128)(2,1)} custom-call(bf16[2,136,2048]{2,1,0:T(8,128)(2,1)} %reshape.213.conv_ref.back_ref, bf16[2,136,2048]{2,1,0:T(8,128)(2,1)} %reshape.213.conv_ref.back_ref, bf16[3,136,2048]{2,1,0:T(8,128)(2,1)} %pad_maximum_fusion.src_ref, bf16[136,2048]{1,0:T(8,128)(2,1)} %get-tuple-element.76.up_ref, ...), custom_call_target="tpu_custom_call" | custom-call | tf_op jit(solution)/shard_map/pallas_call | solution.py:257
  164.5 5.8 %all-to-all-start.5 = ((f32[32,1,640]{2,1,0:T(1,128)}), f32[32,1,640]{2,1,0:T(1,128)S(1)}, u32[]{:S(2)}, u32[]{:S(2)}) async-start(f32[32,1,640]{2,1,0:T(1,128)} %reshape.225), calls=%async_computation.5 | async-start | bytes 163840 | tf_op jit(solution)/shard_map/all_to_all | solution.py:133
  170.3 2.9 %fusion.86 = (bf16[1,128,2048]{2,1,0:T(8,128)(2,1)}, bf16[1,128,2048]{2,1,0:T(8,128)(2,1)}, bf16[1,128,2048]{2,1,0:T(8,128)(2,1)}, bf16[1,128,2048]{2,1,0:T(8,128)(2,1)}) fusion(bf16[4,128,2048]{2,1,0:T(8,128)(2,1)} %shard_map.297), kind=kLoop, calls=%fused_computation.201 | loop fusion | bytes 4194304 | tf_op jit(solution)/shard_map/slice | solution.py:370
  173.2 4.6 %all-to-all-done.5 = f32[32,1,640]{2,1,0:T(1,128)S(1)} async-done(((f32[32,1,640]{2,1,0:T(1,128)}), f32[32,1,640]{2,1,0:T(1,128)S(1)}, u32[]{:S(2)}, u32[]{:S(2)}) %all-to-all-start.5) | async-done | bytes 81952 | tf_op jit(solution)/shard_map/all_to_all | solution.py:133
  (170 shorter events, 61.8 us)
Async XLA Ops:
  0.6 13.5 %copy-start = (bf16[1,128,2048]{2,1,0:T(8,128)(2,1)S(1)}, bf16[1,128,2048]{2,1,0:T(8,128)(2,1)}, u32[]{:S(2)}) copy-start(bf16[1,128,2048]{2,1,0:T(8,128)(2,1)} %param.28) | copy-start | bytes 1572868
  0.6 13.7 %copy-start.2 = (bf16[1,128,2048]{2,1,0:T(8,128)(2,1)S(1)}, bf16[1,128,2048]{2,1,0:T(8,128)(2,1)}, u32[]{:S(2)}) copy-start(bf16[1,128,2048]{2,1,0:T(8,128)(2,1)} %param.26) | copy-start | bytes 1572868
  3.2 10.9 %collective-permute-start.1 = (bf16[4,2,2048]{2,1,0:T(2,128)(2,1)S(1)}, bf16[4,2,2048]{2,1,0:T(2,128)(2,1)S(1)}, u32[]{:S(2)}, u32[]{:S(2)}) collective-permute-start(bf16[4,2,2048]{2,1,0:T(2,128)(2,1)S(1)} %pad_maximum_fusion.4), channel_id=1, source_target_pairs={{1,0},{2,1},{3,2},{4,3},{5,4},{6,5},{7,6},{9,8},{10,9},{11,10},{12... | collective-permute-start | bytes 98312 | tf_op jit(solution)/shard_map/ppermute | solution.py:17
  4.6 9.5 %collective-permute-start = (bf16[3,2,2048]{2,1,0:T(2,128)(2,1)S(1)}, bf16[3,2,2048]{2,1,0:T(2,128)(2,1)S(1)}, u32[]{:S(2)}, u32[]{:S(2)}) collective-permute-start(bf16[3,2,2048]{2,1,0:T(2,128)(2,1)S(1)} %pad_maximum_fusion.5), channel_id=1, source_target_pairs={{0,1},{1,2},{2,3},{3,4},{4,5},{5,6},{6,7},{8,9},{9,10},{10,11},{11... | collective-permute-start | bytes 73736 | tf_op jit(solution)/shard_map/ppermute | solution.py:17
  20.6 25.9 %all-to-all-start.1 = ((bf16[3,8,128,128]{3,2,0,1:T(8,128)(2,1)}), bf16[3,8,128,128]{3,2,0,1:T(8,128)(2,1)S(1)}, u32[]{:S(2)}, u32[]{:S(2)}) async-start(bf16[3,8,128,128]{3,2,0,1:T(8,128)(2,1)} %copy.197), calls=%async_computation.1 | async-start | bytes 1572864 | tf_op jit(solution)/shard_map/all_to_all | solution.py:325
  28.1 22.2 %copy-start.16 = (bf16[128,32,1,1]{0,1,3,2:T(8,128)(2,1)S(1)}, bf16[128,32,1,1]{0,1,3,2:T(8,128)(2,1)}, u32[]{:S(2)}) copy-start(bf16[128,32,1,1]{0,1,3,2:T(8,128)(2,1)} %constant.116) | copy-start | bytes 24580
  46.5 23.9 %all-to-all-start = ((bf16[3,8,128,128]{3,2,0,1:T(8,128)(2,1)}), bf16[3,8,128,128]{3,2,0,1:T(8,128)(2,1)S(1)}, u32[]{:S(2)}, u32[]{:S(2)}) async-start(bf16[3,8,128,128]{3,2,0,1:T(8,128)(2,1)} %copy.194), calls=%async_computation | async-start | bytes 1572864 | tf_op jit(solution)/shard_map/all_to_all | solution.py:325
  51.3 1.1 copy-start.12
  59.5 1.1 copy-start.8
  59.5 1.1 copy-start.9
  89.1 21.5 %all-to-all-start.3 = ((bf16[2,8,136,128]{3,2,0,1:T(8,128)(2,1)}), bf16[2,8,136,128]{3,2,0,1:T(8,128)(2,1)}, u32[]{:S(2)}, u32[]{:S(2)}) async-start(bf16[2,8,136,128]{3,2,0,1:T(8,128)(2,1)} %fusion.71), calls=%async_computation.3 | async-start | bytes 1114112 | tf_op jit(solution)/shard_map/all_to_all | solution.py:346
  94.8 4.0 %copy-start.1 = (bf16[1,128,2048]{2,1,0:T(8,128)(2,1)S(1)}, bf16[1,128,2048]{2,1,0:T(8,128)(2,1)}, u32[]{:S(2)}) copy-start(bf16[1,128,2048]{2,1,0:T(8,128)(2,1)} %param.28) | copy-start | bytes 1572868
  94.8 4.0 %copy-start.3 = (bf16[1,128,2048]{2,1,0:T(8,128)(2,1)S(1)}, bf16[1,128,2048]{2,1,0:T(8,128)(2,1)}, u32[]{:S(2)}) copy-start(bf16[1,128,2048]{2,1,0:T(8,128)(2,1)} %param.26) | copy-start | bytes 1572868
  94.8 3.9 %copy-start.5 = (bf16[1,128,2048]{2,1,0:T(8,128)(2,1)S(1)}, bf16[1,128,2048]{2,1,0:T(8,128)(2,1)}, u32[]{:S(2)}) copy-start(bf16[1,128,2048]{2,1,0:T(8,128)(2,1)} %param.27) | copy-start | bytes 1572868
  96.2 13.3 %collective-permute-start.2 = (f32[2,256,256]{2,1,0:T(8,128)}, f32[2,256,256]{2,1,0:T(8,128)}, u32[]{:S(2)}, u32[]{:S(2)}) collective-permute-start(f32[2,256,256]{2,1,0:T(8,128)} %bitcast.118), channel_id=1, source_target_pairs={{0,16},{8,24},{16,0},{24,8},{1,17},{9,25},{17,1},{25,9},{2,18},{10... | collective-permute-start | bytes 1572872 | tf_op jit(solution)/shard_map/ppermute | solution.py:147
  98.7 10.7 %copy-start.7 = (f32[512,256]{1,0:T(8,128)S(1)}, f32[512,256]{1,0:T(8,128)}, u32[]{:S(2)}) copy-start(f32[512,256]{1,0:T(8,128)} %get-tuple-element.51) | copy-start | bytes 1572868
  110.6 26.8 %all-to-all-start.2 = ((bf16[2,8,136,128]{3,2,0,1:T(8,128)(2,1)}), bf16[2,8,136,128]{3,2,0,1:T(8,128)(2,1)S(1)}, u32[]{:S(2)}, u32[]{:S(2)}) async-start(bf16[2,8,136,128]{3,2,0,1:T(8,128)(2,1)} %fusion.67), calls=%async_computation.2 | async-start | bytes 1114112 | tf_op jit(solution)/shard_map/all_to_all | solution.py:336
  116.4 1.6 collective-permute-start.3
  118.1 34.7 %collective-permute-start.4 = (f32[128,256]{1,0:T(8,128)S(1)}, f32[128,256]{1,0:T(8,128)S(1)}, u32[]{:S(2)}, u32[]{:S(2)}) collective-permute-start(f32[128,256]{1,0:T(8,128)S(1)} %get-tuple-element.59), channel_id=1, source_target_pairs={{0,0},{2,8},{4,16},{6,24},{8,2},{10,10},{12,18},{14,26},{16,4},{18... | collective-permute-start | bytes 393224 | tf_op jit(solution)/shard_map/ppermute | solution.py:166
  118.8 34.1 %collective-permute-start.6 = (f32[128,256]{1,0:T(8,128)S(1)}, f32[128,256]{1,0:T(8,128)S(1)}, u32[]{:S(2)}, u32[]{:S(2)}) collective-permute-start(f32[128,256]{1,0:T(8,128)S(1)} %get-tuple-element.59), channel_id=1, source_target_pairs={{1,0},{3,8},{5,16},{7,24},{9,2},{11,10},{13,18},{15,26},{17,4},{19... | collective-permute-start | bytes 393224 | tf_op jit(solution)/shard_map/ppermute | solution.py:166
  120.1 32.7 %collective-permute-start.5 = (f32[128,256]{1,0:T(8,128)S(1)}, f32[128,256]{1,0:T(8,128)S(1)}, u32[]{:S(2)}, u32[]{:S(2)}) collective-permute-start(f32[128,256]{1,0:T(8,128)S(1)} %get-tuple-element.58), channel_id=1, source_target_pairs={{0,1},{2,9},{4,17},{6,25},{8,3},{10,11},{12,19},{14,27},{16,5},{18... | collective-permute-start | bytes 393224 | tf_op jit(solution)/shard_map/ppermute | solution.py:166
  124.6 28.2 %collective-permute-start.7 = (f32[128,256]{1,0:T(8,128)S(1)}, f32[128,256]{1,0:T(8,128)S(1)}, u32[]{:S(2)}, u32[]{:S(2)}) collective-permute-start(f32[128,256]{1,0:T(8,128)S(1)} %get-tuple-element.58), channel_id=1, source_target_pairs={{1,1},{3,9},{5,17},{7,25},{9,3},{11,11},{13,19},{15,27},{17,5},{19... | collective-permute-start | bytes 393224 | tf_op jit(solution)/shard_map/ppermute | solution.py:166
  150.2 12.0 %all-to-all-start.4 = ((f32[32,1,640]{2,1,0:T(1,128)}), f32[32,1,640]{2,1,0:T(1,128)S(1)}, u32[]{:S(2)}, u32[]{:S(2)}) async-start(f32[32,1,640]{2,1,0:T(1,128)} %reshape.223), calls=%async_computation.4 | async-start | bytes 163840 | tf_op jit(solution)/shard_map/all_to_all | solution.py:131
  164.5 13.3 %all-to-all-start.5 = ((f32[32,1,640]{2,1,0:T(1,128)}), f32[32,1,640]{2,1,0:T(1,128)S(1)}, u32[]{:S(2)}, u32[]{:S(2)}) async-start(f32[32,1,640]{2,1,0:T(1,128)} %reshape.225), calls=%async_computation.5 | async-start | bytes 163840 | tf_op jit(solution)/shard_map/all_to_all | solution.py:133
  (7 other events, 6.4 us)

commit v5 on v3

--- a/solution.py
+++ b/solution.py
@@ -338,7 +338,8 @@
         previous = blocks
     returned.append(lax.all_to_all(previous, "ctx", 1, 1, tiled=True))
     back = jnp.stack(returned, 3).transpose(0, 2, 1, 3, 4).reshape(2, frame, chans)
-    lagged = halving_rows(jnp.concatenate(lagged_parts, 1), "dp")
+    lagged, back = lax.optimization_barrier((jnp.concatenate(lagged_parts, 1), back))
+    lagged = halving_rows(lagged, "dp")
     filter_part = route_filter_grad(lagged, rows)
 
     spot = index * rows - head + jnp.arange(frame, dtype=jnp.int32)

time: 178 us -> 194 us (1.090)
  the two profiles are of different devices: /device:TPU:0 before, /device:TPU:6 now
where the time goes in v5:
time: 194 us; the launch traced here: 192 us
  waiting for transfers between devices  58.7 us (30%)
  starting transfers between devices  48.7 us (25%)
  local copies, waits for them, and re-layouts  36.6 us (19%)
  other arithmetic  23.3 us (12%)
  matrix products  13.7 us (7%)
  Pallas kernels  9.72 us (5%)
    all_to_all x2, waiting for transfers between devices, local(): returned.append(lax.all_to_all(previous, 'ctx', 1, 1, tiled=True))  25.4 us
    all_to_all x2, waiting for transfers between devices, to_columns(): moved = lax.all_to_all(split.transpose(0, 2, 1, 3), 'ctx', 1, 1, tiled=True)  18.1 us
    unnamed x55, local copies, waits for them, and re-layouts  14.1 us
    ppermute x4, starting transfers between devices, route_filter_grad(): got = lax.ppermute(pieces[piece], ('dp', 'ctx'), pairs)  13.2 us
    all_to_all x2, starting transfers between devices, local(): returned.append(lax.all_to_all(previous, 'ctx', 1, 1, tiled=True))  10.4 us
    pallas_call x1, Pallas kernels, epilogue(): pl.pallas_call(epilogue_kernel, grid=grid, in_specs=[pl.BlockSpec((None,...  9.72 us
    dot_general x6, matrix products, split_product(): jnp.einsum(form, upper, data.astype(jnp.bfloat16), preferred_element_type...  9.67 us
    all_to_all x2, starting transfers between devices, to_columns(): moved = lax.all_to_all(split.transpose(0, 2, 1, 3), 'ctx', 1, 1, tiled=True)  9.54 us
  transfers between devices with their start and end apart: 14, of which 8 were waited for; matrix products, arithmetic and copies ran while one was open for 21% of the time, Pallas kernels for 5%

profile of v5, /device:TPU:6, one launch (start us, length us, event | category | flops | bytes accessed | tf_op | source)
XLA Modules:
  0.0 192.3 jit_solution(4800961303648613665)
XLA Ops:
  3.2 2.4 %collective-permute-start.1 = (bf16[4,2,2048]{2,1,0:T(2,128)(2,1)S(1)}, bf16[4,2,2048]{2,1,0:T(2,128)(2,1)S(1)}, u32[]{:S(2)}, u32[]{:S(2)}) collective-permute-start(bf16[4,2,2048]{2,1,0:T(2,128)(2,1)S(1)} %pad_maximum_fusion.4), channel_id=1, source_target_pairs={{1,0},{2,1},{3,2},{4,3},{5,4},{6,5},{7,6},{9,8},{10,9},{11,10},{12... | collective-permute-start | bytes 98312 | tf_op jit(solution)/shard_map/ppermute | solution.py:16
  5.7 4.3 %collective-permute-start = (bf16[3,2,2048]{2,1,0:T(2,128)(2,1)S(1)}, bf16[3,2,2048]{2,1,0:T(2,128)(2,1)S(1)}, u32[]{:S(2)}, u32[]{:S(2)}) collective-permute-start(bf16[3,2,2048]{2,1,0:T(2,128)(2,1)S(1)} %pad_maximum_fusion.5), channel_id=1, source_target_pairs={{0,1},{1,2},{2,3},{3,4},{4,5},{5,6},{6,7},{8,9},{9,10},{10,11},{11... | collective-permute-start | bytes 73736 | tf_op jit(solution)/shard_map/ppermute | solution.py:16
  20.5 5.3 %all-to-all-start = ((bf16[3,8,128,128]{3,2,0,1:T(8,128)(2,1)}), bf16[3,8,128,128]{3,2,0,1:T(8,128)(2,1)S(1)}, u32[]{:S(2)}, u32[]{:S(2)}) async-start(bf16[3,8,128,128]{3,2,0,1:T(8,128)(2,1)} %copy.189), calls=%async_computation | async-start | bytes 1572864 | tf_op jit(solution)/shard_map/all_to_all | solution.py:318
  27.0 17.8 %all-to-all-done = bf16[3,8,128,128]{3,2,0,1:T(8,128)(2,1)S(1)} async-done(((bf16[3,8,128,128]{3,2,0,1:T(8,128)(2,1)}), bf16[3,8,128,128]{3,2,0,1:T(8,128)(2,1)S(1)}, u32[]{:S(2)}, u32[]{:S(2)}) %all-to-all-start) | async-done | bytes 786464 | tf_op jit(solution)/shard_map/all_to_all | solution.py:318
  44.8 4.2 %all-to-all-start.1 = ((bf16[3,8,128,128]{3,2,0,1:T(8,128)(2,1)}), bf16[3,8,128,128]{3,2,0,1:T(8,128)(2,1)S(1)}, u32[]{:S(2)}, u32[]{:S(2)}) async-start(bf16[3,8,128,128]{3,2,0,1:T(8,128)(2,1)} %copy.198), calls=%async_computation.1 | async-start | bytes 1572864 | tf_op jit(solution)/shard_map/all_to_all | solution.py:318
  53.6 2.5 %fusion.18 = f32[64,3,64,128]{3,0,2,1:T(8,128)S(1)} fusion(bf16[64,64,1,1]{1,0,3,2:T(8,128)(2,1)S(1)} %copy-done.12, bf16[64,3,64,128]{3,2,1,0:T(8,128)(2,1)S(1)} %bitcast.253), kind=kOutput, calls=%fused_computation.24 | convolution fusion | flops 201326592 | bytes 9445376 | tf_op jit(solution)/shard_map/ab,bskc->askc/dot_general | solution.py:29
  73.2 2.5 %fusion.14 = f32[64,3,64,128]{3,0,2,1:T(8,128)S(1)} fusion(bf16[64,64,1,1]{1,0,3,2:T(8,128)(2,1)S(1)} %copy-done.12, bf16[64,3,64,128]{3,2,1,0:T(8,128)(2,1)S(1)} %bitcast.252), kind=kOutput, calls=%fused_computation.20 | convolution fusion | flops 201326592 | bytes 9445376 | tf_op jit(solution)/shard_map/ab,bskc->askc/dot_general | solution.py:29
  78.6 1.4 fusion.26
  87.6 5.7 %all-to-all-start.3 = ((bf16[2,8,136,128]{3,2,0,1:T(8,128)(2,1)}), bf16[2,8,136,128]{3,2,0,1:T(8,128)(2,1)}, u32[]{:S(2)}, u32[]{:S(2)}) async-start(bf16[2,8,136,128]{3,2,0,1:T(8,128)(2,1)} %fusion.70), calls=%async_computation.3 | async-start | bytes 1114112 | tf_op jit(solution)/shard_map/all_to_all | solution.py:339
  93.3 14.4 %all-to-all-done.3 = bf16[2,8,136,128]{3,2,0,1:T(8,128)(2,1)} async-done(((bf16[2,8,136,128]{3,2,0,1:T(8,128)(2,1)}), bf16[2,8,136,128]{3,2,0,1:T(8,128)(2,1)}, u32[]{:S(2)}, u32[]{:S(2)}) %all-to-all-start.3) | async-done | bytes 557088 | tf_op jit(solution)/shard_map/all_to_all | solution.py:339
  107.6 4.7 %all-to-all-start.2 = ((bf16[2,8,136,128]{3,2,0,1:T(8,128)(2,1)}), bf16[2,8,136,128]{3,2,0,1:T(8,128)(2,1)}, u32[]{:S(2)}, u32[]{:S(2)}) async-start(bf16[2,8,136,128]{3,2,0,1:T(8,128)(2,1)} %fusion.66), calls=%async_computation.2 | async-start | bytes 1114112 | tf_op jit(solution)/shard_map/all_to_all | solution.py:329
  115.6 11.0 %all-to-all-done.2 = bf16[2,8,136,128]{3,2,0,1:T(8,128)(2,1)} async-done(((bf16[2,8,136,128]{3,2,0,1:T(8,128)(2,1)}), bf16[2,8,136,128]{3,2,0,1:T(8,128)(2,1)}, u32[]{:S(2)}, u32[]{:S(2)}) %all-to-all-start.2) | async-done | bytes 557088 | tf_op jit(solution)/shard_map/all_to_all | solution.py:329
  129.0 1.7 reshape.213.conv_ref.back_ref
  132.1 1.6 maximum_maximum_fusion
  133.7 1.4 pad_maximum_fusion.src_ref
  135.1 9.7 %shard_map.297 = (bf16[4,128,2048]{2,1,0:T(8,128)(2,1)}, f32[16,2048]{1,0:T(8,128)}) custom-call(bf16[2,136,2048]{2,1,0:T(8,128)(2,1)} %reshape.213.conv_ref.back_ref, bf16[2,136,2048]{2,1,0:T(8,128)(2,1)} %reshape.213.conv_ref.back_ref, bf16[3,136,2048]{2,1,0:T(8,128)(2,1)} %pad_maximum_fusion.src_ref, bf16[136,2048]{1,0:T(8,128)(2,1)} %get-tuple-element.84.up_ref, ...), custom_call_target="tpu_custom_call" | custom-call | tf_op jit(solution)/shard_map/pallas_call | solution.py:244
  146.7 4.0 %all-to-all-start.4 = ((f32[32,1,640]{2,1,0:T(1,128)}), f32[32,1,640]{2,1,0:T(1,128)S(1)}, u32[]{:S(2)}, u32[]{:S(2)}) async-start(f32[32,1,640]{2,1,0:T(1,128)} %reshape.223), calls=%async_computation.4 | async-start | bytes 163840 | tf_op jit(solution)/shard_map/all_to_all | solution.py:130
  150.7 5.7 %all-to-all-done.4 = f32[32,1,640]{2,1,0:T(1,128)S(1)} async-done(((f32[32,1,640]{2,1,0:T(1,128)}), f32[32,1,640]{2,1,0:T(1,128)S(1)}, u32[]{:S(2)}, u32[]{:S(2)}) %all-to-all-start.4) | async-done | bytes 81952 | tf_op jit(solution)/shard_map/all_to_all | solution.py:130
  158.7 4.2 %all-to-all-start.5 = ((f32[32,1,640]{2,1,0:T(1,128)}), f32[32,1,640]{2,1,0:T(1,128)S(1)}, u32[]{:S(2)}, u32[]{:S(2)}) async-start(f32[32,1,640]{2,1,0:T(1,128)} %reshape.225), calls=%async_computation.5 | async-start | bytes 163840 | tf_op jit(solution)/shard_map/all_to_all | solution.py:132
  166.3 2.5 %all-to-all-done.5 = f32[32,1,640]{2,1,0:T(1,128)S(1)} async-done(((f32[32,1,640]{2,1,0:T(1,128)}), f32[32,1,640]{2,1,0:T(1,128)S(1)}, u32[]{:S(2)}, u32[]{:S(2)}) %all-to-all-start.5) | async-done | bytes 81952 | tf_op jit(solution)/shard_map/all_to_all | solution.py:132
  171.3 7.7 %collective-permute-start.6 = (f32[128,256]{1,0:T(8,128)S(1)}, f32[128,256]{1,0:T(8,128)S(1)}, u32[]{:S(2)}, u32[]{:S(2)}) collective-permute-start(f32[128,256]{1,0:T(8,128)S(1)} %get-tuple-element.67), channel_id=1, source_target_pairs={{1,0},{3,8},{5,16},{7,24},{9,2},{11,10},{13,18},{15,26},{17,4},{19... | collective-permute-start | bytes 393224 | tf_op jit(solution)/shard_map/ppermute | solution.py:165
  180.2 3.6 %collective-permute-start.7 = (f32[128,256]{1,0:T(8,128)S(1)}, f32[128,256]{1,0:T(8,128)S(1)}, u32[]{:S(2)}, u32[]{:S(2)}) collective-permute-start(f32[128,256]{1,0:T(8,128)S(1)} %get-tuple-element.66), channel_id=1, source_target_pairs={{1,1},{3,9},{5,17},{7,25},{9,3},{11,11},{13,19},{15,27},{17,5},{19... | collective-permute-start | bytes 393224 | tf_op jit(solution)/shard_map/ppermute | solution.py:165
  184.5 5.4 %collective-permute-done.5 = f32[128,256]{1,0:T(8,128)S(1)} collective-permute-done((f32[128,256]{1,0:T(8,128)S(1)}, f32[128,256]{1,0:T(8,128)S(1)}, u32[]{:S(2)}, u32[]{:S(2)}) %collective-permute-start.5) | collective-permute-done | bytes 131104 | tf_op jit(solution)/shard_map/ppermute | solution.py:165
  189.9 1.7 collective-permute-done.7
  (172 shorter events, 65.5 us)
Async XLA Ops:
  0.6 13.5 %copy-start = (bf16[1,128,2048]{2,1,0:T(8,128)(2,1)S(1)}, bf16[1,128,2048]{2,1,0:T(8,128)(2,1)}, u32[]{:S(2)}) copy-start(bf16[1,128,2048]{2,1,0:T(8,128)(2,1)} %param.28) | copy-start | bytes 1572868
  0.6 13.6 %copy-start.2 = (bf16[1,128,2048]{2,1,0:T(8,128)(2,1)S(1)}, bf16[1,128,2048]{2,1,0:T(8,128)(2,1)}, u32[]{:S(2)}) copy-start(bf16[1,128,2048]{2,1,0:T(8,128)(2,1)} %param.26) | copy-start | bytes 1572868
  3.2 10.9 %collective-permute-start.1 = (bf16[4,2,2048]{2,1,0:T(2,128)(2,1)S(1)}, bf16[4,2,2048]{2,1,0:T(2,128)(2,1)S(1)}, u32[]{:S(2)}, u32[]{:S(2)}) collective-permute-start(bf16[4,2,2048]{2,1,0:T(2,128)(2,1)S(1)} %pad_maximum_fusion.4), channel_id=1, source_target_pairs={{1,0},{2,1},{3,2},{4,3},{5,4},{6,5},{7,6},{9,8},{10,9},{11,10},{12... | collective-permute-start | bytes 98312 | tf_op jit(solution)/shard_map/ppermute | solution.py:16
  5.7 8.3 %collective-permute-start = (bf16[3,2,2048]{2,1,0:T(2,128)(2,1)S(1)}, bf16[3,2,2048]{2,1,0:T(2,128)(2,1)S(1)}, u32[]{:S(2)}, u32[]{:S(2)}) collective-permute-start(bf16[3,2,2048]{2,1,0:T(2,128)(2,1)S(1)} %pad_maximum_fusion.5), channel_id=1, source_target_pairs={{0,1},{1,2},{2,3},{3,4},{4,5},{5,6},{6,7},{8,9},{9,10},{10,11},{11... | collective-permute-start | bytes 73736 | tf_op jit(solution)/shard_map/ppermute | solution.py:16
  20.5 24.3 %all-to-all-start = ((bf16[3,8,128,128]{3,2,0,1:T(8,128)(2,1)}), bf16[3,8,128,128]{3,2,0,1:T(8,128)(2,1)S(1)}, u32[]{:S(2)}, u32[]{:S(2)}) async-start(bf16[3,8,128,128]{3,2,0,1:T(8,128)(2,1)} %copy.189), calls=%async_computation | async-start | bytes 1572864 | tf_op jit(solution)/shard_map/all_to_all | solution.py:318
  27.0 22.1 %copy-start.17 = (bf16[128,32,1,1]{0,1,3,2:T(8,128)(2,1)S(1)}, bf16[128,32,1,1]{0,1,3,2:T(8,128)(2,1)}, u32[]{:S(2)}) copy-start(bf16[128,32,1,1]{0,1,3,2:T(8,128)(2,1)} %constant.116) | copy-start | bytes 24580
  44.8 23.9 %all-to-all-start.1 = ((bf16[3,8,128,128]{3,2,0,1:T(8,128)(2,1)}), bf16[3,8,128,128]{3,2,0,1:T(8,128)(2,1)S(1)}, u32[]{:S(2)}, u32[]{:S(2)}) async-start(bf16[3,8,128,128]{3,2,0,1:T(8,128)(2,1)} %copy.198), calls=%async_computation.1 | async-start | bytes 1572864 | tf_op jit(solution)/shard_map/all_to_all | solution.py:318
  58.3 1.1 copy-start.9
  58.3 1.1 copy-start.10
  87.6 20.1 %all-to-all-start.3 = ((bf16[2,8,136,128]{3,2,0,1:T(8,128)(2,1)}), bf16[2,8,136,128]{3,2,0,1:T(8,128)(2,1)}, u32[]{:S(2)}, u32[]{:S(2)}) async-start(bf16[2,8,136,128]{3,2,0,1:T(8,128)(2,1)} %fusion.70), calls=%async_computation.3 | async-start | bytes 1114112 | tf_op jit(solution)/shard_map/all_to_all | solution.py:339
  107.6 19.0 %all-to-all-start.2 = ((bf16[2,8,136,128]{3,2,0,1:T(8,128)(2,1)}), bf16[2,8,136,128]{3,2,0,1:T(8,128)(2,1)}, u32[]{:S(2)}, u32[]{:S(2)}) async-start(bf16[2,8,136,128]{3,2,0,1:T(8,128)(2,1)} %fusion.66), calls=%async_computation.2 | async-start | bytes 1114112 | tf_op jit(solution)/shard_map/all_to_all | solution.py:329
  129.0 3.1 %copy-start.1 = (bf16[1,128,2048]{2,1,0:T(8,128)(2,1)S(1)}, bf16[1,128,2048]{2,1,0:T(8,128)(2,1)}, u32[]{:S(2)}) copy-start(bf16[1,128,2048]{2,1,0:T(8,128)(2,1)} %param.28) | copy-start | bytes 1572868
  129.0 3.1 %copy-start.3 = (bf16[1,128,2048]{2,1,0:T(8,128)(2,1)S(1)}, bf16[1,128,2048]{2,1,0:T(8,128)(2,1)}, u32[]{:S(2)}) copy-start(bf16[1,128,2048]{2,1,0:T(8,128)(2,1)} %param.26) | copy-start | bytes 1572868
  130.7 1.4 copy-start.5
  130.7 1.4 copy-start.7
  131.5 31.4 %collective-permute-start.2 = (f32[2,256,256]{2,1,0:T(8,128)}, f32[2,256,256]{2,1,0:T(8,128)}, u32[]{:S(2)}, u32[]{:S(2)}) collective-permute-start(f32[2,256,256]{2,1,0:T(8,128)} %bitcast.118), channel_id=1, source_target_pairs={{0,16},{8,24},{16,0},{24,8},{1,17},{9,25},{17,1},{25,9},{2,18},{10... | collective-permute-start | bytes 1572872 | tf_op jit(solution)/shard_map/ppermute | solution.py:146
  146.7 9.7 %all-to-all-start.4 = ((f32[32,1,640]{2,1,0:T(1,128)}), f32[32,1,640]{2,1,0:T(1,128)S(1)}, u32[]{:S(2)}, u32[]{:S(2)}) async-start(f32[32,1,640]{2,1,0:T(1,128)} %reshape.223), calls=%async_computation.4 | async-start | bytes 163840 | tf_op jit(solution)/shard_map/all_to_all | solution.py:130
  157.8 7.1 %copy-start.8 = (bf16[4,128,2048]{2,1,0:T(8,128)(2,1)S(1)}, bf16[4,128,2048]{2,1,0:T(8,128)(2,1)}, u32[]{:S(2)}) copy-start(bf16[4,128,2048]{2,1,0:T(8,128)(2,1)} %get-tuple-element.16) | copy-start | bytes 6291460
  158.7 10.0 %all-to-all-start.5 = ((f32[32,1,640]{2,1,0:T(1,128)}), f32[32,1,640]{2,1,0:T(1,128)S(1)}, u32[]{:S(2)}, u32[]{:S(2)}) async-start(f32[32,1,640]{2,1,0:T(1,128)} %reshape.225), calls=%async_computation.5 | async-start | bytes 163840 | tf_op jit(solution)/shard_map/all_to_all | solution.py:132
  164.8 5.7 %collective-permute-start.3 = (f32[1,256,256]{2,1,0:T(8,128)}, f32[1,256,256]{2,1,0:T(8,128)S(1)}, u32[]{:S(2)}, u32[]{:S(2)}) collective-permute-start(f32[1,256,256]{2,1,0:T(8,128)} %slice_select_fusion.5), channel_id=1, source_target_pairs={{0,8},{8,0},{16,24},{24,16},{1,9},{9,1},{17,25},{25,17},{2,10},{10... | collective-permute-start | bytes 786440 | tf_op jit(solution)/shard_map/ppermute | solution.py:146
  170.6 13.9 %collective-permute-start.4 = (f32[128,256]{1,0:T(8,128)S(1)}, f32[128,256]{1,0:T(8,128)S(1)}, u32[]{:S(2)}, u32[]{:S(2)}) collective-permute-start(f32[128,256]{1,0:T(8,128)S(1)} %get-tuple-element.67), channel_id=1, source_target_pairs={{0,0},{2,8},{4,16},{6,24},{8,2},{10,10},{12,18},{14,26},{16,4},{18... | collective-permute-start | bytes 393224 | tf_op jit(solution)/shard_map/ppermute | solution.py:165
  171.3 18.6 %collective-permute-start.6 = (f32[128,256]{1,0:T(8,128)S(1)}, f32[128,256]{1,0:T(8,128)S(1)}, u32[]{:S(2)}, u32[]{:S(2)}) collective-permute-start(f32[128,256]{1,0:T(8,128)S(1)} %get-tuple-element.67), channel_id=1, source_target_pairs={{1,0},{3,8},{5,16},{7,24},{9,2},{11,10},{13,18},{15,26},{17,4},{19... | collective-permute-start | bytes 393224 | tf_op jit(solution)/shard_map/ppermute | solution.py:165
  178.9 11.0 %collective-permute-start.5 = (f32[128,256]{1,0:T(8,128)S(1)}, f32[128,256]{1,0:T(8,128)S(1)}, u32[]{:S(2)}, u32[]{:S(2)}) collective-permute-start(f32[128,256]{1,0:T(8,128)S(1)} %get-tuple-element.66), channel_id=1, source_target_pairs={{0,1},{2,9},{4,17},{6,25},{8,3},{10,11},{12,19},{14,27},{16,5},{18... | collective-permute-start | bytes 393224 | tf_op jit(solution)/shard_map/ppermute | solution.py:165
  180.2 11.3 %collective-permute-start.7 = (f32[128,256]{1,0:T(8,128)S(1)}, f32[128,256]{1,0:T(8,128)S(1)}, u32[]{:S(2)}, u32[]{:S(2)}) collective-permute-start(f32[128,256]{1,0:T(8,128)S(1)} %get-tuple-element.66), channel_id=1, source_target_pairs={{1,1},{3,9},{5,17},{7,25},{9,3},{11,11},{13,19},{15,27},{17,5},{19... | collective-permute-start | bytes 393224 | tf_op jit(solution)/shard_map/ppermute | solution.py:165
  (8 other events, 7.4 us)

commit v6 on v3

--- a/solution.py
+++ b/solution.py
@@ -73,7 +73,7 @@
     phase = 2.0 * np.pi * np.outer(np.arange(outer), np.arange(half)) / outer
     first = np.concatenate([np.cos(phase), -np.sin(phase)], 0)
     blocks = signal.reshape(count, half, inner, lanes).transpose(1, 0, 2, 3)
-    stage = split_product("kn,nsqb->ksqb", first, blocks)
+    stage = split_product("kn,nsqb->ksqb", first, blocks, exact=False)
     real_part, imag_part = stage[:outer], stage[outer:]
     cosine, sine = twiddles(outer, inner, size)
     cosine, sine = cosine.transpose(1, 0, 2, 3), sine.transpose(1, 0, 2, 3)

time: 178 us -> 176 us (0.989)
  matrix products: 13.8 us -> 11.7 us
    dot_general x4 -> x0, matrix products: 4.12 us -> none  [the longest x2 2.08 us: split_product(): return total + jnp.einsum(form, lower, data, preferred_element_type=wide)]
    dot_general x6 -> x8, matrix products: 9.67 us -> 11.7 us  [split_product(): jnp.einsum(form, upper, data.astype(jnp.bfloat16), preferred_element_type...]
    unnamed x55 -> x53, local copies, waits for them, and re-layouts: 14 us -> 14 us
  transfers between devices with their start and end apart: 14 -> 14, of which waited for: 7 -> 7; matrix products, arithmetic and copies ran while one was open for 23% -> 22% of each run, Pallas kernels for 5% -> 6%
where the time goes in v6:
time: 176 us; the launch traced here: 175 us
  waiting for transfers between devices  52.1 us (30%)
  starting transfers between devices  40.8 us (23%)
  local copies, waits for them, and re-layouts  35.4 us (20%)
  other arithmetic  23.5 us (13%)
  matrix products  11.7 us (7%)
  Pallas kernels  9.71 us (6%)
    all_to_all x2, waiting for transfers between devices, to_columns(): moved = lax.all_to_all(split.transpose(0, 2, 1, 3), 'ctx', 1, 1, tiled=True)  20.4 us
    unnamed x53, local copies, waits for them, and re-layouts  14 us
    dot_general x8, matrix products, split_product(): jnp.einsum(form, upper, data.astype(jnp.bfloat16), preferred_element_type...  11.7 us
    all_to_all x2, waiting for transfers between devices, local(): returned.append(lax.all_to_all(previous, 'ctx', 1, 1, tiled=True))  10.9 us
    all_to_all x2, starting transfers between devices, to_columns(): moved = lax.all_to_all(split.transpose(0, 2, 1, 3), 'ctx', 1, 1, tiled=True)  9.94 us
    all_to_all x2, starting transfers between devices, local(): returned.append(lax.all_to_all(previous, 'ctx', 1, 1, tiled=True))  9.91 us
    pallas_call x1, Pallas kernels, epilogue(): pl.pallas_call(epilogue_kernel, grid=grid, in_specs=[pl.BlockSpec((None,...  9.71 us
    ppermute x2, waiting for transfers between devices, halving_rows(): lax.ppermute(give, axis, [(i, i ^ step) for i in range(size)])  8.08 us
  transfers between devices with their start and end apart: 14, of which 7 were waited for; matrix products, arithmetic and copies ran while one was open for 22% of the time, Pallas kernels for 6%

profile of v6, /device:TPU:0, one launch (start us, length us, event | category | flops | bytes accessed | tf_op | source)
XLA Modules:
  0.0 174.8 jit_solution(15184573470900566079)
XLA Ops:
  4.6 5.5 %collective-permute-start = (bf16[3,2,2048]{2,1,0:T(2,128)(2,1)S(1)}, bf16[3,2,2048]{2,1,0:T(2,128)(2,1)S(1)}, u32[]{:S(2)}, u32[]{:S(2)}) collective-permute-start(bf16[3,2,2048]{2,1,0:T(2,128)(2,1)S(1)} %pad_maximum_fusion.5), channel_id=1, source_target_pairs={{0,1},{1,2},{2,3},{3,4},{4,5},{5,6},{6,7},{8,9},{9,10},{10,11},{11... | collective-permute-start | bytes 73736 | tf_op jit(solution)/shard_map/ppermute | solution.py:16
  12.7 1.3 copy.178
  20.5 6.2 %all-to-all-start.1 = ((bf16[3,8,128,128]{3,2,0,1:T(8,128)(2,1)}), bf16[3,8,128,128]{3,2,0,1:T(8,128)(2,1)S(1)}, u32[]{:S(2)}, u32[]{:S(2)}) async-start(bf16[3,8,128,128]{3,2,0,1:T(8,128)(2,1)} %copy.185), calls=%async_computation.1 | async-start | bytes 1572864 | tf_op jit(solution)/shard_map/all_to_all | solution.py:318
  28.0 18.4 %all-to-all-done.1 = bf16[3,8,128,128]{3,2,0,1:T(8,128)(2,1)S(1)} async-done(((bf16[3,8,128,128]{3,2,0,1:T(8,128)(2,1)}), bf16[3,8,128,128]{3,2,0,1:T(8,128)(2,1)S(1)}, u32[]{:S(2)}, u32[]{:S(2)}) %all-to-all-start.1) | async-done | bytes 786464 | tf_op jit(solution)/shard_map/all_to_all | solution.py:318
  46.4 3.7 %all-to-all-start = ((bf16[3,8,128,128]{3,2,0,1:T(8,128)(2,1)}), bf16[3,8,128,128]{3,2,0,1:T(8,128)(2,1)S(1)}, u32[]{:S(2)}, u32[]{:S(2)}) async-start(bf16[3,8,128,128]{3,2,0,1:T(8,128)(2,1)} %copy.182), calls=%async_computation | async-start | bytes 1572864 | tf_op jit(solution)/shard_map/all_to_all | solution.py:318
  53.6 2.5 %fusion.18 = f32[64,3,64,128]{3,0,2,1:T(8,128)S(1)} fusion(bf16[64,64,1,1]{1,0,3,2:T(8,128)(2,1)S(1)} %copy-done.12, bf16[64,3,64,128]{3,2,1,0:T(8,128)(2,1)S(1)} %bitcast.238), kind=kOutput, calls=%fused_computation.22 | convolution fusion | flops 201326592 | bytes 9445376 | tf_op jit(solution)/shard_map/ab,bskc->askc/dot_general | solution.py:29
  68.2 2.0 %all-to-all-done = bf16[3,8,128,128]{3,2,0,1:T(8,128)(2,1)S(1)} async-done(((bf16[3,8,128,128]{3,2,0,1:T(8,128)(2,1)}), bf16[3,8,128,128]{3,2,0,1:T(8,128)(2,1)S(1)}, u32[]{:S(2)}, u32[]{:S(2)}) %all-to-all-start) | async-done | bytes 786464 | tf_op jit(solution)/shard_map/all_to_all | solution.py:318
  71.4 1.5 fusion.24
  73.9 2.5 %fusion.14 = f32[64,3,64,128]{3,0,2,1:T(8,128)S(1)} fusion(bf16[64,64,1,1]{1,0,3,2:T(8,128)(2,1)S(1)} %copy-done.12, bf16[64,3,64,128]{3,2,1,0:T(8,128)(2,1)S(1)} %bitcast.237), kind=kOutput, calls=%fused_computation.18 | convolution fusion | flops 201326592 | bytes 9445376 | tf_op jit(solution)/shard_map/ab,bskc->askc/dot_general | solution.py:29
  87.9 4.2 %all-to-all-start.3 = ((bf16[2,8,136,128]{3,2,0,1:T(8,128)(2,1)}), bf16[2,8,136,128]{3,2,0,1:T(8,128)(2,1)}, u32[]{:S(2)}, u32[]{:S(2)}) async-start(bf16[2,8,136,128]{3,2,0,1:T(8,128)(2,1)} %fusion.68), calls=%async_computation.3 | async-start | bytes 1114112 | tf_op jit(solution)/shard_map/all_to_all | solution.py:339
  94.1 1.5 collective-permute-start.2
  96.7 2.8 %maximum_maximum_fusion = (bf16[136,2048]{1,0:T(8,128)(2,1)}, bf16[1,136,2048]{2,1,0:T(8,128)(2,1)S(1)}, bf16[1,136,2048]{2,1,0:T(8,128)(2,1)S(1)}, bf16[1,136,2048]{2,1,0:T(8,128)(2,1)S(1)}) fusion(bf16[2,2048]{1,0:T(2,128)(2,1)S(1)} %get-tuple-element.75, bf16[128,2048]{1,0:T(8,128)(2,1)} %bitcast.265, bf16[136]{0:T(256)(128)(2,1)S(1)} %pad.13.clone, ...), kind=kLoop, calls=%fused_computation.106 | loop fusion | flops 8077312 | bytes 4383264 | tf_op jit(solution)/shard_map/concatenate | solution.py:356
  99.4 7.9 %collective-permute-done.2 = f32[2,256,256]{2,1,0:T(8,128)} collective-permute-done((f32[2,256,256]{2,1,0:T(8,128)}, f32[2,256,256]{2,1,0:T(8,128)}, u32[]{:S(2)}, u32[]{:S(2)}) %collective-permute-start.2) | collective-permute-done | bytes 524320 | tf_op jit(solution)/shard_map/ppermute | solution.py:146
  108.5 5.7 %all-to-all-start.2 = ((bf16[2,8,136,128]{3,2,0,1:T(8,128)(2,1)}), bf16[2,8,136,128]{3,2,0,1:T(8,128)(2,1)S(1)}, u32[]{:S(2)}, u32[]{:S(2)}) async-start(bf16[2,8,136,128]{3,2,0,1:T(8,128)(2,1)} %fusion.64), calls=%async_computation.2 | async-start | bytes 1114112 | tf_op jit(solution)/shard_map/all_to_all | solution.py:329
  114.3 1.4 pad_maximum_fusion.src_ref
  117.9 4.6 %collective-permute-start.5 = (f32[128,256]{1,0:T(8,128)S(1)}, f32[128,256]{1,0:T(8,128)S(1)}, u32[]{:S(2)}, u32[]{:S(2)}) collective-permute-start(f32[128,256]{1,0:T(8,128)S(1)} %get-tuple-element.62), channel_id=1, source_target_pairs={{0,1},{2,9},{4,17},{6,25},{8,3},{10,11},{12,19},{14,27},{16,5},{18... | collective-permute-start | bytes 393224 | tf_op jit(solution)/shard_map/ppermute | solution.py:165
  124.5 10.9 %all-to-all-done.2 = bf16[2,8,136,128]{3,2,0,1:T(8,128)(2,1)S(1)} async-done(((bf16[2,8,136,128]{3,2,0,1:T(8,128)(2,1)}), bf16[2,8,136,128]{3,2,0,1:T(8,128)(2,1)S(1)}, u32[]{:S(2)}, u32[]{:S(2)}) %all-to-all-start.2) | async-done | bytes 557088 | tf_op jit(solution)/shard_map/all_to_all | solution.py:329
  136.7 1.7 reshape.213.conv_ref.back_ref
  138.4 9.7 %shard_map.279 = (bf16[4,128,2048]{2,1,0:T(8,128)(2,1)}, f32[16,2048]{1,0:T(8,128)}) custom-call(bf16[2,136,2048]{2,1,0:T(8,128)(2,1)} %reshape.213.conv_ref.back_ref, bf16[2,136,2048]{2,1,0:T(8,128)(2,1)} %reshape.213.conv_ref.back_ref, bf16[3,136,2048]{2,1,0:T(8,128)(2,1)} %pad_maximum_fusion.src_ref, bf16[136,2048]{1,0:T(8,128)(2,1)} %get-tuple-element.80.up_ref, ...), custom_call_target="tpu_custom_call" | custom-call | tf_op jit(solution)/shard_map/pallas_call | solution.py:244
  150.0 2.6 %all-to-all-start.4 = ((f32[32,1,640]{2,1,0:T(1,128)}), f32[32,1,640]{2,1,0:T(1,128)S(1)}, u32[]{:S(2)}, u32[]{:S(2)}) async-start(f32[32,1,640]{2,1,0:T(1,128)} %reshape.222), calls=%async_computation.4 | async-start | bytes 163840 | tf_op jit(solution)/shard_map/all_to_all | solution.py:130
  153.4 6.6 %all-to-all-done.4 = f32[32,1,640]{2,1,0:T(1,128)S(1)} async-done(((f32[32,1,640]{2,1,0:T(1,128)}), f32[32,1,640]{2,1,0:T(1,128)S(1)}, u32[]{:S(2)}, u32[]{:S(2)}) %all-to-all-start.4) | async-done | bytes 81952 | tf_op jit(solution)/shard_map/all_to_all | solution.py:130
  162.3 2.6 %all-to-all-start.5 = ((f32[32,1,640]{2,1,0:T(1,128)}), f32[32,1,640]{2,1,0:T(1,128)S(1)}, u32[]{:S(2)}, u32[]{:S(2)}) async-start(f32[32,1,640]{2,1,0:T(1,128)} %reshape.224), calls=%async_computation.5 | async-start | bytes 163840 | tf_op jit(solution)/shard_map/all_to_all | solution.py:132
  164.9 1.3 fusion.83
  166.2 6.1 %all-to-all-done.5 = f32[32,1,640]{2,1,0:T(1,128)S(1)} async-done(((f32[32,1,640]{2,1,0:T(1,128)}), f32[32,1,640]{2,1,0:T(1,128)S(1)}, u32[]{:S(2)}, u32[]{:S(2)}) %all-to-all-start.5) | async-done | bytes 81952 | tf_op jit(solution)/shard_map/all_to_all | solution.py:132
  (167 shorter events, 60.0 us)
Async XLA Ops:
  0.6 13.5 %copy-start = (bf16[1,128,2048]{2,1,0:T(8,128)(2,1)S(1)}, bf16[1,128,2048]{2,1,0:T(8,128)(2,1)}, u32[]{:S(2)}) copy-start(bf16[1,128,2048]{2,1,0:T(8,128)(2,1)} %param.26) | copy-start | bytes 1572868
  0.6 13.6 %copy-start.2 = (bf16[1,128,2048]{2,1,0:T(8,128)(2,1)S(1)}, bf16[1,128,2048]{2,1,0:T(8,128)(2,1)}, u32[]{:S(2)}) copy-start(bf16[1,128,2048]{2,1,0:T(8,128)(2,1)} %param.24) | copy-start | bytes 1572868
  3.2 10.9 %collective-permute-start.1 = (bf16[4,2,2048]{2,1,0:T(2,128)(2,1)S(1)}, bf16[4,2,2048]{2,1,0:T(2,128)(2,1)S(1)}, u32[]{:S(2)}, u32[]{:S(2)}) collective-permute-start(bf16[4,2,2048]{2,1,0:T(2,128)(2,1)S(1)} %pad_maximum_fusion.4), channel_id=1, source_target_pairs={{1,0},{2,1},{3,2},{4,3},{5,4},{6,5},{7,6},{9,8},{10,9},{11,10},{12... | collective-permute-start | bytes 98312 | tf_op jit(solution)/shard_map/ppermute | solution.py:16
  4.6 9.5 %collective-permute-start = (bf16[3,2,2048]{2,1,0:T(2,128)(2,1)S(1)}, bf16[3,2,2048]{2,1,0:T(2,128)(2,1)S(1)}, u32[]{:S(2)}, u32[]{:S(2)}) collective-permute-start(bf16[3,2,2048]{2,1,0:T(2,128)(2,1)S(1)} %pad_maximum_fusion.5), channel_id=1, source_target_pairs={{0,1},{1,2},{2,3},{3,4},{4,5},{5,6},{6,7},{8,9},{9,10},{10,11},{11... | collective-permute-start | bytes 73736 | tf_op jit(solution)/shard_map/ppermute | solution.py:16
  20.5 25.9 %all-to-all-start.1 = ((bf16[3,8,128,128]{3,2,0,1:T(8,128)(2,1)}), bf16[3,8,128,128]{3,2,0,1:T(8,128)(2,1)S(1)}, u32[]{:S(2)}, u32[]{:S(2)}) async-start(bf16[3,8,128,128]{3,2,0,1:T(8,128)(2,1)} %copy.185), calls=%async_computation.1 | async-start | bytes 1572864 | tf_op jit(solution)/shard_map/all_to_all | solution.py:318
  28.0 22.2 %copy-start.16 = (bf16[128,32,1,1]{0,1,3,2:T(8,128)(2,1)S(1)}, bf16[128,32,1,1]{0,1,3,2:T(8,128)(2,1)}, u32[]{:S(2)}) copy-start(bf16[128,32,1,1]{0,1,3,2:T(8,128)(2,1)} %constant.113) | copy-start | bytes 24580
  46.4 23.9 %all-to-all-start = ((bf16[3,8,128,128]{3,2,0,1:T(8,128)(2,1)}), bf16[3,8,128,128]{3,2,0,1:T(8,128)(2,1)S(1)}, u32[]{:S(2)}, u32[]{:S(2)}) async-start(bf16[3,8,128,128]{3,2,0,1:T(8,128)(2,1)} %copy.182), calls=%async_computation | async-start | bytes 1572864 | tf_op jit(solution)/shard_map/all_to_all | solution.py:318
  58.3 1.1 copy-start.9
  58.3 1.1 copy-start.10
  87.9 20.6 %all-to-all-start.3 = ((bf16[2,8,136,128]{3,2,0,1:T(8,128)(2,1)}), bf16[2,8,136,128]{3,2,0,1:T(8,128)(2,1)}, u32[]{:S(2)}, u32[]{:S(2)}) async-start(bf16[2,8,136,128]{3,2,0,1:T(8,128)(2,1)} %fusion.68), calls=%async_computation.3 | async-start | bytes 1114112 | tf_op jit(solution)/shard_map/all_to_all | solution.py:339
  92.7 4.0 %copy-start.1 = (bf16[1,128,2048]{2,1,0:T(8,128)(2,1)S(1)}, bf16[1,128,2048]{2,1,0:T(8,128)(2,1)}, u32[]{:S(2)}) copy-start(bf16[1,128,2048]{2,1,0:T(8,128)(2,1)} %param.26) | copy-start | bytes 1572868
  92.7 3.9 %copy-start.3 = (bf16[1,128,2048]{2,1,0:T(8,128)(2,1)S(1)}, bf16[1,128,2048]{2,1,0:T(8,128)(2,1)}, u32[]{:S(2)}) copy-start(bf16[1,128,2048]{2,1,0:T(8,128)(2,1)} %param.24) | copy-start | bytes 1572868
  92.7 3.9 %copy-start.5 = (bf16[1,128,2048]{2,1,0:T(8,128)(2,1)S(1)}, bf16[1,128,2048]{2,1,0:T(8,128)(2,1)}, u32[]{:S(2)}) copy-start(bf16[1,128,2048]{2,1,0:T(8,128)(2,1)} %param.25) | copy-start | bytes 1572868
  94.1 13.3 %collective-permute-start.2 = (f32[2,256,256]{2,1,0:T(8,128)}, f32[2,256,256]{2,1,0:T(8,128)}, u32[]{:S(2)}, u32[]{:S(2)}) collective-permute-start(f32[2,256,256]{2,1,0:T(8,128)} %bitcast.112), channel_id=1, source_target_pairs={{0,16},{8,24},{16,0},{24,8},{1,17},{9,25},{17,1},{25,9},{2,18},{10... | collective-permute-start | bytes 1572872 | tf_op jit(solution)/shard_map/ppermute | solution.py:146
  96.7 10.7 %copy-start.7 = (f32[512,256]{1,0:T(8,128)S(1)}, f32[512,256]{1,0:T(8,128)}, u32[]{:S(2)}) copy-start(f32[512,256]{1,0:T(8,128)} %get-tuple-element.55) | copy-start | bytes 1572868
  108.5 26.9 %all-to-all-start.2 = ((bf16[2,8,136,128]{3,2,0,1:T(8,128)(2,1)}), bf16[2,8,136,128]{3,2,0,1:T(8,128)(2,1)S(1)}, u32[]{:S(2)}, u32[]{:S(2)}) async-start(bf16[2,8,136,128]{3,2,0,1:T(8,128)(2,1)} %fusion.64), calls=%async_computation.2 | async-start | bytes 1114112 | tf_op jit(solution)/shard_map/all_to_all | solution.py:329
  114.3 1.6 collective-permute-start.3
  115.9 36.6 %collective-permute-start.4 = (f32[128,256]{1,0:T(8,128)S(1)}, f32[128,256]{1,0:T(8,128)S(1)}, u32[]{:S(2)}, u32[]{:S(2)}) collective-permute-start(f32[128,256]{1,0:T(8,128)S(1)} %get-tuple-element.63), channel_id=1, source_target_pairs={{0,0},{2,8},{4,16},{6,24},{8,2},{10,10},{12,18},{14,26},{16,4},{18... | collective-permute-start | bytes 393224 | tf_op jit(solution)/shard_map/ppermute | solution.py:165
  116.6 36.0 %collective-permute-start.6 = (f32[128,256]{1,0:T(8,128)S(1)}, f32[128,256]{1,0:T(8,128)S(1)}, u32[]{:S(2)}, u32[]{:S(2)}) collective-permute-start(f32[128,256]{1,0:T(8,128)S(1)} %get-tuple-element.63), channel_id=1, source_target_pairs={{1,0},{3,8},{5,16},{7,24},{9,2},{11,10},{13,18},{15,26},{17,4},{19... | collective-permute-start | bytes 393224 | tf_op jit(solution)/shard_map/ppermute | solution.py:165
  117.9 34.6 %collective-permute-start.5 = (f32[128,256]{1,0:T(8,128)S(1)}, f32[128,256]{1,0:T(8,128)S(1)}, u32[]{:S(2)}, u32[]{:S(2)}) collective-permute-start(f32[128,256]{1,0:T(8,128)S(1)} %get-tuple-element.62), channel_id=1, source_target_pairs={{0,1},{2,9},{4,17},{6,25},{8,3},{10,11},{12,19},{14,27},{16,5},{18... | collective-permute-start | bytes 393224 | tf_op jit(solution)/shard_map/ppermute | solution.py:165
  122.5 30.1 %collective-permute-start.7 = (f32[128,256]{1,0:T(8,128)S(1)}, f32[128,256]{1,0:T(8,128)S(1)}, u32[]{:S(2)}, u32[]{:S(2)}) collective-permute-start(f32[128,256]{1,0:T(8,128)S(1)} %get-tuple-element.62), channel_id=1, source_target_pairs={{1,1},{3,9},{5,17},{7,25},{9,3},{11,11},{13,19},{15,27},{17,5},{19... | collective-permute-start | bytes 393224 | tf_op jit(solution)/shard_map/ppermute | solution.py:165
  149.2 15.7 %copy-start.8 = (bf16[4,128,2048]{2,1,0:T(8,128)(2,1)S(1)}, bf16[4,128,2048]{2,1,0:T(8,128)(2,1)}, u32[]{:S(2)}) copy-start(bf16[4,128,2048]{2,1,0:T(8,128)(2,1)} %get-tuple-element.13) | copy-start | bytes 6291460
  150.0 10.0 %all-to-all-start.4 = ((f32[32,1,640]{2,1,0:T(1,128)}), f32[32,1,640]{2,1,0:T(1,128)S(1)}, u32[]{:S(2)}, u32[]{:S(2)}) async-start(f32[32,1,640]{2,1,0:T(1,128)} %reshape.222), calls=%async_computation.4 | async-start | bytes 163840 | tf_op jit(solution)/shard_map/all_to_all | solution.py:130
  162.3 10.0 %all-to-all-start.5 = ((f32[32,1,640]{2,1,0:T(1,128)}), f32[32,1,640]{2,1,0:T(1,128)S(1)}, u32[]{:S(2)}, u32[]{:S(2)}) async-start(f32[32,1,640]{2,1,0:T(1,128)} %reshape.224), calls=%async_computation.5 | async-start | bytes 163840 | tf_op jit(solution)/shard_map/all_to_all | solution.py:132
  (7 other events, 6.3 us)

commit v7 on v6

--- a/solution.py
+++ b/solution.py
@@ -238,7 +238,7 @@
 def epilogue(back, sources, upstream, masks, short_weights, skip, rows):
     _, frame, chans = back.shape
     taps = short_weights.shape[1]
-    block = 256 if chans % 256 == 0 else chans
+    block = 512 if chans % 512 == 0 else chans
     grid = (chans // block,)
     stat_rows = 16
     return pl.pallas_call(

time: 176 us -> 175 us (level)
  transfers between devices with their start and end apart: 14 -> 14, of which waited for: 7 -> 7; matrix products, arithmetic and copies ran while one was open for 22% -> 22% of each run, Pallas kernels for 6% -> 5%
where the time goes in v7:
time: 175 us; the launch traced here: 174 us
  waiting for transfers between devices  52.1 us (30%)
  starting transfers between devices  40.8 us (23%)
  local copies, waits for them, and re-layouts  35.4 us (20%)
  other arithmetic  23.5 us (13%)
  matrix products  11.7 us (7%)
  Pallas kernels  8.68 us (5%)
    all_to_all x2, waiting for transfers between devices, to_columns(): moved = lax.all_to_all(split.transpose(0, 2, 1, 3), 'ctx', 1, 1, tiled=True)  20.4 us
    unnamed x53, local copies, waits for them, and re-layouts  14 us
    dot_general x8, matrix products, split_product(): jnp.einsum(form, upper, data.astype(jnp.bfloat16), preferred_element_type...  11.7 us
    all_to_all x2, waiting for transfers between devices, local(): returned.append(lax.all_to_all(previous, 'ctx', 1, 1, tiled=True))  10.9 us
    all_to_all x2, starting transfers between devices, to_columns(): moved = lax.all_to_all(split.transpose(0, 2, 1, 3), 'ctx', 1, 1, tiled=True)  9.94 us
    all_to_all x2, starting transfers between devices, local(): returned.append(lax.all_to_all(previous, 'ctx', 1, 1, tiled=True))  9.91 us
    pallas_call x1, Pallas kernels, epilogue(): pl.pallas_call(epilogue_kernel, grid=grid, in_specs=[pl.BlockSpec((None,...  8.68 us
    ppermute x2, waiting for transfers between devices, halving_rows(): lax.ppermute(give, axis, [(i, i ^ step) for i in range(size)])  8.08 us
  transfers between devices with their start and end apart: 14, of which 7 were waited for; matrix products, arithmetic and copies ran while one was open for 22% of the time, Pallas kernels for 5%

profile of v7, /device:TPU:0, one launch (start us, length us, event | category | flops | bytes accessed | tf_op | source)
XLA Modules:
  0.0 173.7 jit_solution(18057957090139086865)
XLA Ops:
  4.6 5.5 %collective-permute-start = (bf16[3,2,2048]{2,1,0:T(2,128)(2,1)S(1)}, bf16[3,2,2048]{2,1,0:T(2,128)(2,1)S(1)}, u32[]{:S(2)}, u32[]{:S(2)}) collective-permute-start(bf16[3,2,2048]{2,1,0:T(2,128)(2,1)S(1)} %pad_maximum_fusion.5), channel_id=1, source_target_pairs={{0,1},{1,2},{2,3},{3,4},{4,5},{5,6},{6,7},{8,9},{9,10},{10,11},{11... | collective-permute-start | bytes 73736 | tf_op jit(solution)/shard_map/ppermute | solution.py:16
  12.7 1.3 copy.178
  20.5 6.2 %all-to-all-start.1 = ((bf16[3,8,128,128]{3,2,0,1:T(8,128)(2,1)}), bf16[3,8,128,128]{3,2,0,1:T(8,128)(2,1)S(1)}, u32[]{:S(2)}, u32[]{:S(2)}) async-start(bf16[3,8,128,128]{3,2,0,1:T(8,128)(2,1)} %copy.185), calls=%async_computation.1 | async-start | bytes 1572864 | tf_op jit(solution)/shard_map/all_to_all | solution.py:318
  28.0 18.4 %all-to-all-done.1 = bf16[3,8,128,128]{3,2,0,1:T(8,128)(2,1)S(1)} async-done(((bf16[3,8,128,128]{3,2,0,1:T(8,128)(2,1)}), bf16[3,8,128,128]{3,2,0,1:T(8,128)(2,1)S(1)}, u32[]{:S(2)}, u32[]{:S(2)}) %all-to-all-start.1) | async-done | bytes 786464 | tf_op jit(solution)/shard_map/all_to_all | solution.py:318
  46.4 3.7 %all-to-all-start = ((bf16[3,8,128,128]{3,2,0,1:T(8,128)(2,1)}), bf16[3,8,128,128]{3,2,0,1:T(8,128)(2,1)S(1)}, u32[]{:S(2)}, u32[]{:S(2)}) async-start(bf16[3,8,128,128]{3,2,0,1:T(8,128)(2,1)} %copy.182), calls=%async_computation | async-start | bytes 1572864 | tf_op jit(solution)/shard_map/all_to_all | solution.py:318
  53.6 2.5 %fusion.18 = f32[64,3,64,128]{3,0,2,1:T(8,128)S(1)} fusion(bf16[64,64,1,1]{1,0,3,2:T(8,128)(2,1)S(1)} %copy-done.12, bf16[64,3,64,128]{3,2,1,0:T(8,128)(2,1)S(1)} %bitcast.238), kind=kOutput, calls=%fused_computation.22 | convolution fusion | flops 201326592 | bytes 9445376 | tf_op jit(solution)/shard_map/ab,bskc->askc/dot_general | solution.py:29
  68.2 2.0 %all-to-all-done = bf16[3,8,128,128]{3,2,0,1:T(8,128)(2,1)S(1)} async-done(((bf16[3,8,128,128]{3,2,0,1:T(8,128)(2,1)}), bf16[3,8,128,128]{3,2,0,1:T(8,128)(2,1)S(1)}, u32[]{:S(2)}, u32[]{:S(2)}) %all-to-all-start) | async-done | bytes 786464 | tf_op jit(solution)/shard_map/all_to_all | solution.py:318
  71.4 1.5 fusion.24
  73.9 2.5 %fusion.14 = f32[64,3,64,128]{3,0,2,1:T(8,128)S(1)} fusion(bf16[64,64,1,1]{1,0,3,2:T(8,128)(2,1)S(1)} %copy-done.12, bf16[64,3,64,128]{3,2,1,0:T(8,128)(2,1)S(1)} %bitcast.237), kind=kOutput, calls=%fused_computation.18 | convolution fusion | flops 201326592 | bytes 9445376 | tf_op jit(solution)/shard_map/ab,bskc->askc/dot_general | solution.py:29
  87.9 4.2 %all-to-all-start.3 = ((bf16[2,8,136,128]{3,2,0,1:T(8,128)(2,1)}), bf16[2,8,136,128]{3,2,0,1:T(8,128)(2,1)}, u32[]{:S(2)}, u32[]{:S(2)}) async-start(bf16[2,8,136,128]{3,2,0,1:T(8,128)(2,1)} %fusion.68), calls=%async_computation.3 | async-start | bytes 1114112 | tf_op jit(solution)/shard_map/all_to_all | solution.py:339
  94.1 1.5 collective-permute-start.2
  96.7 2.8 %maximum_maximum_fusion = (bf16[136,2048]{1,0:T(8,128)(2,1)}, bf16[1,136,2048]{2,1,0:T(8,128)(2,1)S(1)}, bf16[1,136,2048]{2,1,0:T(8,128)(2,1)S(1)}, bf16[1,136,2048]{2,1,0:T(8,128)(2,1)S(1)}) fusion(bf16[2,2048]{1,0:T(2,128)(2,1)S(1)} %get-tuple-element.75, bf16[128,2048]{1,0:T(8,128)(2,1)} %bitcast.265, bf16[136]{0:T(256)(128)(2,1)S(1)} %pad.13.clone, ...), kind=kLoop, calls=%fused_computation.106 | loop fusion | flops 8077312 | bytes 4383264 | tf_op jit(solution)/shard_map/concatenate | solution.py:356
  99.4 7.9 %collective-permute-done.2 = f32[2,256,256]{2,1,0:T(8,128)} collective-permute-done((f32[2,256,256]{2,1,0:T(8,128)}, f32[2,256,256]{2,1,0:T(8,128)}, u32[]{:S(2)}, u32[]{:S(2)}) %collective-permute-start.2) | collective-permute-done | bytes 524320 | tf_op jit(solution)/shard_map/ppermute | solution.py:146
  108.5 5.7 %all-to-all-start.2 = ((bf16[2,8,136,128]{3,2,0,1:T(8,128)(2,1)}), bf16[2,8,136,128]{3,2,0,1:T(8,128)(2,1)S(1)}, u32[]{:S(2)}, u32[]{:S(2)}) async-start(bf16[2,8,136,128]{3,2,0,1:T(8,128)(2,1)} %fusion.64), calls=%async_computation.2 | async-start | bytes 1114112 | tf_op jit(solution)/shard_map/all_to_all | solution.py:329
  114.3 1.4 pad_maximum_fusion.src_ref
  117.9 4.6 %collective-permute-start.5 = (f32[128,256]{1,0:T(8,128)S(1)}, f32[128,256]{1,0:T(8,128)S(1)}, u32[]{:S(2)}, u32[]{:S(2)}) collective-permute-start(f32[128,256]{1,0:T(8,128)S(1)} %get-tuple-element.62), channel_id=1, source_target_pairs={{0,1},{2,9},{4,17},{6,25},{8,3},{10,11},{12,19},{14,27},{16,5},{18... | collective-permute-start | bytes 393224 | tf_op jit(solution)/shard_map/ppermute | solution.py:165
  124.5 10.9 %all-to-all-done.2 = bf16[2,8,136,128]{3,2,0,1:T(8,128)(2,1)S(1)} async-done(((bf16[2,8,136,128]{3,2,0,1:T(8,128)(2,1)}), bf16[2,8,136,128]{3,2,0,1:T(8,128)(2,1)S(1)}, u32[]{:S(2)}, u32[]{:S(2)}) %all-to-all-start.2) | async-done | bytes 557088 | tf_op jit(solution)/shard_map/all_to_all | solution.py:329
  136.7 1.7 reshape.213.conv_ref.back_ref
  138.4 8.7 %shard_map.279 = (bf16[4,128,2048]{2,1,0:T(8,128)(2,1)}, f32[16,2048]{1,0:T(8,128)}) custom-call(bf16[2,136,2048]{2,1,0:T(8,128)(2,1)} %reshape.213.conv_ref.back_ref, bf16[2,136,2048]{2,1,0:T(8,128)(2,1)} %reshape.213.conv_ref.back_ref, bf16[3,136,2048]{2,1,0:T(8,128)(2,1)} %pad_maximum_fusion.src_ref, bf16[136,2048]{1,0:T(8,128)(2,1)} %get-tuple-element.80.up_ref, ...), custom_call_target="tpu_custom_call" | custom-call | tf_op jit(solution)/shard_map/pallas_call | solution.py:244
  148.9 2.6 %all-to-all-start.4 = ((f32[32,1,640]{2,1,0:T(1,128)}), f32[32,1,640]{2,1,0:T(1,128)S(1)}, u32[]{:S(2)}, u32[]{:S(2)}) async-start(f32[32,1,640]{2,1,0:T(1,128)} %reshape.222), calls=%async_computation.4 | async-start | bytes 163840 | tf_op jit(solution)/shard_map/all_to_all | solution.py:130
  152.3 6.6 %all-to-all-done.4 = f32[32,1,640]{2,1,0:T(1,128)S(1)} async-done(((f32[32,1,640]{2,1,0:T(1,128)}), f32[32,1,640]{2,1,0:T(1,128)S(1)}, u32[]{:S(2)}, u32[]{:S(2)}) %all-to-all-start.4) | async-done | bytes 81952 | tf_op jit(solution)/shard_map/all_to_all | solution.py:130
  161.3 2.6 %all-to-all-start.5 = ((f32[32,1,640]{2,1,0:T(1,128)}), f32[32,1,640]{2,1,0:T(1,128)S(1)}, u32[]{:S(2)}, u32[]{:S(2)}) async-start(f32[32,1,640]{2,1,0:T(1,128)} %reshape.224), calls=%async_computation.5 | async-start | bytes 163840 | tf_op jit(solution)/shard_map/all_to_all | solution.py:132
  163.8 1.3 fusion.83
  165.2 6.1 %all-to-all-done.5 = f32[32,1,640]{2,1,0:T(1,128)S(1)} async-done(((f32[32,1,640]{2,1,0:T(1,128)}), f32[32,1,640]{2,1,0:T(1,128)S(1)}, u32[]{:S(2)}, u32[]{:S(2)}) %all-to-all-start.5) | async-done | bytes 81952 | tf_op jit(solution)/shard_map/all_to_all | solution.py:132
  (167 shorter events, 60.0 us)
Async XLA Ops:
  0.6 13.5 %copy-start = (bf16[1,128,2048]{2,1,0:T(8,128)(2,1)S(1)}, bf16[1,128,2048]{2,1,0:T(8,128)(2,1)}, u32[]{:S(2)}) copy-start(bf16[1,128,2048]{2,1,0:T(8,128)(2,1)} %param.26) | copy-start | bytes 1572868
  0.6 13.6 %copy-start.2 = (bf16[1,128,2048]{2,1,0:T(8,128)(2,1)S(1)}, bf16[1,128,2048]{2,1,0:T(8,128)(2,1)}, u32[]{:S(2)}) copy-start(bf16[1,128,2048]{2,1,0:T(8,128)(2,1)} %param.24) | copy-start | bytes 1572868
  3.2 10.9 %collective-permute-start.1 = (bf16[4,2,2048]{2,1,0:T(2,128)(2,1)S(1)}, bf16[4,2,2048]{2,1,0:T(2,128)(2,1)S(1)}, u32[]{:S(2)}, u32[]{:S(2)}) collective-permute-start(bf16[4,2,2048]{2,1,0:T(2,128)(2,1)S(1)} %pad_maximum_fusion.4), channel_id=1, source_target_pairs={{1,0},{2,1},{3,2},{4,3},{5,4},{6,5},{7,6},{9,8},{10,9},{11,10},{12... | collective-permute-start | bytes 98312 | tf_op jit(solution)/shard_map/ppermute | solution.py:16
  4.6 9.5 %collective-permute-start = (bf16[3,2,2048]{2,1,0:T(2,128)(2,1)S(1)}, bf16[3,2,2048]{2,1,0:T(2,128)(2,1)S(1)}, u32[]{:S(2)}, u32[]{:S(2)}) collective-permute-start(bf16[3,2,2048]{2,1,0:T(2,128)(2,1)S(1)} %pad_maximum_fusion.5), channel_id=1, source_target_pairs={{0,1},{1,2},{2,3},{3,4},{4,5},{5,6},{6,7},{8,9},{9,10},{10,11},{11... | collective-permute-start | bytes 73736 | tf_op jit(solution)/shard_map/ppermute | solution.py:16
  20.5 25.9 %all-to-all-start.1 = ((bf16[3,8,128,128]{3,2,0,1:T(8,128)(2,1)}), bf16[3,8,128,128]{3,2,0,1:T(8,128)(2,1)S(1)}, u32[]{:S(2)}, u32[]{:S(2)}) async-start(bf16[3,8,128,128]{3,2,0,1:T(8,128)(2,1)} %copy.185), calls=%async_computation.1 | async-start | bytes 1572864 | tf_op jit(solution)/shard_map/all_to_all | solution.py:318
  28.0 22.2 %copy-start.16 = (bf16[128,32,1,1]{0,1,3,2:T(8,128)(2,1)S(1)}, bf16[128,32,1,1]{0,1,3,2:T(8,128)(2,1)}, u32[]{:S(2)}) copy-start(bf16[128,32,1,1]{0,1,3,2:T(8,128)(2,1)} %constant.113) | copy-start | bytes 24580
  46.4 23.9 %all-to-all-start = ((bf16[3,8,128,128]{3,2,0,1:T(8,128)(2,1)}), bf16[3,8,128,128]{3,2,0,1:T(8,128)(2,1)S(1)}, u32[]{:S(2)}, u32[]{:S(2)}) async-start(bf16[3,8,128,128]{3,2,0,1:T(8,128)(2,1)} %copy.182), calls=%async_computation | async-start | bytes 1572864 | tf_op jit(solution)/shard_map/all_to_all | solution.py:318
  58.3 1.1 copy-start.9
  58.3 1.1 copy-start.10
  87.9 20.6 %all-to-all-start.3 = ((bf16[2,8,136,128]{3,2,0,1:T(8,128)(2,1)}), bf16[2,8,136,128]{3,2,0,1:T(8,128)(2,1)}, u32[]{:S(2)}, u32[]{:S(2)}) async-start(bf16[2,8,136,128]{3,2,0,1:T(8,128)(2,1)} %fusion.68), calls=%async_computation.3 | async-start | bytes 1114112 | tf_op jit(solution)/shard_map/all_to_all | solution.py:339
  92.7 4.0 %copy-start.1 = (bf16[1,128,2048]{2,1,0:T(8,128)(2,1)S(1)}, bf16[1,128,2048]{2,1,0:T(8,128)(2,1)}, u32[]{:S(2)}) copy-start(bf16[1,128,2048]{2,1,0:T(8,128)(2,1)} %param.26) | copy-start | bytes 1572868
  92.7 3.9 %copy-start.3 = (bf16[1,128,2048]{2,1,0:T(8,128)(2,1)S(1)}, bf16[1,128,2048]{2,1,0:T(8,128)(2,1)}, u32[]{:S(2)}) copy-start(bf16[1,128,2048]{2,1,0:T(8,128)(2,1)} %param.24) | copy-start | bytes 1572868
  92.7 3.9 %copy-start.5 = (bf16[1,128,2048]{2,1,0:T(8,128)(2,1)S(1)}, bf16[1,128,2048]{2,1,0:T(8,128)(2,1)}, u32[]{:S(2)}) copy-start(bf16[1,128,2048]{2,1,0:T(8,128)(2,1)} %param.25) | copy-start | bytes 1572868
  94.1 13.3 %collective-permute-start.2 = (f32[2,256,256]{2,1,0:T(8,128)}, f32[2,256,256]{2,1,0:T(8,128)}, u32[]{:S(2)}, u32[]{:S(2)}) collective-permute-start(f32[2,256,256]{2,1,0:T(8,128)} %bitcast.112), channel_id=1, source_target_pairs={{0,16},{8,24},{16,0},{24,8},{1,17},{9,25},{17,1},{25,9},{2,18},{10... | collective-permute-start | bytes 1572872 | tf_op jit(solution)/shard_map/ppermute | solution.py:146
  96.7 10.7 %copy-start.7 = (f32[512,256]{1,0:T(8,128)S(1)}, f32[512,256]{1,0:T(8,128)}, u32[]{:S(2)}) copy-start(f32[512,256]{1,0:T(8,128)} %get-tuple-element.55) | copy-start | bytes 1572868
  108.5 26.9 %all-to-all-start.2 = ((bf16[2,8,136,128]{3,2,0,1:T(8,128)(2,1)}), bf16[2,8,136,128]{3,2,0,1:T(8,128)(2,1)S(1)}, u32[]{:S(2)}, u32[]{:S(2)}) async-start(bf16[2,8,136,128]{3,2,0,1:T(8,128)(2,1)} %fusion.64), calls=%async_computation.2 | async-start | bytes 1114112 | tf_op jit(solution)/shard_map/all_to_all | solution.py:329
  114.3 1.6 collective-permute-start.3
  115.9 35.6 %collective-permute-start.4 = (f32[128,256]{1,0:T(8,128)S(1)}, f32[128,256]{1,0:T(8,128)S(1)}, u32[]{:S(2)}, u32[]{:S(2)}) collective-permute-start(f32[128,256]{1,0:T(8,128)S(1)} %get-tuple-element.63), channel_id=1, source_target_pairs={{0,0},{2,8},{4,16},{6,24},{8,2},{10,10},{12,18},{14,26},{16,4},{18... | collective-permute-start | bytes 393224 | tf_op jit(solution)/shard_map/ppermute | solution.py:165
  116.6 34.9 %collective-permute-start.6 = (f32[128,256]{1,0:T(8,128)S(1)}, f32[128,256]{1,0:T(8,128)S(1)}, u32[]{:S(2)}, u32[]{:S(2)}) collective-permute-start(f32[128,256]{1,0:T(8,128)S(1)} %get-tuple-element.63), channel_id=1, source_target_pairs={{1,0},{3,8},{5,16},{7,24},{9,2},{11,10},{13,18},{15,26},{17,4},{19... | collective-permute-start | bytes 393224 | tf_op jit(solution)/shard_map/ppermute | solution.py:165
  117.9 33.6 %collective-permute-start.5 = (f32[128,256]{1,0:T(8,128)S(1)}, f32[128,256]{1,0:T(8,128)S(1)}, u32[]{:S(2)}, u32[]{:S(2)}) collective-permute-start(f32[128,256]{1,0:T(8,128)S(1)} %get-tuple-element.62), channel_id=1, source_target_pairs={{0,1},{2,9},{4,17},{6,25},{8,3},{10,11},{12,19},{14,27},{16,5},{18... | collective-permute-start | bytes 393224 | tf_op jit(solution)/shard_map/ppermute | solution.py:165
  122.5 29.1 %collective-permute-start.7 = (f32[128,256]{1,0:T(8,128)S(1)}, f32[128,256]{1,0:T(8,128)S(1)}, u32[]{:S(2)}, u32[]{:S(2)}) collective-permute-start(f32[128,256]{1,0:T(8,128)S(1)} %get-tuple-element.62), channel_id=1, source_target_pairs={{1,1},{3,9},{5,17},{7,25},{9,3},{11,11},{13,19},{15,27},{17,5},{19... | collective-permute-start | bytes 393224 | tf_op jit(solution)/shard_map/ppermute | solution.py:165
  148.2 15.7 %copy-start.8 = (bf16[4,128,2048]{2,1,0:T(8,128)(2,1)S(1)}, bf16[4,128,2048]{2,1,0:T(8,128)(2,1)}, u32[]{:S(2)}) copy-start(bf16[4,128,2048]{2,1,0:T(8,128)(2,1)} %get-tuple-element.13) | copy-start | bytes 6291460
  148.9 10.0 %all-to-all-start.4 = ((f32[32,1,640]{2,1,0:T(1,128)}), f32[32,1,640]{2,1,0:T(1,128)S(1)}, u32[]{:S(2)}, u32[]{:S(2)}) async-start(f32[32,1,640]{2,1,0:T(1,128)} %reshape.222), calls=%async_computation.4 | async-start | bytes 163840 | tf_op jit(solution)/shard_map/all_to_all | solution.py:130
  161.3 10.0 %all-to-all-start.5 = ((f32[32,1,640]{2,1,0:T(1,128)}), f32[32,1,640]{2,1,0:T(1,128)S(1)}, u32[]{:S(2)}, u32[]{:S(2)}) async-start(f32[32,1,640]{2,1,0:T(1,128)} %reshape.224), calls=%async_computation.5 | async-start | bytes 163840 | tf_op jit(solution)/shard_map/all_to_all | solution.py:132
  (7 other events, 6.3 us)

commit v8 on v7

--- a/solution.py
+++ b/solution.py
@@ -287,27 +287,24 @@
     prev = shifted(jnp.stack([a[rows - head :] for a in (q_rows, k_rows, v_rows)]), "ctx", 1)
     nxt = shifted(jnp.stack([a[:head] for a in (q_rows, k_rows, v_rows, c_rows)]), "ctx", -1)
     padded = [
-        jnp.concatenate([prev[i], src, nxt[i]], 0).astype(jnp.float32)
+        jnp.concatenate([prev[i], src], 0).astype(jnp.float32)
         for i, src in enumerate((q_rows, k_rows, v_rows))
     ]
 
     def short_forward(wide, weights):
-        summed = weights[0] * wide[head : head + ext]
+        summed = weights[0] * wide[head : head + rows]
         for offset in range(1, taps):
             begin_at = head - offset
             summed = summed + jnp.where(
-                valid[offset][:, None], weights[offset] * wide[begin_at : begin_at + ext], 0.0
+                valid[offset, :rows][:, None], weights[offset] * wide[begin_at : begin_at + rows], 0.0
             )
         return summed.astype(jnp.bfloat16).astype(jnp.float32)
 
     q_short = short_forward(padded[0], short_weights[0])
     k_short = short_forward(padded[1], short_weights[1])
     v_short = short_forward(padded[2], short_weights[2])
-    upstream = jnp.concatenate([c_rows, nxt[3]], 0).astype(jnp.float32)
     mixed = (k_short * v_short).astype(jnp.bfloat16)
-    grad_conv = (upstream * q_short).astype(jnp.bfloat16)
-    mixed_wide = mixed.astype(jnp.float32)
-    grad_wide = grad_conv.astype(jnp.float32)
+    grad_conv = (c_rows.astype(jnp.float32) * q_short).astype(jnp.bfloat16)
 
     chunks = 2 if lanes % 2 == 0 else 1
     width = lanes // chunks
@@ -318,7 +315,7 @@
         moved = lax.all_to_all(split.transpose(0, 2, 1, 3), "ctx", 1, 1, tiled=True)
         return moved.reshape(count, seq_len, width)
 
-    sent = jnp.stack([long_filter, mixed[:rows], grad_conv[:rows]])
+    sent = jnp.stack([long_filter, mixed, grad_conv])
     returned = []
     lagged_parts = []
     previous = None

time: 175 us -> 169 us (0.966)
  waiting for transfers between devices: 52.1 us -> 48.8 us
  local copies, waits for them, and re-layouts: 35.4 us -> 33.3 us
    ppermute x4, starting transfers between devices: 7.45 us -> 9.96 us  [route_filter_grad(): got = lax.ppermute(pieces[piece], ('dp', 'ctx'), pairs)]
    all_to_all x2, waiting for transfers between devices: 20.4 us -> 18 us  [to_columns(): moved = lax.all_to_all(split.transpose(0, 2, 1, 3), 'ctx', 1, 1, tiled=True)]
    add x2, other arithmetic: 0.04 us -> 1.91 us  [route_filter_grad(): total = got if total is None else total + got]
    all_to_all x1, waiting for transfers between devices: 6.61 us -> 4.75 us  [mesh_sum(): mine = jnp.sum(lax.all_to_all(pieces, axes, 0, 0, tiled=True), axis=0)]
    unnamed x53 -> x47, local copies, waits for them, and re-layouts: 14 us -> 12.9 us
  transfers between devices with their start and end apart: 14 -> 14, of which waited for: 7 -> 8; matrix products, arithmetic and copies ran while one was open for 22% -> 34% of each run, Pallas kernels for 5% -> 5%
where the time goes in v8:
time: 169 us; the launch traced here: 167 us
  waiting for transfers between devices  48.8 us (29%)
  starting transfers between devices  39.9 us (24%)
  local copies, waits for them, and re-layouts  33.3 us (20%)
  other arithmetic  23.6 us (14%)
  matrix products  11.7 us (7%)
  Pallas kernels  8.66 us (5%)
    all_to_all x2, waiting for transfers between devices, to_columns(): moved = lax.all_to_all(split.transpose(0, 2, 1, 3), 'ctx', 1, 1, tiled=True)  18 us
    unnamed x47, local copies, waits for them, and re-layouts  12.9 us
    dot_general x8, matrix products, split_product(): jnp.einsum(form, upper, data.astype(jnp.bfloat16), preferred_element_type...  11.7 us
    all_to_all x2, waiting for transfers between devices, local(): returned.append(lax.all_to_all(previous, 'ctx', 1, 1, tiled=True))  11.3 us
    ppermute x4, starting transfers between devices, route_filter_grad(): got = lax.ppermute(pieces[piece], ('dp', 'ctx'), pairs)  9.96 us
    all_to_all x2, starting transfers between devices, to_columns(): moved = lax.all_to_all(split.transpose(0, 2, 1, 3), 'ctx', 1, 1, tiled=True)  8.74 us
    ppermute x2, waiting for transfers between devices, halving_rows(): lax.ppermute(give, axis, [(i, i ^ step) for i in range(size)])  8.69 us
    pallas_call x1, Pallas kernels, epilogue(): pl.pallas_call(epilogue_kernel, grid=grid, in_specs=[pl.BlockSpec((None,...  8.66 us
  transfers between devices with their start and end apart: 14, of which 8 were waited for; matrix products, arithmetic and copies ran while one was open for 34% of the time, Pallas kernels for 5%

profile of v8, /device:TPU:0, one launch (start us, length us, event | category | flops | bytes accessed | tf_op | source)
XLA Modules:
  0.0 167.4 jit_solution(17110707022573455683)
XLA Ops:
  2.4 4.9 %collective-permute-start = (bf16[3,2,2048]{2,1,0:T(2,128)(2,1)S(1)}, bf16[3,2,2048]{2,1,0:T(2,128)(2,1)S(1)}, u32[]{:S(2)}, u32[]{:S(2)}) collective-permute-start(bf16[3,2,2048]{2,1,0:T(2,128)(2,1)S(1)} %pad_maximum_fusion.4), channel_id=1, source_target_pairs={{0,1},{1,2},{2,3},{3,4},{4,5},{5,6},{6,7},{8,9},{9,10},{10,11},{11... | collective-permute-start | bytes 73736 | tf_op jit(solution)/shard_map/ppermute | solution.py:16
  16.6 5.0 %all-to-all-start.1 = ((bf16[3,8,128,128]{3,2,0,1:T(8,128)(2,1)}), bf16[3,8,128,128]{3,2,0,1:T(8,128)(2,1)S(1)}, u32[]{:S(2)}, u32[]{:S(2)}) async-start(bf16[3,8,128,128]{3,2,0,1:T(8,128)(2,1)} %copy.185), calls=%async_computation.1 | async-start | bytes 1572864 | tf_op jit(solution)/shard_map/all_to_all | solution.py:315
  25.5 16.4 %all-to-all-done.1 = bf16[3,8,128,128]{3,2,0,1:T(8,128)(2,1)S(1)} async-done(((bf16[3,8,128,128]{3,2,0,1:T(8,128)(2,1)}), bf16[3,8,128,128]{3,2,0,1:T(8,128)(2,1)S(1)}, u32[]{:S(2)}, u32[]{:S(2)}) %all-to-all-start.1) | async-done | bytes 786464 | tf_op jit(solution)/shard_map/all_to_all | solution.py:315
  41.9 3.7 %all-to-all-start = ((bf16[3,8,128,128]{3,2,0,1:T(8,128)(2,1)}), bf16[3,8,128,128]{3,2,0,1:T(8,128)(2,1)S(1)}, u32[]{:S(2)}, u32[]{:S(2)}) async-start(bf16[3,8,128,128]{3,2,0,1:T(8,128)(2,1)} %copy.182), calls=%async_computation | async-start | bytes 1572864 | tf_op jit(solution)/shard_map/all_to_all | solution.py:315
  49.1 2.5 %fusion.18 = f32[64,3,64,128]{3,0,2,1:T(8,128)S(1)} fusion(bf16[64,64,1,1]{1,0,3,2:T(8,128)(2,1)S(1)} %copy-done.9, bf16[64,3,64,128]{3,2,1,0:T(8,128)(2,1)S(1)} %bitcast.242), kind=kOutput, calls=%fused_computation.22 | convolution fusion | flops 201326592 | bytes 9445376 | tf_op jit(solution)/shard_map/ab,bskc->askc/dot_general | solution.py:29
  63.9 1.6 all-to-all-done
  66.5 1.5 fusion.24
  69.1 2.5 %fusion.14 = f32[64,3,64,128]{3,0,2,1:T(8,128)S(1)} fusion(bf16[64,64,1,1]{1,0,3,2:T(8,128)(2,1)S(1)} %copy-done.9, bf16[64,3,64,128]{3,2,1,0:T(8,128)(2,1)S(1)} %bitcast.241), kind=kOutput, calls=%fused_computation.18 | convolution fusion | flops 201326592 | bytes 9445376 | tf_op jit(solution)/shard_map/ab,bskc->askc/dot_general | solution.py:29
  83.9 4.2 %all-to-all-start.3 = ((bf16[2,8,136,128]{3,2,0,1:T(8,128)(2,1)}), bf16[2,8,136,128]{3,2,0,1:T(8,128)(2,1)S(1)}, u32[]{:S(2)}, u32[]{:S(2)}) async-start(bf16[2,8,136,128]{3,2,0,1:T(8,128)(2,1)} %fusion.74), calls=%async_computation.3 | async-start | bytes 1114112 | tf_op jit(solution)/shard_map/all_to_all | solution.py:336
  88.1 1.6 collective-permute-start.2
  89.7 2.8 %maximum_maximum_fusion = (bf16[136,2048]{1,0:T(8,128)(2,1)}, bf16[1,136,2048]{2,1,0:T(8,128)(2,1)S(1)}, bf16[1,136,2048]{2,1,0:T(8,128)(2,1)S(1)}, bf16[1,136,2048]{2,1,0:T(8,128)(2,1)S(1)}) fusion(bf16[2,2048]{1,0:T(2,128)(2,1)S(1)} %get-tuple-element.62, bf16[128,2048]{1,0:T(8,128)(2,1)} %bitcast.269, bf16[136]{0:T(256)(128)(2,1)S(1)} %pad.13.clone, ...), kind=kLoop, calls=%fused_computation.106 | loop fusion | flops 8077312 | bytes 4383264 | tf_op jit(solution)/shard_map/concatenate | solution.py:353
  92.5 8.5 %collective-permute-done.2 = f32[2,256,256]{2,1,0:T(8,128)S(1)} collective-permute-done((f32[2,256,256]{2,1,0:T(8,128)S(1)}, f32[2,256,256]{2,1,0:T(8,128)S(1)}, u32[]{:S(2)}, u32[]{:S(2)}) %collective-permute-start.2) | collective-permute-done | bytes 524320 | tf_op jit(solution)/shard_map/ppermute | solution.py:146
  101.2 1.6 all-to-all-done.3
  102.8 4.1 %all-to-all-start.2 = ((bf16[2,8,136,128]{3,2,0,1:T(8,128)(2,1)}), bf16[2,8,136,128]{3,2,0,1:T(8,128)(2,1)S(1)}, u32[]{:S(2)}, u32[]{:S(2)}) async-start(bf16[2,8,136,128]{3,2,0,1:T(8,128)(2,1)} %fusion.70), calls=%async_computation.2 | async-start | bytes 1114112 | tf_op jit(solution)/shard_map/all_to_all | solution.py:326
  107.0 1.4 pad_maximum_fusion.src_ref
  109.3 2.2 %collective-permute-start.4 = (f32[128,256]{1,0:T(8,128)}, f32[128,256]{1,0:T(8,128)}, u32[]{:S(2)}, u32[]{:S(2)}) collective-permute-start(f32[128,256]{1,0:T(8,128)} %get-tuple-element.52), channel_id=1, source_target_pairs={{0,0},{2,8},{4,16},{6,24},{8,2},{10,10},{12,18},{14,26},{16,4},{18... | collective-permute-start | bytes 393224 | tf_op jit(solution)/shard_map/ppermute | solution.py:165
  112.7 5.2 %collective-permute-start.5 = (f32[128,256]{1,0:T(8,128)}, f32[128,256]{1,0:T(8,128)}, u32[]{:S(2)}, u32[]{:S(2)}) collective-permute-start(f32[128,256]{1,0:T(8,128)} %get-tuple-element.51), channel_id=1, source_target_pairs={{0,1},{2,9},{4,17},{6,25},{8,3},{10,11},{12,19},{14,27},{16,5},{18... | collective-permute-start | bytes 393224 | tf_op jit(solution)/shard_map/ppermute | solution.py:165
  119.3 9.6 %all-to-all-done.2 = bf16[2,8,136,128]{3,2,0,1:T(8,128)(2,1)S(1)} async-done(((bf16[2,8,136,128]{3,2,0,1:T(8,128)(2,1)}), bf16[2,8,136,128]{3,2,0,1:T(8,128)(2,1)S(1)}, u32[]{:S(2)}, u32[]{:S(2)}) %all-to-all-start.2) | async-done | bytes 557088 | tf_op jit(solution)/shard_map/all_to_all | solution.py:326
  130.3 1.7 reshape.213.conv_ref.back_ref
  131.9 8.7 %shard_map.279 = (bf16[4,128,2048]{2,1,0:T(8,128)(2,1)}, f32[16,2048]{1,0:T(8,128)}) custom-call(bf16[2,136,2048]{2,1,0:T(8,128)(2,1)} %reshape.213.conv_ref.back_ref, bf16[2,136,2048]{2,1,0:T(8,128)(2,1)} %reshape.213.conv_ref.back_ref, bf16[3,136,2048]{2,1,0:T(8,128)(2,1)} %pad_maximum_fusion.src_ref, bf16[136,2048]{1,0:T(8,128)(2,1)} %get-tuple-element.71.up_ref, ...), custom_call_target="tpu_custom_call" | custom-call | tf_op jit(solution)/shard_map/pallas_call | solution.py:244
  142.6 2.6 %all-to-all-start.4 = ((f32[32,1,640]{2,1,0:T(1,128)}), f32[32,1,640]{2,1,0:T(1,128)S(1)}, u32[]{:S(2)}, u32[]{:S(2)}) async-start(f32[32,1,640]{2,1,0:T(1,128)} %reshape.220), calls=%async_computation.4 | async-start | bytes 163840 | tf_op jit(solution)/shard_map/all_to_all | solution.py:130
  147.9 4.7 %all-to-all-done.4 = f32[32,1,640]{2,1,0:T(1,128)S(1)} async-done(((f32[32,1,640]{2,1,0:T(1,128)}), f32[32,1,640]{2,1,0:T(1,128)S(1)}, u32[]{:S(2)}, u32[]{:S(2)}) %all-to-all-start.4) | async-done | bytes 81952 | tf_op jit(solution)/shard_map/all_to_all | solution.py:130
  155.0 2.6 %all-to-all-start.5 = ((f32[32,1,640]{2,1,0:T(1,128)}), f32[32,1,640]{2,1,0:T(1,128)S(1)}, u32[]{:S(2)}, u32[]{:S(2)}) async-start(f32[32,1,640]{2,1,0:T(1,128)} %reshape.222), calls=%async_computation.5 | async-start | bytes 163840 | tf_op jit(solution)/shard_map/all_to_all | solution.py:132
  158.9 6.1 %all-to-all-done.5 = f32[32,1,640]{2,1,0:T(1,128)S(1)} async-done(((f32[32,1,640]{2,1,0:T(1,128)}), f32[32,1,640]{2,1,0:T(1,128)S(1)}, u32[]{:S(2)}, u32[]{:S(2)}) %all-to-all-start.5) | async-done | bytes 81952 | tf_op jit(solution)/shard_map/all_to_all | solution.py:132
  (160 shorter events, 60.3 us)
Async XLA Ops:
  0.6 11.9 %copy-start.2 = (bf16[1,128,2048]{2,1,0:T(8,128)(2,1)S(1)}, bf16[1,128,2048]{2,1,0:T(8,128)(2,1)}, u32[]{:S(2)}) copy-start(bf16[1,128,2048]{2,1,0:T(8,128)(2,1)} %param.26) | copy-start | bytes 1572868
  2.4 8.9 %collective-permute-start = (bf16[3,2,2048]{2,1,0:T(2,128)(2,1)S(1)}, bf16[3,2,2048]{2,1,0:T(2,128)(2,1)S(1)}, u32[]{:S(2)}, u32[]{:S(2)}) collective-permute-start(bf16[3,2,2048]{2,1,0:T(2,128)(2,1)S(1)} %pad_maximum_fusion.4), channel_id=1, source_target_pairs={{0,1},{1,2},{2,3},{3,4},{4,5},{5,6},{6,7},{8,9},{9,10},{10,11},{11... | collective-permute-start | bytes 73736 | tf_op jit(solution)/shard_map/ppermute | solution.py:16
  12.7 1.3 copy-start.1
  12.7 1.5 copy-start.4
  16.6 29.1 %copy-start.13 = (bf16[128,32,1,1]{0,1,3,2:T(8,128)(2,1)S(1)}, bf16[128,32,1,1]{0,1,3,2:T(8,128)(2,1)}, u32[]{:S(2)}) copy-start(bf16[128,32,1,1]{0,1,3,2:T(8,128)(2,1)} %constant.113) | copy-start | bytes 24580
  16.6 25.3 %all-to-all-start.1 = ((bf16[3,8,128,128]{3,2,0,1:T(8,128)(2,1)}), bf16[3,8,128,128]{3,2,0,1:T(8,128)(2,1)S(1)}, u32[]{:S(2)}, u32[]{:S(2)}) async-start(bf16[3,8,128,128]{3,2,0,1:T(8,128)(2,1)} %copy.185), calls=%async_computation.1 | async-start | bytes 1572864 | tf_op jit(solution)/shard_map/all_to_all | solution.py:315
  21.7 68.0 %collective-permute-start.1 = (bf16[4,2,2048]{2,1,0:T(2,128)(2,1)S(1)}, bf16[4,2,2048]{2,1,0:T(2,128)(2,1)S(1)}, u32[]{:S(2)}, u32[]{:S(2)}) collective-permute-start(bf16[4,2,2048]{2,1,0:T(2,128)(2,1)S(1)} %pad_maximum_fusion.3), channel_id=1, source_target_pairs={{1,0},{2,1},{3,2},{4,3},{5,4},{6,5},{7,6},{9,8},{10,9},{11,10},{12... | collective-permute-start | bytes 98312 | tf_op jit(solution)/shard_map/ppermute | solution.py:16
  41.9 23.6 %all-to-all-start = ((bf16[3,8,128,128]{3,2,0,1:T(8,128)(2,1)}), bf16[3,8,128,128]{3,2,0,1:T(8,128)(2,1)S(1)}, u32[]{:S(2)}, u32[]{:S(2)}) async-start(bf16[3,8,128,128]{3,2,0,1:T(8,128)(2,1)} %copy.182), calls=%async_computation | async-start | bytes 1572864 | tf_op jit(solution)/shard_map/all_to_all | solution.py:315
  53.6 1.1 copy-start.6
  53.6 1.1 copy-start.7
  58.1 14.8 %copy-start = (f32[3,32,32,128]{3,1,2,0:T(8,128)}, f32[3,32,32,128]{3,1,2,0:T(8,128)S(1)}, u32[]{:S(2)}) copy-start(f32[3,32,32,128]{3,1,2,0:T(8,128)S(1)} %fusion.28) | copy-start | bytes 4718596
  76.5 1.7 %slice-start = ((f32[3,32,32,128]{3,1,2,0:T(8,128)}), f32[1,32,32,128]{3,1,2,0:T(8,128)S(1)}, s32[]{:S(2)}) async-start(f32[3,32,32,128]{3,1,2,0:T(8,128)} %copy-done), calls=%async_computation.6 | async-start | bytes 1048576 | tf_op jit(solution)/shard_map/slice | solution.py:329
  78.5 11.2 %copy-start.3 = (bf16[1,128,2048]{2,1,0:T(8,128)(2,1)S(1)}, bf16[1,128,2048]{2,1,0:T(8,128)(2,1)}, u32[]{:S(2)}) copy-start(bf16[1,128,2048]{2,1,0:T(8,128)(2,1)} %param.26) | copy-start | bytes 1572868
  83.9 18.9 %all-to-all-start.3 = ((bf16[2,8,136,128]{3,2,0,1:T(8,128)(2,1)}), bf16[2,8,136,128]{3,2,0,1:T(8,128)(2,1)S(1)}, u32[]{:S(2)}, u32[]{:S(2)}) async-start(bf16[2,8,136,128]{3,2,0,1:T(8,128)(2,1)} %fusion.74), calls=%async_computation.3 | async-start | bytes 1114112 | tf_op jit(solution)/shard_map/all_to_all | solution.py:336
  88.1 13.0 %collective-permute-start.2 = (f32[2,256,256]{2,1,0:T(8,128)S(1)}, f32[2,256,256]{2,1,0:T(8,128)S(1)}, u32[]{:S(2)}, u32[]{:S(2)}) collective-permute-start(f32[2,256,256]{2,1,0:T(8,128)S(1)} %bitcast.279), channel_id=1, source_target_pairs={{0,16},{8,24},{16,0},{24,8},{1,17},{9,25},{17,1},{25,9},{2,18},{10... | collective-permute-start | bytes 1572872 | tf_op jit(solution)/shard_map/ppermute | solution.py:146
  102.8 26.2 %all-to-all-start.2 = ((bf16[2,8,136,128]{3,2,0,1:T(8,128)(2,1)}), bf16[2,8,136,128]{3,2,0,1:T(8,128)(2,1)S(1)}, u32[]{:S(2)}, u32[]{:S(2)}) async-start(bf16[2,8,136,128]{3,2,0,1:T(8,128)(2,1)} %fusion.70), calls=%async_computation.2 | async-start | bytes 1114112 | tf_op jit(solution)/shard_map/all_to_all | solution.py:326
  106.9 1.6 collective-permute-start.3
  109.3 35.9 %collective-permute-start.4 = (f32[128,256]{1,0:T(8,128)}, f32[128,256]{1,0:T(8,128)}, u32[]{:S(2)}, u32[]{:S(2)}) collective-permute-start(f32[128,256]{1,0:T(8,128)} %get-tuple-element.52), channel_id=1, source_target_pairs={{0,0},{2,8},{4,16},{6,24},{8,2},{10,10},{12,18},{14,26},{16,4},{18... | collective-permute-start | bytes 393224 | tf_op jit(solution)/shard_map/ppermute | solution.py:165
  111.5 34.8 %collective-permute-start.6 = (f32[128,256]{1,0:T(8,128)}, f32[128,256]{1,0:T(8,128)S(1)}, u32[]{:S(2)}, u32[]{:S(2)}) collective-permute-start(f32[128,256]{1,0:T(8,128)} %get-tuple-element.52), channel_id=1, source_target_pairs={{1,0},{3,8},{5,16},{7,24},{9,2},{11,10},{13,18},{15,26},{17,4},{19... | collective-permute-start | bytes 393224 | tf_op jit(solution)/shard_map/ppermute | solution.py:165
  112.7 32.5 %collective-permute-start.5 = (f32[128,256]{1,0:T(8,128)}, f32[128,256]{1,0:T(8,128)}, u32[]{:S(2)}, u32[]{:S(2)}) collective-permute-start(f32[128,256]{1,0:T(8,128)} %get-tuple-element.51), channel_id=1, source_target_pairs={{0,1},{2,9},{4,17},{6,25},{8,3},{10,11},{12,19},{14,27},{16,5},{18... | collective-permute-start | bytes 393224 | tf_op jit(solution)/shard_map/ppermute | solution.py:165
  118.0 28.3 %collective-permute-start.7 = (f32[128,256]{1,0:T(8,128)}, f32[128,256]{1,0:T(8,128)}, u32[]{:S(2)}, u32[]{:S(2)}) collective-permute-start(f32[128,256]{1,0:T(8,128)} %get-tuple-element.51), channel_id=1, source_target_pairs={{1,1},{3,9},{5,17},{7,25},{9,3},{11,11},{13,19},{15,27},{17,5},{19... | collective-permute-start | bytes 393224 | tf_op jit(solution)/shard_map/ppermute | solution.py:165
  140.6 16.9 %copy-start.5 = (bf16[4,128,2048]{2,1,0:T(8,128)(2,1)S(1)}, bf16[4,128,2048]{2,1,0:T(8,128)(2,1)}, u32[]{:S(2)}) copy-start(bf16[4,128,2048]{2,1,0:T(8,128)(2,1)} %get-tuple-element.13) | copy-start | bytes 6291460
  142.6 10.0 %all-to-all-start.4 = ((f32[32,1,640]{2,1,0:T(1,128)}), f32[32,1,640]{2,1,0:T(1,128)S(1)}, u32[]{:S(2)}, u32[]{:S(2)}) async-start(f32[32,1,640]{2,1,0:T(1,128)} %reshape.220), calls=%async_computation.4 | async-start | bytes 163840 | tf_op jit(solution)/shard_map/all_to_all | solution.py:130
  155.0 10.0 %all-to-all-start.5 = ((f32[32,1,640]{2,1,0:T(1,128)}), f32[32,1,640]{2,1,0:T(1,128)S(1)}, u32[]{:S(2)}, u32[]{:S(2)}) async-start(f32[32,1,640]{2,1,0:T(1,128)} %reshape.222), calls=%async_computation.5 | async-start | bytes 163840 | tf_op jit(solution)/shard_map/all_to_all | solution.py:132
  (5 other events, 4.2 us)

commit v9 on v8

--- a/solution.py
+++ b/solution.py
@@ -285,7 +285,6 @@
     valid_after = valid & (position < seq_len)[None, :]
 
     prev = shifted(jnp.stack([a[rows - head :] for a in (q_rows, k_rows, v_rows)]), "ctx", 1)
-    nxt = shifted(jnp.stack([a[:head] for a in (q_rows, k_rows, v_rows, c_rows)]), "ctx", -1)
     padded = [
         jnp.concatenate([prev[i], src], 0).astype(jnp.float32)
         for i, src in enumerate((q_rows, k_rows, v_rows))
@@ -333,7 +332,10 @@
         )
         blocks = jnp.stack([raw[:, j * rows : j * rows + frame] for j in range(parts)], 1)
         previous = blocks
+    following = jnp.stack([a[:head] for a in (q_rows, k_rows, v_rows, c_rows)])
+    following, previous = lax.optimization_barrier((following, previous))
     returned.append(lax.all_to_all(previous, "ctx", 1, 1, tiled=True))
+    nxt = shifted(following, "ctx", -1)
     back = jnp.stack(returned, 3).transpose(0, 2, 1, 3, 4).reshape(2, frame, chans)
     lagged = halving_rows(jnp.concatenate(lagged_parts, 1), "dp")
     filter_part = route_filter_grad(lagged, rows)

time: 169 us -> 163 us (0.964)
  starting transfers between devices: 39.9 us -> 47.7 us
  waiting for transfers between devices: 48.8 us -> 41.7 us
  local copies, waits for them, and re-layouts: 33.3 us -> 28.3 us
    all_to_all x2, waiting for transfers between devices: 11.3 us -> 1.43 us  [local(): returned.append(lax.all_to_all(previous, 'ctx', 1, 1, tiled=True))]
    all_to_all x1, starting transfers between devices: 2.57 us -> 8.61 us  [mesh_sum(): mine = jnp.sum(lax.all_to_all(pieces, axes, 0, 0, tiled=True), axis=0)]
    unnamed x47 -> x53, local copies, waits for them, and re-layouts: 12.9 us -> 8.52 us
    ppermute x2, waiting for transfers between devices: 0.01 us -> 3.74 us  [shifted(): return lax.ppermute(x, axis, pairs)]
    ppermute x2, waiting for transfers between devices: 8.69 us -> 6.47 us  [halving_rows(): lax.ppermute(give, axis, [(i, i ^ step) for i in range(size)])]
    all_to_all x2, starting transfers between devices: 8.26 us -> 10.5 us  [local(): returned.append(lax.all_to_all(previous, 'ctx', 1, 1, tiled=True))]
  transfers between devices with their start and end apart: 14 -> 14, of which waited for: 8 -> 8; matrix products, arithmetic and copies ran while one was open for 34% -> 23% of each run, Pallas kernels for 5% -> 5%
where the time goes in v9:
time: 163 us; the launch traced here: 162 us
  starting transfers between devices  47.7 us (29%)
  waiting for transfers between devices  41.7 us (26%)
  local copies, waits for them, and re-layouts  28.3 us (17%)
  other arithmetic  22.6 us (14%)
  matrix products  11.7 us (7%)
  Pallas kernels  8.68 us (5%)
    all_to_all x2, waiting for transfers between devices, to_columns(): moved = lax.all_to_all(split.transpose(0, 2, 1, 3), 'ctx', 1, 1, tiled=True)  19.3 us
    dot_general x8, matrix products, split_product(): jnp.einsum(form, upper, data.astype(jnp.bfloat16), preferred_element_type...  11.7 us
    all_to_all x2, starting transfers between devices, local(): returned.append(lax.all_to_all(previous, 'ctx', 1, 1, tiled=True))  10.5 us
    ppermute x4, starting transfers between devices, route_filter_grad(): got = lax.ppermute(pieces[piece], ('dp', 'ctx'), pairs)  9.54 us
    all_to_all x2, starting transfers between devices, to_columns(): moved = lax.all_to_all(split.transpose(0, 2, 1, 3), 'ctx', 1, 1, tiled=True)  8.74 us
    pallas_call x1, Pallas kernels, epilogue(): pl.pallas_call(epilogue_kernel, grid=grid, in_specs=[pl.BlockSpec((None,...  8.68 us
    all_to_all x1, starting transfers between devices, mesh_sum(): mine = jnp.sum(lax.all_to_all(pieces, axes, 0, 0, tiled=True), axis=0)  8.61 us
    unnamed x53, local copies, waits for them, and re-layouts  8.52 us
  transfers between devices with their start and end apart: 14, of which 8 were waited for; matrix products, arithmetic and copies ran while one was open for 23% of the time, Pallas kernels for 5%

profile of v9, /device:TPU:0, one launch (start us, length us, event | category | flops | bytes accessed | tf_op | source)
XLA Modules:
  0.0 162.2 jit_solution(4442289594504982724)
XLA Ops:
  2.4 4.9 %collective-permute-start = (bf16[3,2,2048]{2,1,0:T(2,128)(2,1)S(1)}, bf16[3,2,2048]{2,1,0:T(2,128)(2,1)S(1)}, u32[]{:S(2)}, u32[]{:S(2)}) collective-permute-start(bf16[3,2,2048]{2,1,0:T(2,128)(2,1)S(1)} %pad_maximum_fusion.4), channel_id=1, source_target_pairs={{0,1},{1,2},{2,3},{3,4},{4,5},{5,6},{6,7},{8,9},{9,10},{10,11},{11... | collective-permute-start | bytes 73736 | tf_op jit(solution)/shard_map/ppermute | solution.py:16
  16.6 5.0 %all-to-all-start.1 = ((bf16[3,8,128,128]{3,2,0,1:T(8,128)(2,1)}), bf16[3,8,128,128]{3,2,0,1:T(8,128)(2,1)S(1)}, u32[]{:S(2)}, u32[]{:S(2)}) async-start(bf16[3,8,128,128]{3,2,0,1:T(8,128)(2,1)} %copy.185), calls=%async_computation.1 | async-start | bytes 1572864 | tf_op jit(solution)/shard_map/all_to_all | solution.py:314
  24.3 17.3 %all-to-all-done.1 = bf16[3,8,128,128]{3,2,0,1:T(8,128)(2,1)S(1)} async-done(((bf16[3,8,128,128]{3,2,0,1:T(8,128)(2,1)}), bf16[3,8,128,128]{3,2,0,1:T(8,128)(2,1)S(1)}, u32[]{:S(2)}, u32[]{:S(2)}) %all-to-all-start.1) | async-done | bytes 786464 | tf_op jit(solution)/shard_map/all_to_all | solution.py:314
  41.6 3.7 %all-to-all-start = ((bf16[3,8,128,128]{3,2,0,1:T(8,128)(2,1)}), bf16[3,8,128,128]{3,2,0,1:T(8,128)(2,1)S(1)}, u32[]{:S(2)}, u32[]{:S(2)}) async-start(bf16[3,8,128,128]{3,2,0,1:T(8,128)(2,1)} %copy.182), calls=%async_computation | async-start | bytes 1572864 | tf_op jit(solution)/shard_map/all_to_all | solution.py:314
  48.8 2.5 %fusion.18 = f32[64,3,64,128]{3,0,2,1:T(8,128)S(1)} fusion(bf16[64,64,1,1]{1,0,3,2:T(8,128)(2,1)S(1)} %copy-done.12, bf16[64,3,64,128]{3,2,1,0:T(8,128)(2,1)S(1)} %bitcast.242), kind=kOutput, calls=%fused_computation.22 | convolution fusion | flops 201326592 | bytes 9445376 | tf_op jit(solution)/shard_map/ab,bskc->askc/dot_general | solution.py:29
  63.6 1.9 %all-to-all-done = bf16[3,8,128,128]{3,2,0,1:T(8,128)(2,1)S(1)} async-done(((bf16[3,8,128,128]{3,2,0,1:T(8,128)(2,1)}), bf16[3,8,128,128]{3,2,0,1:T(8,128)(2,1)S(1)}, u32[]{:S(2)}, u32[]{:S(2)}) %all-to-all-start) | async-done | bytes 786464 | tf_op jit(solution)/shard_map/all_to_all | solution.py:314
  66.6 1.5 fusion.24
  69.1 2.5 %fusion.14 = f32[64,3,64,128]{3,0,2,1:T(8,128)S(1)} fusion(bf16[64,64,1,1]{1,0,3,2:T(8,128)(2,1)S(1)} %copy-done.12, bf16[64,3,64,128]{3,2,1,0:T(8,128)(2,1)S(1)} %bitcast.241), kind=kOutput, calls=%fused_computation.18 | convolution fusion | flops 201326592 | bytes 9445376 | tf_op jit(solution)/shard_map/ab,bskc->askc/dot_general | solution.py:29
  78.2 3.9 %all-to-all-start.2 = ((bf16[2,8,136,128]{3,2,0,1:T(8,128)(2,1)}), bf16[2,8,136,128]{3,2,0,1:T(8,128)(2,1)S(1)}, u32[]{:S(2)}, u32[]{:S(2)}) async-start(bf16[2,8,136,128]{3,2,0,1:T(8,128)(2,1)} %fusion.70), calls=%async_computation.2 | async-start | bytes 1114112 | tf_op jit(solution)/shard_map/all_to_all | solution.py:325
  84.3 1.5 collective-permute-start.2
  85.8 3.7 %collective-permute-done.1 = bf16[4,2,2048]{2,1,0:T(2,128)(2,1)S(1)} collective-permute-done((bf16[4,2,2048]{2,1,0:T(2,128)(2,1)S(1)}, bf16[4,2,2048]{2,1,0:T(2,128)(2,1)S(1)}, u32[]{:S(2)}, u32[]{:S(2)}) %collective-permute-start.1) | collective-permute-done | bytes 32800 | tf_op jit(solution)/shard_map/ppermute | solution.py:16
  89.6 1.7 %maximum_maximum_fusion = (bf16[136,2048]{1,0:T(8,128)(2,1)}, bf16[1,136,2048]{2,1,0:T(8,128)(2,1)S(1)}, bf16[1,136,2048]{2,1,0:T(8,128)(2,1)S(1)}, bf16[1,136,2048]{2,1,0:T(8,128)(2,1)S(1)}) fusion(bf16[2,2048]{1,0:T(2,128)(2,1)S(1)} %get-tuple-element.66, bf16[128,2048]{1,0:T(8,128)(2,1)S(1)} %bitcast.269, bf16[136]{0:T(256)(128)(2,1)S(1)} %pad.13.clone, ...), kind=kLoop, calls=%fused_computation.106 | loop fusion | flops 8077312 | bytes 4383264 | tf_op jit(solution)/shard_map/concatenate | solution.py:355
  91.3 6.3 %collective-permute-done.2 = f32[2,256,256]{2,1,0:T(8,128)S(1)} collective-permute-done((f32[2,256,256]{2,1,0:T(8,128)S(1)}, f32[2,256,256]{2,1,0:T(8,128)S(1)}, u32[]{:S(2)}, u32[]{:S(2)}) %collective-permute-start.2) | collective-permute-done | bytes 524320 | tf_op jit(solution)/shard_map/ppermute | solution.py:146
  97.7 6.6 %all-to-all-start.3 = ((bf16[2,8,136,128]{3,2,0,1:T(8,128)(2,1)}), bf16[2,8,136,128]{3,2,0,1:T(8,128)(2,1)S(1)}, u32[]{:S(2)}, u32[]{:S(2)}) async-start(bf16[2,8,136,128]{3,2,0,1:T(8,128)(2,1)} %copy-done.8), calls=%async_computation.3 | async-start | bytes 1114112 | tf_op jit(solution)/shard_map/all_to_all | solution.py:337
  104.4 1.4 pad_maximum_fusion.src_ref
  108.0 4.8 %collective-permute-start.5 = (f32[128,256]{1,0:T(8,128)}, f32[128,256]{1,0:T(8,128)S(1)}, u32[]{:S(2)}, u32[]{:S(2)}) collective-permute-start(f32[128,256]{1,0:T(8,128)} %get-tuple-element.55), channel_id=1, source_target_pairs={{0,1},{2,9},{4,17},{6,25},{8,3},{10,11},{12,19},{14,27},{16,5},{18... | collective-permute-start | bytes 393224 | tf_op jit(solution)/shard_map/ppermute | solution.py:165
  114.1 2.2 %collective-permute-start.4 = (f32[128,256]{1,0:T(8,128)}, f32[128,256]{1,0:T(8,128)}, u32[]{:S(2)}, u32[]{:S(2)}) collective-permute-start(f32[128,256]{1,0:T(8,128)} %get-tuple-element.56), channel_id=1, source_target_pairs={{0,0},{2,8},{4,16},{6,24},{8,2},{10,10},{12,18},{14,26},{16,4},{18... | collective-permute-start | bytes 393224 | tf_op jit(solution)/shard_map/ppermute | solution.py:165
  116.3 1.4 all-to-all-done.3
  119.0 1.6 %reshape.213.conv_ref.back_ref = bf16[2,136,2048]{2,1,0:T(8,128)(2,1)} reshape(bf16[2,136,8,2,128]{4,3,2,1,0:T(2,128)(2,1)S(1)} %copy.201) | data formatting | bytes 2228224 | tf_op jit(solution)/shard_map/reshape | solution.py:339
  120.7 8.7 %shard_map.279 = (bf16[4,128,2048]{2,1,0:T(8,128)(2,1)}, f32[16,2048]{1,0:T(8,128)}) custom-call(bf16[2,136,2048]{2,1,0:T(8,128)(2,1)} %reshape.213.conv_ref.back_ref, bf16[2,136,2048]{2,1,0:T(8,128)(2,1)} %reshape.213.conv_ref.back_ref, bf16[3,136,2048]{2,1,0:T(8,128)(2,1)} %pad_maximum_fusion.src_ref, bf16[136,2048]{1,0:T(8,128)(2,1)} %get-tuple-element.75.up_ref, ...), custom_call_target="tpu_custom_call" | custom-call | tf_op jit(solution)/shard_map/pallas_call | solution.py:244
  131.4 8.6 %all-to-all-start.4 = ((f32[32,1,640]{2,1,0:T(1,128)}), f32[32,1,640]{2,1,0:T(1,128)S(1)}, u32[]{:S(2)}, u32[]{:S(2)}) async-start(f32[32,1,640]{2,1,0:T(1,128)} %reshape.220), calls=%async_computation.4 | async-start | bytes 163840 | tf_op jit(solution)/shard_map/all_to_all | solution.py:130
  142.7 4.7 %all-to-all-done.4 = f32[32,1,640]{2,1,0:T(1,128)S(1)} async-done(((f32[32,1,640]{2,1,0:T(1,128)}), f32[32,1,640]{2,1,0:T(1,128)S(1)}, u32[]{:S(2)}, u32[]{:S(2)}) %all-to-all-start.4) | async-done | bytes 81952 | tf_op jit(solution)/shard_map/all_to_all | solution.py:130
  149.8 2.6 %all-to-all-start.5 = ((f32[32,1,640]{2,1,0:T(1,128)}), f32[32,1,640]{2,1,0:T(1,128)S(1)}, u32[]{:S(2)}, u32[]{:S(2)}) async-start(f32[32,1,640]{2,1,0:T(1,128)} %reshape.222), calls=%async_computation.5 | async-start | bytes 163840 | tf_op jit(solution)/shard_map/all_to_all | solution.py:132
  153.7 6.1 %all-to-all-done.5 = f32[32,1,640]{2,1,0:T(1,128)S(1)} async-done(((f32[32,1,640]{2,1,0:T(1,128)}), f32[32,1,640]{2,1,0:T(1,128)S(1)}, u32[]{:S(2)}, u32[]{:S(2)}) %all-to-all-start.5) | async-done | bytes 81952 | tf_op jit(solution)/shard_map/all_to_all | solution.py:132
  (166 shorter events, 55.5 us)
Async XLA Ops:
  0.6 11.9 %copy-start.5 = (bf16[1,128,2048]{2,1,0:T(8,128)(2,1)S(1)}, bf16[1,128,2048]{2,1,0:T(8,128)(2,1)}, u32[]{:S(2)}) copy-start(bf16[1,128,2048]{2,1,0:T(8,128)(2,1)} %param.27) | copy-start | bytes 1572868
  2.4 8.9 %collective-permute-start = (bf16[3,2,2048]{2,1,0:T(2,128)(2,1)S(1)}, bf16[3,2,2048]{2,1,0:T(2,128)(2,1)S(1)}, u32[]{:S(2)}, u32[]{:S(2)}) collective-permute-start(bf16[3,2,2048]{2,1,0:T(2,128)(2,1)S(1)} %pad_maximum_fusion.4), channel_id=1, source_target_pairs={{0,1},{1,2},{2,3},{3,4},{4,5},{5,6},{6,7},{8,9},{9,10},{10,11},{11... | collective-permute-start | bytes 73736 | tf_op jit(solution)/shard_map/ppermute | solution.py:16
  11.3 2.2 %copy-start.2 = (bf16[1,128,2048]{2,1,0:T(8,128)(2,1)S(1)}, bf16[1,128,2048]{2,1,0:T(8,128)(2,1)}, u32[]{:S(2)}) copy-start(bf16[1,128,2048]{2,1,0:T(8,128)(2,1)} %param.26) | copy-start | bytes 1572868
  16.6 28.8 %copy-start.16 = (bf16[128,32,1,1]{0,1,3,2:T(8,128)(2,1)S(1)}, bf16[128,32,1,1]{0,1,3,2:T(8,128)(2,1)}, u32[]{:S(2)}) copy-start(bf16[128,32,1,1]{0,1,3,2:T(8,128)(2,1)} %constant.113) | copy-start | bytes 24580
  16.6 25.0 %all-to-all-start.1 = ((bf16[3,8,128,128]{3,2,0,1:T(8,128)(2,1)}), bf16[3,8,128,128]{3,2,0,1:T(8,128)(2,1)S(1)}, u32[]{:S(2)}, u32[]{:S(2)}) async-start(bf16[3,8,128,128]{3,2,0,1:T(8,128)(2,1)} %copy.185), calls=%async_computation.1 | async-start | bytes 1572864 | tf_op jit(solution)/shard_map/all_to_all | solution.py:314
  41.6 23.9 %all-to-all-start = ((bf16[3,8,128,128]{3,2,0,1:T(8,128)(2,1)}), bf16[3,8,128,128]{3,2,0,1:T(8,128)(2,1)S(1)}, u32[]{:S(2)}, u32[]{:S(2)}) async-start(bf16[3,8,128,128]{3,2,0,1:T(8,128)(2,1)} %copy.182), calls=%async_computation | async-start | bytes 1572864 | tf_op jit(solution)/shard_map/all_to_all | solution.py:314
  57.8 7.7 %copy-start = (f32[3,32,32,128]{3,1,2,0:T(8,128)}, f32[3,32,32,128]{3,1,2,0:T(8,128)S(1)}, u32[]{:S(2)}) copy-start(f32[3,32,32,128]{3,1,2,0:T(8,128)S(1)} %fusion.28) | copy-start | bytes 4718596
  76.5 1.4 slice-start
  78.2 19.5 %all-to-all-start.2 = ((bf16[2,8,136,128]{3,2,0,1:T(8,128)(2,1)}), bf16[2,8,136,128]{3,2,0,1:T(8,128)(2,1)S(1)}, u32[]{:S(2)}, u32[]{:S(2)}) async-start(bf16[2,8,136,128]{3,2,0,1:T(8,128)(2,1)} %fusion.70), calls=%async_computation.2 | async-start | bytes 1114112 | tf_op jit(solution)/shard_map/all_to_all | solution.py:325
  82.0 7.5 %copy-start.1 = (bf16[1,128,2048]{2,1,0:T(8,128)(2,1)S(1)}, bf16[1,128,2048]{2,1,0:T(8,128)(2,1)}, u32[]{:S(2)}) copy-start(bf16[1,128,2048]{2,1,0:T(8,128)(2,1)} %param.24) | copy-start | bytes 1572868
  82.0 7.6 %copy-start.4 = (bf16[1,128,2048]{2,1,0:T(8,128)(2,1)S(1)}, bf16[1,128,2048]{2,1,0:T(8,128)(2,1)}, u32[]{:S(2)}) copy-start(bf16[1,128,2048]{2,1,0:T(8,128)(2,1)} %param.25) | copy-start | bytes 1572868
  82.0 7.6 %copy-start.6 = (bf16[1,128,2048]{2,1,0:T(8,128)(2,1)S(1)}, bf16[1,128,2048]{2,1,0:T(8,128)(2,1)}, u32[]{:S(2)}) copy-start(bf16[1,128,2048]{2,1,0:T(8,128)(2,1)} %param.27) | copy-start | bytes 1572868
  82.9 6.7 %copy-start.8 = (bf16[2,8,136,128]{3,2,0,1:T(8,128)(2,1)}, bf16[2,8,136,128]{3,2,0,1:T(8,128)(2,1)S(1)}, u32[]{:S(2)}) copy-start(bf16[2,8,136,128]{3,2,0,1:T(8,128)(2,1)S(1)} %fusion.74) | copy-start | bytes 1671172
  82.9 6.7 %collective-permute-start.1 = (bf16[4,2,2048]{2,1,0:T(2,128)(2,1)S(1)}, bf16[4,2,2048]{2,1,0:T(2,128)(2,1)S(1)}, u32[]{:S(2)}, u32[]{:S(2)}) collective-permute-start(bf16[4,2,2048]{2,1,0:T(2,128)(2,1)S(1)} %pad_maximum_fusion.3), channel_id=1, source_target_pairs={{1,0},{2,1},{3,2},{4,3},{5,4},{6,5},{7,6},{9,8},{10,9},{11,10},{12... | collective-permute-start | bytes 98312 | tf_op jit(solution)/shard_map/ppermute | solution.py:16
  84.3 13.3 %collective-permute-start.2 = (f32[2,256,256]{2,1,0:T(8,128)S(1)}, f32[2,256,256]{2,1,0:T(8,128)S(1)}, u32[]{:S(2)}, u32[]{:S(2)}) collective-permute-start(f32[2,256,256]{2,1,0:T(8,128)S(1)} %bitcast.279), channel_id=1, source_target_pairs={{0,16},{8,24},{16,0},{24,8},{1,17},{9,25},{17,1},{25,9},{2,18},{10... | collective-permute-start | bytes 1572872 | tf_op jit(solution)/shard_map/ppermute | solution.py:146
  97.7 20.1 %all-to-all-start.3 = ((bf16[2,8,136,128]{3,2,0,1:T(8,128)(2,1)}), bf16[2,8,136,128]{3,2,0,1:T(8,128)(2,1)S(1)}, u32[]{:S(2)}, u32[]{:S(2)}) async-start(bf16[2,8,136,128]{3,2,0,1:T(8,128)(2,1)} %copy-done.8), calls=%async_computation.3 | async-start | bytes 1114112 | tf_op jit(solution)/shard_map/all_to_all | solution.py:337
  104.3 1.6 collective-permute-start.3
  106.7 33.3 %collective-permute-start.7 = (f32[128,256]{1,0:T(8,128)}, f32[128,256]{1,0:T(8,128)}, u32[]{:S(2)}, u32[]{:S(2)}) collective-permute-start(f32[128,256]{1,0:T(8,128)} %get-tuple-element.55), channel_id=1, source_target_pairs={{1,1},{3,9},{5,17},{7,25},{9,3},{11,11},{13,19},{15,27},{17,5},{19... | collective-permute-start | bytes 393224 | tf_op jit(solution)/shard_map/ppermute | solution.py:165
  108.0 33.0 %collective-permute-start.5 = (f32[128,256]{1,0:T(8,128)}, f32[128,256]{1,0:T(8,128)S(1)}, u32[]{:S(2)}, u32[]{:S(2)}) collective-permute-start(f32[128,256]{1,0:T(8,128)} %get-tuple-element.55), channel_id=1, source_target_pairs={{0,1},{2,9},{4,17},{6,25},{8,3},{10,11},{12,19},{14,27},{16,5},{18... | collective-permute-start | bytes 393224 | tf_op jit(solution)/shard_map/ppermute | solution.py:165
  112.8 27.3 %collective-permute-start.6 = (f32[128,256]{1,0:T(8,128)}, f32[128,256]{1,0:T(8,128)}, u32[]{:S(2)}, u32[]{:S(2)}) collective-permute-start(f32[128,256]{1,0:T(8,128)} %get-tuple-element.56), channel_id=1, source_target_pairs={{1,0},{3,8},{5,16},{7,24},{9,2},{11,10},{13,18},{15,26},{17,4},{19... | collective-permute-start | bytes 393224 | tf_op jit(solution)/shard_map/ppermute | solution.py:165
  114.1 27.0 %collective-permute-start.4 = (f32[128,256]{1,0:T(8,128)}, f32[128,256]{1,0:T(8,128)}, u32[]{:S(2)}, u32[]{:S(2)}) collective-permute-start(f32[128,256]{1,0:T(8,128)} %get-tuple-element.56), channel_id=1, source_target_pairs={{0,0},{2,8},{4,16},{6,24},{8,2},{10,10},{12,18},{14,26},{16,4},{18... | collective-permute-start | bytes 393224 | tf_op jit(solution)/shard_map/ppermute | solution.py:165
  129.4 23.0 %copy-start.7 = (bf16[4,128,2048]{2,1,0:T(8,128)(2,1)S(1)}, bf16[4,128,2048]{2,1,0:T(8,128)(2,1)}, u32[]{:S(2)}) copy-start(bf16[4,128,2048]{2,1,0:T(8,128)(2,1)} %get-tuple-element.17) | copy-start | bytes 6291460
  131.4 16.1 %all-to-all-start.4 = ((f32[32,1,640]{2,1,0:T(1,128)}), f32[32,1,640]{2,1,0:T(1,128)S(1)}, u32[]{:S(2)}, u32[]{:S(2)}) async-start(f32[32,1,640]{2,1,0:T(1,128)} %reshape.220), calls=%async_computation.4 | async-start | bytes 163840 | tf_op jit(solution)/shard_map/all_to_all | solution.py:130
  149.8 10.0 %all-to-all-start.5 = ((f32[32,1,640]{2,1,0:T(1,128)}), f32[32,1,640]{2,1,0:T(1,128)S(1)}, u32[]{:S(2)}, u32[]{:S(2)}) async-start(f32[32,1,640]{2,1,0:T(1,128)} %reshape.222), calls=%async_computation.5 | async-start | bytes 163840 | tf_op jit(solution)/shard_map/all_to_all | solution.py:132
  (8 other events, 7.5 us)

commit v10 on v9

--- a/solution.py
+++ b/solution.py
@@ -349,12 +349,14 @@
     masks = jnp.concatenate([masks, jnp.zeros(((-masks.shape[0]) % 8, frame), jnp.float32)], 0)
     tail = frame - rows - 2 * head
     sources = jnp.stack([
-        jnp.concatenate([prev[i], src, nxt[i], jnp.zeros((tail, chans), src.dtype)], 0)
+        jnp.concatenate([prev[i], src, jnp.zeros((head + tail, chans), src.dtype)], 0)
         for i, src in enumerate((q_rows, k_rows, v_rows))
     ])
     framed_up = jnp.concatenate(
-        [jnp.zeros((head, chans), c_rows.dtype), c_rows, nxt[3], jnp.zeros((tail, chans), c_rows.dtype)], 0
-    )
+        [jnp.zeros((head, chans), c_rows.dtype), c_rows, jnp.zeros((head + tail, chans), c_rows.dtype)], 0
+    )
+    sources = lax.dynamic_update_slice(sources, nxt[:3], (0, head + rows, 0))
+    framed_up = lax.dynamic_update_slice(framed_up, nxt[3], (head + rows, 0))
     outs, stats = epilogue(back, sources, framed_up, masks[:, :, None], short_weights, skip, rows)
     summed = mesh_sum(stats[: 3 * taps + 1], ("dp", "ctx"))
     gated, grad_q, grad_k, grad_v = outs[0], outs[1], outs[2], outs[3]

time: 163 us -> 169 us (1.037)
  waiting for transfers between devices: 41.7 us -> 49.4 us
  starting transfers between devices: 47.7 us -> 40.7 us
  local copies, waits for them, and re-layouts: 28.3 us -> 34.6 us
  other arithmetic: 22.6 us -> 20.8 us
    all_to_all x1, starting transfers between devices: 8.61 us -> 3.35 us  [mesh_sum(): mine = jnp.sum(lax.all_to_all(pieces, axes, 0, 0, tiled=True), axis=0)]
    all_to_all x2, waiting for transfers between devices: 1.43 us -> 6.34 us  [local(): returned.append(lax.all_to_all(previous, 'ctx', 1, 1, tiled=True))]
    unnamed x53 -> x45, local copies, waits for them, and re-layouts: 8.52 us -> 12.6 us
    add x2, other arithmetic: 1.91 us -> 0.04 us  [route_filter_grad(): total = got if total is None else total + got]
    all_to_all x1, waiting for transfers between devices: 4.75 us -> 6.61 us  [mesh_sum(): mine = jnp.sum(lax.all_to_all(pieces, axes, 0, 0, tiled=True), axis=0)]
  transfers between devices with their start and end apart: 14 -> 14, of which waited for: 8 -> 8; matrix products, arithmetic and copies ran while one was open for 23% -> 22% of each run, Pallas kernels for 5% -> 5%
where the time goes in v10:
time: 169 us; the launch traced here: 167 us
  waiting for transfers between devices  49.4 us (29%)
  starting transfers between devices  40.7 us (24%)
  local copies, waits for them, and re-layouts  34.6 us (20%)
  other arithmetic  20.8 us (12%)
  matrix products  11.7 us (7%)
  Pallas kernels  8.68 us (5%)
    all_to_all x2, waiting for transfers between devices, to_columns(): moved = lax.all_to_all(split.transpose(0, 2, 1, 3), 'ctx', 1, 1, tiled=True)  19.5 us
    unnamed x45, local copies, waits for them, and re-layouts  12.6 us
    dot_general x8, matrix products, split_product(): jnp.einsum(form, upper, data.astype(jnp.bfloat16), preferred_element_type...  11.7 us
    all_to_all x2, starting transfers between devices, local(): returned.append(lax.all_to_all(previous, 'ctx', 1, 1, tiled=True))  9.91 us
    all_to_all x2, starting transfers between devices, to_columns(): moved = lax.all_to_all(split.transpose(0, 2, 1, 3), 'ctx', 1, 1, tiled=True)  8.74 us
    pallas_call x1, Pallas kernels, epilogue(): pl.pallas_call(epilogue_kernel, grid=grid, in_specs=[pl.BlockSpec((None,...  8.68 us
    ppermute x4, starting transfers between devices, route_filter_grad(): got = lax.ppermute(pieces[piece], ('dp', 'ctx'), pairs)  8.32 us
    all_to_all x1, waiting for transfers between devices, mesh_sum(): mine = jnp.sum(lax.all_to_all(pieces, axes, 0, 0, tiled=True), axis=0)  6.61 us
  transfers between devices with their start and end apart: 14, of which 8 were waited for; matrix products, arithmetic and copies ran while one was open for 22% of the time, Pallas kernels for 5%

profile of v10, /device:TPU:0, one launch (start us, length us, event | category | flops | bytes accessed | tf_op | source)
XLA Modules:
  0.0 167.3 jit_solution(5665426316376323577)
XLA Ops:
  2.4 4.9 %collective-permute-start = (bf16[3,2,2048]{2,1,0:T(2,128)(2,1)S(1)}, bf16[3,2,2048]{2,1,0:T(2,128)(2,1)S(1)}, u32[]{:S(2)}, u32[]{:S(2)}) collective-permute-start(bf16[3,2,2048]{2,1,0:T(2,128)(2,1)S(1)} %pad_maximum_fusion.4), channel_id=1, source_target_pairs={{0,1},{1,2},{2,3},{3,4},{4,5},{5,6},{6,7},{8,9},{9,10},{10,11},{11... | collective-permute-start | bytes 73736 | tf_op jit(solution)/shard_map/ppermute | solution.py:16
  16.5 5.0 %all-to-all-start.1 = ((bf16[3,8,128,128]{3,2,0,1:T(8,128)(2,1)}), bf16[3,8,128,128]{3,2,0,1:T(8,128)(2,1)S(1)}, u32[]{:S(2)}, u32[]{:S(2)}) async-start(bf16[3,8,128,128]{3,2,0,1:T(8,128)(2,1)} %copy.185), calls=%async_computation.1 | async-start | bytes 1572864 | tf_op jit(solution)/shard_map/all_to_all | solution.py:314
  24.2 17.3 %all-to-all-done.1 = bf16[3,8,128,128]{3,2,0,1:T(8,128)(2,1)S(1)} async-done(((bf16[3,8,128,128]{3,2,0,1:T(8,128)(2,1)}), bf16[3,8,128,128]{3,2,0,1:T(8,128)(2,1)S(1)}, u32[]{:S(2)}, u32[]{:S(2)}) %all-to-all-start.1) | async-done | bytes 786464 | tf_op jit(solution)/shard_map/all_to_all | solution.py:314
  41.5 3.7 %all-to-all-start = ((bf16[3,8,128,128]{3,2,0,1:T(8,128)(2,1)}), bf16[3,8,128,128]{3,2,0,1:T(8,128)(2,1)S(1)}, u32[]{:S(2)}, u32[]{:S(2)}) async-start(bf16[3,8,128,128]{3,2,0,1:T(8,128)(2,1)} %copy.182), calls=%async_computation | async-start | bytes 1572864 | tf_op jit(solution)/shard_map/all_to_all | solution.py:314
  48.7 2.5 %fusion.18 = f32[64,3,64,128]{3,0,2,1:T(8,128)S(1)} fusion(bf16[64,64,1,1]{1,0,3,2:T(8,128)(2,1)S(1)} %copy-done.8, bf16[64,3,64,128]{3,2,1,0:T(8,128)(2,1)S(1)} %bitcast.238), kind=kOutput, calls=%fused_computation.22 | convolution fusion | flops 201326592 | bytes 9445376 | tf_op jit(solution)/shard_map/ab,bskc->askc/dot_general | solution.py:29
  63.2 2.2 %all-to-all-done = bf16[3,8,128,128]{3,2,0,1:T(8,128)(2,1)S(1)} async-done(((bf16[3,8,128,128]{3,2,0,1:T(8,128)(2,1)}), bf16[3,8,128,128]{3,2,0,1:T(8,128)(2,1)S(1)}, u32[]{:S(2)}, u32[]{:S(2)}) %all-to-all-start) | async-done | bytes 786464 | tf_op jit(solution)/shard_map/all_to_all | solution.py:314
  66.4 1.5 fusion.24
  69.0 2.5 %fusion.14 = f32[64,3,64,128]{3,0,2,1:T(8,128)S(1)} fusion(bf16[64,64,1,1]{1,0,3,2:T(8,128)(2,1)S(1)} %copy-done.8, bf16[64,3,64,128]{3,2,1,0:T(8,128)(2,1)S(1)} %bitcast.237), kind=kOutput, calls=%fused_computation.18 | convolution fusion | flops 201326592 | bytes 9445376 | tf_op jit(solution)/shard_map/ab,bskc->askc/dot_general | solution.py:29
  83.0 4.2 %all-to-all-start.3 = ((bf16[2,8,136,128]{3,2,0,1:T(8,128)(2,1)}), bf16[2,8,136,128]{3,2,0,1:T(8,128)(2,1)}, u32[]{:S(2)}, u32[]{:S(2)}) async-start(bf16[2,8,136,128]{3,2,0,1:T(8,128)(2,1)} %fusion.74), calls=%async_computation.3 | async-start | bytes 1114112 | tf_op jit(solution)/shard_map/all_to_all | solution.py:337
  87.2 3.1 %maximum_maximum_fusion = (bf16[136,2048]{1,0:T(8,128)(2,1)}, bf16[1,136,2048]{2,1,0:T(8,128)(2,1)S(1)}, bf16[1,136,2048]{2,1,0:T(8,128)(2,1)S(1)}, bf16[1,136,2048]{2,1,0:T(8,128)(2,1)S(1)}) fusion(bf16[128,2048]{1,0:T(8,128)(2,1)} %bitcast.265, bf16[136]{0:T(256)(128)(2,1)S(1)} %pad.13.clone, bf16[136]{0:T(256)(128)(2,1)S(1)} %pad.27.clone, ...), kind=kLoop, calls=%fused_computation.106 | loop fusion | flops 5849088 | bytes 4350496 | tf_op jit(solution)/shard_map/concatenate | solution.py:355
  91.1 1.6 collective-permute-start.2
  94.2 4.3 %collective-permute-done.1 = bf16[4,2,2048]{2,1,0:T(2,128)(2,1)S(1)} collective-permute-done((bf16[4,2,2048]{2,1,0:T(2,128)(2,1)S(1)}, bf16[4,2,2048]{2,1,0:T(2,128)(2,1)S(1)}, u32[]{:S(2)}, u32[]{:S(2)}) %collective-permute-start.1) | collective-permute-done | bytes 32800 | tf_op jit(solution)/shard_map/ppermute | solution.py:16
  98.5 5.6 %collective-permute-done.2 = f32[2,256,256]{2,1,0:T(8,128)S(1)} collective-permute-done((f32[2,256,256]{2,1,0:T(8,128)S(1)}, f32[2,256,256]{2,1,0:T(8,128)S(1)}, u32[]{:S(2)}, u32[]{:S(2)}) %collective-permute-start.2) | collective-permute-done | bytes 524320 | tf_op jit(solution)/shard_map/ppermute | solution.py:146
  104.2 5.7 %all-to-all-start.2 = ((bf16[2,8,136,128]{3,2,0,1:T(8,128)(2,1)}), bf16[2,8,136,128]{3,2,0,1:T(8,128)(2,1)S(1)}, u32[]{:S(2)}, u32[]{:S(2)}) async-start(bf16[2,8,136,128]{3,2,0,1:T(8,128)(2,1)} %fusion.70), calls=%async_computation.2 | async-start | bytes 1114112 | tf_op jit(solution)/shard_map/all_to_all | solution.py:325
  112.3 1.6 collective-permute-start.4
  115.1 4.6 %collective-permute-start.5 = (f32[128,256]{1,0:T(8,128)S(1)}, f32[128,256]{1,0:T(8,128)S(1)}, u32[]{:S(2)}, u32[]{:S(2)}) collective-permute-start(f32[128,256]{1,0:T(8,128)S(1)} %get-tuple-element.55), channel_id=1, source_target_pairs={{0,1},{2,9},{4,17},{6,25},{8,3},{10,11},{12,19},{14,27},{16,5},{18... | collective-permute-start | bytes 393224 | tf_op jit(solution)/shard_map/ppermute | solution.py:165
  121.7 6.3 %all-to-all-done.2 = bf16[2,8,136,128]{3,2,0,1:T(8,128)(2,1)S(1)} async-done(((bf16[2,8,136,128]{3,2,0,1:T(8,128)(2,1)}), bf16[2,8,136,128]{3,2,0,1:T(8,128)(2,1)S(1)}, u32[]{:S(2)}, u32[]{:S(2)}) %all-to-all-start.2) | async-done | bytes 557088 | tf_op jit(solution)/shard_map/all_to_all | solution.py:325
  129.4 1.6 reshape.213.conv_ref.back_ref
  131.1 8.7 %shard_map.279 = (bf16[4,128,2048]{2,1,0:T(8,128)(2,1)}, f32[16,2048]{1,0:T(8,128)}) custom-call(bf16[2,136,2048]{2,1,0:T(8,128)(2,1)} %reshape.213.conv_ref.back_ref, bf16[2,136,2048]{2,1,0:T(8,128)(2,1)} %reshape.213.conv_ref.back_ref, bf16[3,136,2048]{2,1,0:T(8,128)(2,1)} %copy-done, bf16[136,2048]{1,0:T(8,128)(2,1)} %fusion.87.up_ref, ...), custom_call_target="tpu_custom_call" | custom-call | tf_op jit(solution)/shard_map/pallas_call | solution.py:244
  141.8 3.3 %all-to-all-start.4 = ((f32[32,1,640]{2,1,0:T(1,128)}), f32[32,1,640]{2,1,0:T(1,128)S(1)}, u32[]{:S(2)}, u32[]{:S(2)}) async-start(f32[32,1,640]{2,1,0:T(1,128)} %reshape.220), calls=%async_computation.4 | async-start | bytes 163840 | tf_op jit(solution)/shard_map/all_to_all | solution.py:130
  146.0 6.6 %all-to-all-done.4 = f32[32,1,640]{2,1,0:T(1,128)S(1)} async-done(((f32[32,1,640]{2,1,0:T(1,128)}), f32[32,1,640]{2,1,0:T(1,128)S(1)}, u32[]{:S(2)}, u32[]{:S(2)}) %all-to-all-start.4) | async-done | bytes 81952 | tf_op jit(solution)/shard_map/all_to_all | solution.py:130
  154.9 2.6 %all-to-all-start.5 = ((f32[32,1,640]{2,1,0:T(1,128)}), f32[32,1,640]{2,1,0:T(1,128)S(1)}, u32[]{:S(2)}, u32[]{:S(2)}) async-start(f32[32,1,640]{2,1,0:T(1,128)} %reshape.222), calls=%async_computation.5 | async-start | bytes 163840 | tf_op jit(solution)/shard_map/all_to_all | solution.py:132
  157.5 1.3 fusion.90
  158.8 6.1 %all-to-all-done.5 = f32[32,1,640]{2,1,0:T(1,128)S(1)} async-done(((f32[32,1,640]{2,1,0:T(1,128)}), f32[32,1,640]{2,1,0:T(1,128)S(1)}, u32[]{:S(2)}, u32[]{:S(2)}) %all-to-all-start.5) | async-done | bytes 81952 | tf_op jit(solution)/shard_map/all_to_all | solution.py:132
  (158 shorter events, 59.0 us)
Async XLA Ops:
  0.6 11.8 %copy-start.2 = (bf16[1,128,2048]{2,1,0:T(8,128)(2,1)S(1)}, bf16[1,128,2048]{2,1,0:T(8,128)(2,1)}, u32[]{:S(2)}) copy-start(bf16[1,128,2048]{2,1,0:T(8,128)(2,1)} %param.26) | copy-start | bytes 1572868
  2.4 8.8 %collective-permute-start = (bf16[3,2,2048]{2,1,0:T(2,128)(2,1)S(1)}, bf16[3,2,2048]{2,1,0:T(2,128)(2,1)S(1)}, u32[]{:S(2)}, u32[]{:S(2)}) collective-permute-start(bf16[3,2,2048]{2,1,0:T(2,128)(2,1)S(1)} %pad_maximum_fusion.4), channel_id=1, source_target_pairs={{0,1},{1,2},{2,3},{3,4},{4,5},{5,6},{6,7},{8,9},{9,10},{10,11},{11... | collective-permute-start | bytes 73736 | tf_op jit(solution)/shard_map/ppermute | solution.py:16
  12.6 1.3 copy-start.1
  12.6 1.5 copy-start.3
  16.5 28.8 %copy-start.12 = (bf16[128,32,1,1]{0,1,3,2:T(8,128)(2,1)S(1)}, bf16[128,32,1,1]{0,1,3,2:T(8,128)(2,1)}, u32[]{:S(2)}) copy-start(bf16[128,32,1,1]{0,1,3,2:T(8,128)(2,1)} %constant.115) | copy-start | bytes 24580
  16.5 25.0 %all-to-all-start.1 = ((bf16[3,8,128,128]{3,2,0,1:T(8,128)(2,1)}), bf16[3,8,128,128]{3,2,0,1:T(8,128)(2,1)S(1)}, u32[]{:S(2)}, u32[]{:S(2)}) async-start(bf16[3,8,128,128]{3,2,0,1:T(8,128)(2,1)} %copy.185), calls=%async_computation.1 | async-start | bytes 1572864 | tf_op jit(solution)/shard_map/all_to_all | solution.py:314
  41.5 23.9 %all-to-all-start = ((bf16[3,8,128,128]{3,2,0,1:T(8,128)(2,1)}), bf16[3,8,128,128]{3,2,0,1:T(8,128)(2,1)S(1)}, u32[]{:S(2)}, u32[]{:S(2)}) async-start(bf16[3,8,128,128]{3,2,0,1:T(8,128)(2,1)} %copy.182), calls=%async_computation | async-start | bytes 1572864 | tf_op jit(solution)/shard_map/all_to_all | solution.py:314
  45.3 1.0 copy-start.9
  45.4 1.0 copy-start.10
  53.3 1.1 copy-start.5
  53.3 1.1 copy-start.6
  83.0 21.2 %all-to-all-start.3 = ((bf16[2,8,136,128]{3,2,0,1:T(8,128)(2,1)}), bf16[2,8,136,128]{3,2,0,1:T(8,128)(2,1)}, u32[]{:S(2)}, u32[]{:S(2)}) async-start(bf16[2,8,136,128]{3,2,0,1:T(8,128)(2,1)} %fusion.74), calls=%async_computation.3 | async-start | bytes 1114112 | tf_op jit(solution)/shard_map/all_to_all | solution.py:337
  91.1 13.0 %collective-permute-start.2 = (f32[2,256,256]{2,1,0:T(8,128)S(1)}, f32[2,256,256]{2,1,0:T(8,128)S(1)}, u32[]{:S(2)}, u32[]{:S(2)}) collective-permute-start(f32[2,256,256]{2,1,0:T(8,128)S(1)} %bitcast.275), channel_id=1, source_target_pairs={{0,16},{8,24},{16,0},{24,8},{1,17},{9,25},{17,1},{25,9},{2,18},{10... | collective-permute-start | bytes 1572872 | tf_op jit(solution)/shard_map/ppermute | solution.py:146
  92.7 5.8 %collective-permute-start.1 = (bf16[4,2,2048]{2,1,0:T(2,128)(2,1)S(1)}, bf16[4,2,2048]{2,1,0:T(2,128)(2,1)S(1)}, u32[]{:S(2)}, u32[]{:S(2)}) collective-permute-start(bf16[4,2,2048]{2,1,0:T(2,128)(2,1)S(1)} %pad_maximum_fusion.3), channel_id=1, source_target_pairs={{1,0},{2,1},{3,2},{4,3},{5,4},{6,5},{7,6},{9,8},{10,9},{11,10},{12... | collective-permute-start | bytes 98312 | tf_op jit(solution)/shard_map/ppermute | solution.py:16
  98.5 29.6 %copy-start = (bf16[3,136,2048]{2,1,0:T(8,128)(2,1)}, bf16[3,136,2048]{2,1,0:T(8,128)(2,1)S(1)}, u32[]{:S(2)}) copy-start(bf16[3,136,2048]{2,1,0:T(8,128)(2,1)S(1)} %slice_dynamic-update-slice_fusion.src_ref) | copy-start | bytes 5013508
  104.2 23.9 %all-to-all-start.2 = ((bf16[2,8,136,128]{3,2,0,1:T(8,128)(2,1)}), bf16[2,8,136,128]{3,2,0,1:T(8,128)(2,1)S(1)}, u32[]{:S(2)}, u32[]{:S(2)}) async-start(bf16[2,8,136,128]{3,2,0,1:T(8,128)(2,1)} %fusion.70), calls=%async_computation.2 | async-start | bytes 1114112 | tf_op jit(solution)/shard_map/all_to_all | solution.py:325
  110.0 1.6 collective-permute-start.3
  112.3 32.8 %collective-permute-start.4 = (f32[128,256]{1,0:T(8,128)}, f32[128,256]{1,0:T(8,128)S(1)}, u32[]{:S(2)}, u32[]{:S(2)}) collective-permute-start(f32[128,256]{1,0:T(8,128)} %get-tuple-element.56), channel_id=1, source_target_pairs={{0,0},{2,8},{4,16},{6,24},{8,2},{10,10},{12,18},{14,26},{16,4},{18... | collective-permute-start | bytes 393224 | tf_op jit(solution)/shard_map/ppermute | solution.py:165
  113.9 31.3 %collective-permute-start.6 = (f32[128,256]{1,0:T(8,128)}, f32[128,256]{1,0:T(8,128)S(1)}, u32[]{:S(2)}, u32[]{:S(2)}) collective-permute-start(f32[128,256]{1,0:T(8,128)} %get-tuple-element.56), channel_id=1, source_target_pairs={{1,0},{3,8},{5,16},{7,24},{9,2},{11,10},{13,18},{15,26},{17,4},{19... | collective-permute-start | bytes 393224 | tf_op jit(solution)/shard_map/ppermute | solution.py:165
  115.1 30.0 %collective-permute-start.5 = (f32[128,256]{1,0:T(8,128)S(1)}, f32[128,256]{1,0:T(8,128)S(1)}, u32[]{:S(2)}, u32[]{:S(2)}) collective-permute-start(f32[128,256]{1,0:T(8,128)S(1)} %get-tuple-element.55), channel_id=1, source_target_pairs={{0,1},{2,9},{4,17},{6,25},{8,3},{10,11},{12,19},{14,27},{16,5},{18... | collective-permute-start | bytes 393224 | tf_op jit(solution)/shard_map/ppermute | solution.py:165
  119.7 25.5 %collective-permute-start.7 = (f32[128,256]{1,0:T(8,128)S(1)}, f32[128,256]{1,0:T(8,128)S(1)}, u32[]{:S(2)}, u32[]{:S(2)}) collective-permute-start(f32[128,256]{1,0:T(8,128)S(1)} %get-tuple-element.55), channel_id=1, source_target_pairs={{1,1},{3,9},{5,17},{7,25},{9,3},{11,11},{13,19},{15,27},{17,5},{19... | collective-permute-start | bytes 393224 | tf_op jit(solution)/shard_map/ppermute | solution.py:165
  139.7 17.7 %copy-start.4 = (bf16[4,128,2048]{2,1,0:T(8,128)(2,1)S(1)}, bf16[4,128,2048]{2,1,0:T(8,128)(2,1)}, u32[]{:S(2)}) copy-start(bf16[4,128,2048]{2,1,0:T(8,128)(2,1)} %get-tuple-element.17) | copy-start | bytes 6291460
  141.8 10.8 %all-to-all-start.4 = ((f32[32,1,640]{2,1,0:T(1,128)}), f32[32,1,640]{2,1,0:T(1,128)S(1)}, u32[]{:S(2)}, u32[]{:S(2)}) async-start(f32[32,1,640]{2,1,0:T(1,128)} %reshape.220), calls=%async_computation.4 | async-start | bytes 163840 | tf_op jit(solution)/shard_map/all_to_all | solution.py:130
  154.9 10.0 %all-to-all-start.5 = ((f32[32,1,640]{2,1,0:T(1,128)}), f32[32,1,640]{2,1,0:T(1,128)S(1)}, u32[]{:S(2)}, u32[]{:S(2)}) async-start(f32[32,1,640]{2,1,0:T(1,128)} %reshape.222), calls=%async_computation.5 | async-start | bytes 163840 | tf_op jit(solution)/shard_map/all_to_all | solution.py:132
  (3 other events, 2.1 us)
